TPU v7x, 32 devices: a whole 2x2x4 slice. The times are simulated.
32 devices in a mesh: dp: 16 (over z, y, x), mp: 2 (over core).
Axes of the slice: x: 2, y: 2, z: 4, core: 2. Of those that a mesh axis runs over, the one named last changes fastest.
Arguments:
- patch_rows: bfloat16 [32, 384, 768], P('dp'), may hold values from -6 to 6
- cotangent: bfloat16 [32, 34, 16, 768], P(None, None, 'dp', 'mp'), may hold values from -6 to 6
- mask_token: bfloat16 [768], P('mp'), may hold values from -6 to 6
- lengths: int32 [32], replicated, may hold values from 66 to 529, as said below
- masked: int32 [32, 529], replicated, may hold values from 0 to 1, as said below
- dealing: int32 [32], replicated, may hold values from 0 to 31, each once
- qkv_master: float32 [2, 884736], P('mp', 'dp'), may hold values from -0.21875 to 0.21875
- qkv_first: float32 [2, 884736], P('mp', 'dp'), may hold values from -48 to 48
- qkv_second: float32 [2, 884736], P('mp', 'dp'), may hold values from 2.94912 to 47.18592
- out_master: float32 [2, 294912], P('mp', 'dp'), may hold values from -3.5 to 3.5
- out_first: float32 [2, 294912], P('mp', 'dp'), may hold values from -6 to 6
- out_second: float32 [2, 294912], P('mp', 'dp'), may hold values from 0.0466944 to 0.73728
- fc1_master: float32 [2, 1179648], P('mp', 'dp'), may hold values from -0.21875 to 0.21875
- fc1_first: float32 [2, 1179648], P('mp', 'dp'), may hold values from -20 to 20
- fc1_second: float32 [2, 1179648], P('mp', 'dp'), may hold values from 0.4153344 to 6.63552
- fc2_master: float32 [2, 1179648], P('mp', 'dp'), may hold values from -0.109375 to 0.109375
- fc2_first: float32 [2, 1179648], P('mp', 'dp'), may hold values from -40 to 40
- fc2_second: float32 [2, 1179648], P('mp', 'dp'), may hold values from 1.65888 to 26.54208
- rep_master: float32 [6, 768], replicated
- rep_first: float32 [6, 768], replicated, may hold values from -64 to 64
- rep_second: float32 [6, 768], replicated, may hold values from 4.608 to 73.728
- split_master: float32 [2, 6, 384], P('mp'), may hold values from -1.2 to 1.2
- split_first: float32 [2, 6, 384], P('mp'), may hold values from -64 to 64
- split_second: float32 [2, 6, 384], P('mp'), may hold values from 4.608 to 73.728
Outputs:
- full_out: bfloat16 [32, 34, 16, 768], P(None, None, 'dp', 'mp')
- input_grad: float32 [32, 384, 768], P('dp')
- mask_grad: float32 [768], P('mp')
- qkv_new: float32 [2, 884736], P('mp', 'dp')
- qkv_first_new: float32 [2, 884736], P('mp', 'dp')
- qkv_second_new: float32 [2, 884736], P('mp', 'dp')
- out_new: float32 [2, 294912], P('mp', 'dp')
- out_first_new: float32 [2, 294912], P('mp', 'dp')
- out_second_new: float32 [2, 294912], P('mp', 'dp')
- fc1_new: float32 [2, 1179648], P('mp', 'dp')
- fc1_first_new: float32 [2, 1179648], P('mp', 'dp')
- fc1_second_new: float32 [2, 1179648], P('mp', 'dp')
- fc2_new: float32 [2, 1179648], P('mp', 'dp')
- fc2_first_new: float32 [2, 1179648], P('mp', 'dp')
- fc2_second_new: float32 [2, 1179648], P('mp', 'dp')
- rep_new: float32 [6, 768], replicated
- rep_first_new: float32 [6, 768], replicated
- rep_second_new: float32 [6, 768], replicated
- split_new: float32 [2, 6, 384], P('mp')
- split_first_new: float32 [2, 6, 384], P('mp')
- split_second_new: float32 [2, 6, 384], P('mp')
Inputs may be any that keep to these rules, and one draw needn't show every extreme that they name: `lengths`: some strips have full length 529, at least one in every draw; the others lie between 66 and 396. `masked`: masked positions lie within the text; a strip of length L has max(L - 384, L // 4) of them, so at most 384 of its patches are visible, exactly 384 for a full-length strip. `dealing`: each strip stands in exactly one slot.
All inputs are finite; a program needn't handle non-finite values.
Results may differ from a plain program's by a relative error of at most 0.012.
Values may be sent and summed in bfloat16 or wider, within the bound.
No kernel may reach another device: no remote copies, remote signals or barrier semaphores. Data moves between devices by JAX's collectives and lax.ppermute only.
A program may use at most 960 MiB of HBM per device.

v0:
```python
import jax
import jax.numpy as jnp
from jax import lax
from jax.experimental import pallas as pl
from jax.experimental.pallas import tpu as pltpu
from jax.sharding import PartitionSpec as P

HEAD = 64
PATCHES = 529
STEP = 10


NORM_EPS = 1e-06
BETA_ONE = 0.9
BETA_TWO = 0.999
ADAM_EPS = 1e-08
MATRIX_RATE = 0.15
MATRIX_DECAY = 0.05
VECTOR_RATE = 0.6


def layer_norm(signal, norm_gain, norm_shift):
    average = jnp.mean(signal, axis=-1, keepdims=True)
    centered = signal - average
    spread = jnp.mean(centered * centered, axis=-1, keepdims=True)
    return centered * lax.rsqrt(spread + NORM_EPS) * norm_gain + norm_shift


def exact_gelu(signal):
    return jax.nn.gelu(signal, approximate=False)


def product(left, right):
    return jnp.dot(left, right, preferred_element_type=jnp.float32)


def contract_last(left, right):
    return lax.dot_general(
        left, right, (((1,), (1,)), ((), ())), preferred_element_type=jnp.float32
    )


def contract_rows(left, right):
    return lax.dot_general(
        left, right, (((0,), (0,)), ((), ())), preferred_element_type=jnp.float32
    )


def adam_step(weight, moment_one, moment_two, gradient, step_rate, decay_rate):
    one_new = BETA_ONE * moment_one + (1.0 - BETA_ONE) * gradient
    two_new = BETA_TWO * moment_two + (1.0 - BETA_TWO) * gradient * gradient
    one_hat = one_new / (1.0 - BETA_ONE**STEP)
    two_hat = two_new / (1.0 - BETA_TWO**STEP)
    weight_new = weight - step_rate * (
        one_hat / (jnp.sqrt(two_hat) + ADAM_EPS) + decay_rate * weight
    )
    return (weight_new, one_new, two_new)


def total_over_cores(partial):
    return partial.astype(jnp.float32) + swap_cores(partial).astype(jnp.float32)


def pair_scores(queries, key_rows, valid_rows):
    scores = jnp.einsum(
        "qhd,khd->hqk", queries, key_rows, preferred_element_type=jnp.float32
    ) * HEAD ** (-0.5)
    return jnp.where(valid_rows[None, None, :], scores, -1e30)


def attend_pair(pair_block):
    queries, key_rows, value_rows, valid_rows = pair_block
    scores = pair_scores(queries, key_rows, valid_rows)
    row_max = jnp.max(scores, axis=2, keepdims=True)
    lifted = jnp.exp(scores - row_max)
    row_total = jnp.sum(lifted, axis=2, keepdims=True)
    probability = (lifted / row_total).astype(jnp.bfloat16)
    attended = jnp.einsum(
        "hqk,khd->qhd", probability, value_rows, preferred_element_type=jnp.float32
    )
    return (attended.astype(jnp.bfloat16), row_max[:, :, 0] + jnp.log(row_total[:, :, 0]))


def attend_pair_back(pair_block):
    queries, key_rows, value_rows, valid_rows, log_total, grad_attended = pair_block
    scores = pair_scores(queries, key_rows, valid_rows)
    probability = jnp.exp(scores - log_total[:, :, None])
    grad_prob = jnp.einsum(
        "qhd,khd->hqk", grad_attended, value_rows, preferred_element_type=jnp.float32
    )
    inner_sum = jnp.sum(probability * grad_prob, axis=2, keepdims=True)
    grad_scores = (probability * (grad_prob - inner_sum)).astype(jnp.bfloat16)
    score_scale = HEAD ** (-0.5)
    grad_queries = (
        jnp.einsum("hqk,khd->qhd", grad_scores, key_rows, preferred_element_type=jnp.float32)
        * score_scale
    )
    grad_keys = (
        jnp.einsum("hqk,qhd->khd", grad_scores, queries, preferred_element_type=jnp.float32)
        * score_scale
    )
    grad_values = jnp.einsum(
        "hqk,qhd->khd",
        probability.astype(jnp.bfloat16),
        grad_attended,
        preferred_element_type=jnp.float32,
    )
    return (
        grad_queries.astype(jnp.bfloat16),
        grad_keys.astype(jnp.bfloat16),
        grad_values.astype(jnp.bfloat16),
    )


def hop(array, distance, axis_count):
    return lax.ppermute(array, "dp", [(i, i ^ distance) for i in range(axis_count)])


def swap_cores(array):
    return lax.ppermute(array, "mp", [(0, 1), (1, 0)])


def place_chunks(pieces, chunk_ids, member, count):
    rows, width = pieces[0].shape[1:]

    def body(member_ref, *refs):
        sources, target, semaphores = refs[:-2], refs[-2], refs[-1]
        copies = []
        for source, ids in zip(sources, chunk_ids):
            for place, distance in enumerate(ids):
                copies.append(
                    pltpu.make_async_copy(
                        source.at[place],
                        target.at[member_ref[0] ^ distance],
                        semaphores.at[len(copies)],
                    )
                )
        for copy in copies:
            copy.start()
        for copy in copies:
            copy.wait()

    return pl.pallas_call(
        body,
        in_specs=[pl.BlockSpec(memory_space=pltpu.SMEM)]
        + [pl.BlockSpec(memory_space=pl.ANY)] * len(pieces),
        out_specs=pl.BlockSpec(memory_space=pltpu.VMEM),
        out_shape=jax.ShapeDtypeStruct((count, rows, width), pieces[0].dtype),
        scratch_shapes=[pltpu.SemaphoreType.DMA((count,))],
        cost_estimate=pl.CostEstimate(
            flops=0, transcendentals=0, bytes_accessed=4 * count * rows * width
        ),
        name="place_chunks",
    )(member, *pieces)


def pick_chunks(whole, chunk_ids, member):
    count, rows, width = whole.shape

    def body(member_ref, source, *refs):
        targets, semaphores = refs[:-1], refs[-1]
        copies = []
        for target, ids in zip(targets, chunk_ids):
            for place, distance in enumerate(ids):
                copies.append(
                    pltpu.make_async_copy(
                        source.at[member_ref[0] ^ distance],
                        target.at[place],
                        semaphores.at[len(copies)],
                    )
                )
        for copy in copies:
            copy.start()
        for copy in copies:
            copy.wait()

    return pl.pallas_call(
        body,
        in_specs=[pl.BlockSpec(memory_space=pltpu.SMEM), pl.BlockSpec(memory_space=pltpu.VMEM)],
        out_specs=[pl.BlockSpec(memory_space=pl.ANY)] * len(chunk_ids),
        out_shape=[
            jax.ShapeDtypeStruct((len(ids), rows, width), whole.dtype) for ids in chunk_ids
        ],
        scratch_shapes=[pltpu.SemaphoreType.DMA((count,))],
        cost_estimate=pl.CostEstimate(
            flops=0, transcendentals=0, bytes_accessed=4 * count * rows * width
        ),
        name="pick_chunks",
    )(member, whole)


def gather_chunks(chunk, member, count):
    own = chunk[None]
    if count == 16:
        near, far, last = (hop(own, k, count) for k in (4, 8, 12))
        first, second = jnp.concatenate([own, near]), jnp.concatenate([far, last])
        x_first, x_second = hop(first, 1, count), hop(second, 1, count)
        y_first, y_second = hop(first, 2, count), hop(second, 2, count)
        d_first, d_second = hop(y_first, 1, count), hop(x_second, 2, count)
        pieces = [first, second, x_first, x_second, y_first, y_second, d_first, d_second]
        ids = [(0, 4), (8, 12), (1, 5), (9, 13), (2, 6), (10, 14), (3, 7), (11, 15)]
    else:
        held, step = own, 1
        while step < count:
            held = jnp.concatenate([held, hop(held, step, count)])
            step *= 2
        pieces, ids = [held], [tuple(range(count))]
    return place_chunks(pieces, ids, member, count)


def scatter_chunks(whole, member, count):
    def wide(array):
        return array.astype(jnp.float32)

    if count == 16:
        ids = [(3, 7), (11, 15), (2, 6), (9, 13), (10, 14), (1, 5), (0, 4), (8, 12)]
        d_first, d_second, y_first, x_second, y_second, x_first, first, second = pick_chunks(
            whole, ids, member
        )
        d_first, d_second = hop(d_first, 1, count), hop(d_second, 2, count)
        y_second, x_first = hop(y_second, 2, count), hop(x_first, 1, count)
        y_first = hop((wide(y_first) + wide(d_first)).astype(jnp.bfloat16), 2, count)
        x_second = hop((wide(x_second) + wide(d_second)).astype(jnp.bfloat16), 1, count)
        first = wide(first) + wide(y_first) + wide(x_first)
        second = wide(second) + wide(y_second) + wide(x_second)
        near = hop(first[1].astype(jnp.bfloat16), 4, count)
        far = hop(second[0].astype(jnp.bfloat16), 8, count)
        last = hop(second[1].astype(jnp.bfloat16), 12, count)
        return first[0] + wide(near) + wide(far) + wide(last)
    (held,) = pick_chunks(whole, [tuple(range(count))], member)
    held = wide(held)
    step = count // 2
    while step:
        held = held[:step] + wide(hop(held[step:].astype(jnp.bfloat16), step, count))
        step //= 2
    return held[0]


def sum_over_dp(vector, count):
    if count == 16:
        for low, high in ((1, 2), (4, 8)):
            other, third, fourth = (hop(vector, k, count) for k in (low, high, low + high))
            vector = (vector + other) + (third + fourth)
        return vector
    step = 1
    while step < count:
        vector = vector + hop(vector, step, count)
        step *= 2
    return vector


def on_device_general(
    patch_rows,
    cotangent,
    mask_token,
    lengths,
    masked,
    dealing,
    qkv_master,
    qkv_first,
    qkv_second,
    out_master,
    out_first,
    out_second,
    fc1_master,
    fc1_first,
    fc1_second,
    fc2_master,
    fc2_first,
    fc2_second,
    rep_master,
    rep_first,
    rep_second,
    split_master,
    split_first,
    split_second,
):
    slot_count, capacity, feature_width = patch_rows.shape
    half_width = mask_token.shape[0]
    dp_count = lax.axis_size("dp")
    member = lax.axis_index("dp")
    core_index = lax.axis_index("mp")
    positions_here = cotangent.shape[1]
    position_span = positions_here * dp_count
    heads_here = half_width // HEAD
    hidden_width = (split_master.shape[1] - 2) * half_width
    row_count = slot_count * capacity
    pair_count = slot_count // 2
    pair_length = 2 * capacity
    patch_index = jnp.arange(PATCHES, dtype=jnp.int32)
    visible_all = (patch_index[None, :] < lengths[:, None]) & (masked == 0)
    strips_here = lax.dynamic_slice_in_dim(dealing, member * slot_count, slot_count)
    visible_here = visible_all[strips_here]
    rank_here = jnp.cumsum(visible_here.astype(jnp.int32), axis=1) - 1
    counts_here = jnp.sum(visible_here.astype(jnp.int32), axis=1)
    valid_rows = jnp.arange(capacity, dtype=jnp.int32)[None, :] < counts_here[:, None]
    padding = position_span - PATCHES
    visible_padded = jnp.pad(visible_here, ((0, 0), (0, padding)))
    rank_padded = jnp.pad(jnp.maximum(rank_here, 0), ((0, 0), (0, padding)))
    own_positions = jnp.arange(positions_here, dtype=jnp.int32) * dp_count + member
    inside = own_positions < PATCHES
    visible_own = visible_all[:, jnp.minimum(own_positions, PATCHES - 1)] & inside[None, :]
    strip_count = lengths.shape[0]
    held_count = strip_count * positions_here
    strip_row = (
        jnp.arange(positions_here, dtype=jnp.int32)[None, :] * strip_count + dealing[:, None]
    ).reshape(held_count)
    deal = (
        strip_row[:, None] == jnp.arange(held_count, dtype=jnp.int32)[None, :]
    ).astype(jnp.bfloat16)
    encoder_row = jnp.where(
        visible_padded,
        rank_padded + jnp.arange(slot_count, dtype=jnp.int32)[:, None] * capacity,
        -1,
    )
    encoder_row = jnp.transpose(
        encoder_row.reshape(slot_count, positions_here, dp_count), (2, 0, 1)
    ).reshape(held_count)
    pick = (
        jnp.arange(row_count, dtype=jnp.int32)[:, None] == encoder_row[None, :]
    ).astype(jnp.bfloat16)
    unseen = jnp.transpose(jnp.logical_not(visible_own) & inside[None, :]).reshape(held_count)
    member_word = member.astype(jnp.int32).reshape(1)

    cotangent_rows = jnp.transpose(cotangent.reshape(strip_count, positions_here, half_width), (1, 0, 2))
    cotangent_rows = cotangent_rows.reshape(held_count, half_width)
    dealt = product(deal, cotangent_rows).astype(jnp.bfloat16)
    returned = lax.all_to_all(
        dealt.reshape(dp_count, slot_count * positions_here, half_width),
        "dp",
        split_axis=0,
        concat_axis=0,
        tiled=True,
    ).reshape(held_count, half_width)
    gathered = product(pick, returned).astype(jnp.bfloat16)
    gathered_other = swap_cores(gathered)
    grad_out = jnp.where(
        core_index == 0,
        jnp.concatenate([gathered, gathered_other], axis=1),
        jnp.concatenate([gathered_other, gathered], axis=1),
    )
    mask_grad = product(unseen.astype(jnp.bfloat16)[None, :], cotangent_rows)[0]

    def gathered_matrix(master, rows, width):
        chunk = master.astype(jnp.bfloat16).reshape(rows // dp_count, width)
        return gather_chunks(chunk, member_word, dp_count).reshape(rows, width)

    w_attention = gathered_matrix(qkv_master, feature_width, 3 * half_width)
    w_output = gathered_matrix(out_master, half_width, feature_width)
    w_first = gathered_matrix(fc1_master, feature_width, hidden_width)
    w_second = gathered_matrix(fc2_master, hidden_width, feature_width)
    inputs = patch_rows.reshape(row_count, feature_width).astype(jnp.float32)
    normed_full, norm_back_one = jax.vjp(layer_norm, inputs, rep_master[0], rep_master[1])
    normed = normed_full.astype(jnp.bfloat16)
    projected = product(normed, w_attention).reshape(row_count, 3, half_width)
    queries = (projected[:, 0] + split_master[0, 0]).astype(jnp.bfloat16)
    key_rows = projected[:, 1].astype(jnp.bfloat16)
    value_rows = (projected[:, 2] + split_master[0, 1]).astype(jnp.bfloat16)

    def by_pair(array):
        return array.reshape(pair_count, pair_length, heads_here, HEAD)

    pair_valid = valid_rows.reshape(pair_count, pair_length)
    attended, log_total = lax.map(
        attend_pair, (by_pair(queries), by_pair(key_rows), by_pair(value_rows), pair_valid)
    )
    attended = attended.reshape(row_count, half_width)
    branch = total_over_cores(product(attended, w_output)) + rep_master[4]
    middle = inputs + branch
    normed_two_full, norm_back_two = jax.vjp(layer_norm, middle, rep_master[2], rep_master[3])
    normed_two = normed_two_full.astype(jnp.bfloat16)
    hidden = product(normed_two, w_first) + split_master[0, 2:].reshape(hidden_width)
    active_full, gelu_back = jax.vjp(exact_gelu, hidden)
    active = active_full.astype(jnp.bfloat16)
    second = total_over_cores(product(active, w_second).astype(jnp.bfloat16)) + rep_master[5]
    result = (middle + second).astype(jnp.bfloat16)
    result_half = lax.dynamic_slice_in_dim(result, core_index * half_width, half_width, 1)
    outgoing = contract_rows(pick, result_half).astype(jnp.bfloat16)
    arrived = lax.all_to_all(
        outgoing.reshape(dp_count, slot_count * positions_here, half_width),
        "dp",
        split_axis=0,
        concat_axis=0,
        tiled=True,
    ).reshape(held_count, half_width)
    full_out = contract_rows(deal, arrived)
    full_out = jnp.where(unseen[:, None], mask_token.astype(jnp.float32)[None, :], full_out)
    full_out = full_out.astype(jnp.bfloat16).reshape(positions_here, strip_count, half_width)
    full_out = jnp.transpose(full_out, (1, 0, 2))[:, :, None, :]
    grad_rows = grad_out.astype(jnp.float32)
    bias_two_grad = jnp.sum(grad_rows, axis=0)
    grad_active = contract_last(grad_out, w_second)
    grad_hidden = gelu_back(grad_active)[0].astype(jnp.bfloat16)
    fc2_grad = contract_rows(active, grad_out)
    fc1_grad = contract_rows(normed_two, grad_hidden)
    hidden_bias_grad = jnp.sum(grad_hidden.astype(jnp.float32), axis=0)
    grad_normed_two = total_over_cores(contract_last(grad_hidden, w_first))
    grad_middle_part, gain_two_grad, shift_two_grad = norm_back_two(grad_normed_two)
    grad_middle = grad_rows + grad_middle_part
    grad_branch = grad_middle.astype(jnp.bfloat16)
    out_bias_grad = jnp.sum(grad_branch.astype(jnp.float32), axis=0)
    out_grad = contract_rows(attended, grad_branch)
    grad_attended = contract_last(grad_branch, w_output).astype(jnp.bfloat16)
    grad_queries, grad_keys, grad_values = lax.map(
        attend_pair_back,
        (
            by_pair(queries),
            by_pair(key_rows),
            by_pair(value_rows),
            pair_valid,
            log_total,
            by_pair(grad_attended),
        ),
    )
    grad_queries = grad_queries.reshape(row_count, half_width)
    grad_keys = grad_keys.reshape(row_count, half_width)
    grad_values = grad_values.reshape(row_count, half_width)
    grad_projected = jnp.stack([grad_queries, grad_keys, grad_values], axis=1).reshape(
        row_count, 3 * half_width
    )
    qkv_grad = contract_rows(normed, grad_projected)
    query_bias_grad = jnp.sum(grad_queries.astype(jnp.float32), axis=0)
    value_bias_grad = jnp.sum(grad_values.astype(jnp.float32), axis=0)
    grad_normed = total_over_cores(contract_last(grad_projected, w_attention))
    grad_inputs_part, gain_one_grad, shift_one_grad = norm_back_one(grad_normed)
    input_grad = (grad_middle + grad_inputs_part).reshape(slot_count, capacity, feature_width)
    def scattered(gradient):
        rows, width = gradient.shape
        chunks = gradient.astype(jnp.bfloat16).reshape(dp_count, rows // dp_count, width)
        return scatter_chunks(chunks, member_word, dp_count).reshape(1, -1)

    fc2_total = scattered(fc2_grad)
    fc1_total = scattered(fc1_grad)
    out_total = scattered(out_grad)
    qkv_total = scattered(qkv_grad)
    rep_grad = jnp.stack(
        [gain_one_grad, shift_one_grad, gain_two_grad, shift_two_grad, out_bias_grad, bias_two_grad]
    )
    split_grad = jnp.concatenate(
        [query_bias_grad[None], value_bias_grad[None], hidden_bias_grad.reshape(-1, half_width)],
        axis=0,
    )[None]
    packed = jnp.concatenate([mask_grad, rep_grad.reshape(-1), split_grad.reshape(-1)])
    packed = sum_over_dp(packed.reshape(-1, 128), dp_count).reshape(-1)
    mask_total = packed[:half_width]
    rep_total = packed[half_width : half_width + rep_grad.size].reshape(rep_grad.shape)
    split_total = packed[half_width + rep_grad.size :].reshape(split_grad.shape)
    qkv_new = adam_step(qkv_master, qkv_first, qkv_second, qkv_total, MATRIX_RATE, MATRIX_DECAY)
    out_new = adam_step(out_master, out_first, out_second, out_total, MATRIX_RATE, MATRIX_DECAY)
    fc1_new = adam_step(fc1_master, fc1_first, fc1_second, fc1_total, MATRIX_RATE, MATRIX_DECAY)
    fc2_new = adam_step(fc2_master, fc2_first, fc2_second, fc2_total, MATRIX_RATE, MATRIX_DECAY)
    rep_new = adam_step(rep_master, rep_first, rep_second, rep_total, VECTOR_RATE, 0.0)
    split_new = adam_step(split_master, split_first, split_second, split_total, VECTOR_RATE, 0.0)
    return (
        full_out,
        input_grad,
        mask_total,
        qkv_new[0],
        qkv_new[1],
        qkv_new[2],
        out_new[0],
        out_new[1],
        out_new[2],
        fc1_new[0],
        fc1_new[1],
        fc1_new[2],
        fc2_new[0],
        fc2_new[1],
        fc2_new[2],
        rep_new[0],
        rep_new[1],
        rep_new[2],
        split_new[0],
        split_new[1],
        split_new[2],
    )


BLOCK = 384
UNIT_ROWS = 48
UNIT_WIDTH = 1536
Z_ORDER = (0, 12, 4, 8)
VMEM_BYTES = 60 * 1024 * 1024
ANY = pl.BlockSpec(memory_space=pl.ANY)
IN_VMEM = pl.BlockSpec(memory_space=pltpu.VMEM)
IN_SMEM = pl.BlockSpec(memory_space=pltpu.SMEM)


def shaped(shape, dtype):
    return jax.ShapeDtypeStruct(shape, dtype)


def params(grid_axes=0):
    semantics = ("arbitrary",) * grid_axes if grid_axes else None
    return pltpu.CompilerParams(dimension_semantics=semantics, vmem_limit_bytes=VMEM_BYTES)


def cost(microseconds):
    return pl.CostEstimate(
        flops=int(microseconds * 1.15e9), transcendentals=0, bytes_accessed=1000000
    )


def together(*values):
    return lax.optimization_barrier(values)


def hop_by_core(array, first_core, second_core, count):
    pairs = []
    for i in range(count):
        pairs.append((2 * i, 2 * (i ^ first_core)))
        pairs.append((2 * i + 1, 2 * (i ^ second_core) + 1))
    return lax.ppermute(array, ("dp", "mp"), pairs)


def pack_units(qkv, out, fc1, fc2):
    def body(qkv_ref, out_ref, fc1_ref, fc2_ref, unit_a, unit_b, unit_c):
        def put(unit, column, rows):
            unit[0, :, column * 128 : (column + 1) * 128] = rows.astype(jnp.bfloat16)

        for j in range(9):
            put(unit_a, j, qkv_ref[pl.ds(j, UNIT_ROWS, stride=9), :])
        for j in range(3):
            put(unit_a, 9 + j, out_ref[pl.ds(j, UNIT_ROWS, stride=3), :])
        for j in range(12):
            put(unit_b, j, fc1_ref[pl.ds(j, UNIT_ROWS, stride=12), :])
        for half in range(2):
            for j in range(6):
                start = half * UNIT_ROWS * 6 + j
                put(unit_c, half * 6 + j, fc2_ref[pl.ds(start, UNIT_ROWS, stride=6), :])

    unit = shaped((1, UNIT_ROWS, UNIT_WIDTH), jnp.bfloat16)
    return pl.pallas_call(
        body,
        out_shape=[unit, unit, unit],
        compiler_params=params(),
        cost_estimate=cost(2),
        name="pack_units",
    )(
        *(array.reshape(-1, 128) for array in (qkv, out, fc1, fc2))
    )


def owner_of(words, piece, entry):
    extra = (0, words[1], words[2], 3)[piece]
    return words[0] ^ Z_ORDER[entry] ^ extra


def join_chunks(chunks):
    def body(*refs):
        for entry, ref in enumerate(refs[:-1]):
            refs[-1][entry] = ref[0]

    return pl.pallas_call(
        body,
        out_shape=shaped((len(chunks),) + chunks[0].shape[1:], chunks[0].dtype),
        compiler_params=params(),
        cost_estimate=cost(1.3),
        name="join_chunks",
    )(*chunks)


def last_messages(kept, one, two, carried):
    def body(kept_ref, one_ref, two_ref, carried_ref, *targets):
        vectors = carried_ref[...].astype(jnp.float32)
        vectors = (vectors + two_ref[4 * UNIT_ROWS :, :].astype(jnp.float32)).astype(jnp.bfloat16)
        for entry, target in enumerate(targets):
            rows = slice((entry + 1) * UNIT_ROWS, (entry + 2) * UNIT_ROWS)
            total = kept_ref[rows, :].astype(jnp.float32) + one_ref[rows, :].astype(jnp.float32)
            total = total + two_ref[rows, :].astype(jnp.float32)
            target[:UNIT_ROWS, :] = total.astype(jnp.bfloat16)
            target[UNIT_ROWS:, :] = vectors

    def rows(count, start=0):
        return pl.BlockSpec((count, UNIT_WIDTH), lambda i: (start, 0))

    message = shaped((UNIT_ROWS + 16, UNIT_WIDTH), jnp.bfloat16)
    return pl.pallas_call(
        body,
        grid=(1,),
        in_specs=[
            rows(4 * UNIT_ROWS), rows(4 * UNIT_ROWS), rows(4 * UNIT_ROWS + 16),
            rows(16, 4 * UNIT_ROWS // 16),
        ],
        out_specs=[rows(UNIT_ROWS + 16)] * 3,
        out_shape=[message] * 3,
        compiler_params=params(1),
        cost_estimate=cost(1.5),
        name="last_messages",
    )(kept, one, two, carried)


def added(start, stop, *arrays):
    total = 0.0
    for array, offset in arrays:
        total = total + array[start - offset : stop - offset].astype(jnp.float32)
    return total.astype(jnp.bfloat16)


def unit_shapes(extra=0):
    return [shaped((8 * UNIT_ROWS + extra, UNIT_WIDTH), jnp.bfloat16)] * 2


def unit_targets(words, sent, kept):
    def rows(array, entry):
        return array.at[pl.ds(entry * UNIT_ROWS, UNIT_ROWS), :]

    places = []
    for entry, distance in enumerate(Z_ORDER):
        own = words[0] ^ distance
        places.append((rows(sent, 4 + entry), own ^ 3))
        places.append((rows(sent, entry), own ^ words[2]))
        places.append((rows(kept, entry), own))
        places.append((rows(kept, 4 + entry), own ^ words[1]))
    return places


def unit_rows(owner, rows=UNIT_ROWS):
    return pl.ds(pl.multiple_of(owner * rows, 16), rows)


def norm_parts(signal):
    average = jnp.mean(signal, axis=1, keepdims=True)
    centered = signal - average
    scale = lax.rsqrt(jnp.mean(centered * centered, axis=1, keepdims=True) + NORM_EPS)
    return centered * scale, scale


def norm_back(grad, unit_signal, scale, gain):
    scaled = grad * gain
    mean_one = jnp.mean(scaled, axis=1, keepdims=True)
    mean_two = jnp.mean(scaled * unit_signal, axis=1, keepdims=True)
    return scale * (scaled - mean_one - unit_signal * mean_two)


def first_norm(rows, rep):
    count, width = rows.shape

    def body(rows_ref, rep_ref, normed_ref):
        unit_signal, _ = norm_parts(rows_ref[...].astype(jnp.float32))
        normed = unit_signal * rep_ref[0:1, :] + rep_ref[1:2, :]
        normed_ref[...] = normed.astype(jnp.bfloat16)

    return pl.pallas_call(
        body,
        grid=(count // BLOCK,),
        in_specs=[
            pl.BlockSpec((BLOCK, width), lambda i: (i, 0)),
            pl.BlockSpec(rep.shape, lambda i: (0, 0)),
        ],
        out_specs=pl.BlockSpec((BLOCK, width), lambda i: (i, 0)),
        out_shape=shaped((count, width), jnp.bfloat16),
        compiler_params=params(1),
        cost_estimate=cost(3.5),
        name="first_norm",
    )(rows, rep)


def fixed(*shape):
    return pl.BlockSpec(shape, lambda i: (0,) * len(shape))


def run_copies(pairs, semaphores):
    copies = [
        pltpu.make_async_copy(source, target, semaphores.at[i])
        for i, (source, target) in enumerate(pairs)
    ]
    for copy in copies:
        copy.start()
    for copy in copies:
        copy.wait()


class Copies:
    def __init__(self, semaphores):
        self.semaphores, self.used = semaphores, 0

    def start(self, pairs):
        started = []
        for source, target in pairs:
            copy = pltpu.make_async_copy(source, target, self.semaphores.at[self.used])
            self.used += 1
            copy.start()
            started.append(copy)
        return started


def finish(copies):
    for copy in copies:
        copy.wait()


def chunk_pairs(words_ref, pieces, target):
    pairs = []
    for piece, source in enumerate(pieces):
        for entry in range(4):
            owner = owner_of(words_ref, piece, entry)
            pairs.append((source.at[entry], target.at[unit_rows(owner), :]))
    return pairs


def attention_forward(words, normed, split, column_bias, pieces):
    count, width = normed.shape
    half = split.shape[1]
    pairs_of_heads = half // (2 * HEAD)

    def body(
        words_ref, normed_ref, split_ref, bias_ref, p0, p1, p2, p3,
        qkv_ref, prob_ref, attended_ref, partial_ref, weights_ref, w_out_ref, spread, semaphores,
    ):
        pair = pl.program_id(0)

        @pl.when(pair == 0)
        def _():
            copies = Copies(semaphores)
            finish(copies.start(chunk_pairs(words_ref, (p0, p1, p2, p3), weights_ref)))
            for block in range(count // BLOCK):
                rows = pl.ds(block * BLOCK, BLOCK)
                for part in range(3):
                    columns = slice(part * half, (part + 1) * half)
                    projected = product(normed_ref[rows, :], weights_ref[:, columns])
                    if part != 1:
                        projected = projected + split_ref[part // 2 : part // 2 + 1, :]
                    qkv_ref[rows, columns] = projected.astype(jnp.bfloat16)

        lane = pl.multiple_of(pair * (2 * HEAD), 2 * HEAD)
        upper = lax.broadcasted_iota(jnp.int32, (1, 2 * HEAD), 1) >= HEAD
        keys = qkv_ref[:, pl.ds(half + lane, 2 * HEAD)]
        values = qkv_ref[:, pl.ds(2 * half + lane, 2 * HEAD)]
        for block in range(count // BLOCK):
            rows = pl.ds(block * BLOCK, BLOCK)
            queries = qkv_ref[rows, pl.ds(lane, 2 * HEAD)]
            found = []
            for side in range(2):
                chosen = upper if side else jnp.logical_not(upper)
                own = jnp.where(chosen, queries, jnp.zeros_like(queries))
                scores = contract_last(own, keys) * HEAD ** (-0.5) + bias_ref[...]
                lifted = jnp.exp(scores - jnp.max(scores, axis=1, keepdims=True))
                total = jnp.sum(lifted, axis=1, keepdims=True)
                probability = (lifted * (1.0 / total)).astype(jnp.bfloat16)
                prob_ref[side, rows, :] = probability
                found.append(product(probability, values))
            attended = jnp.where(upper, found[1], found[0])
            attended_ref[rows, pl.ds(lane, 2 * HEAD)] = attended.astype(jnp.bfloat16)

        @pl.when(pair == pairs_of_heads - 1)
        def _():
            for strip in range(half // 128):
                start = 3 * half + strip * 128
                spread[strip] = weights_ref[:, start : start + 128].astype(jnp.float32)
                for side in range(2):
                    start = side * half + strip * 128
                    w_out_ref[:, start : start + 128] = spread[
                        strip, pl.ds(side, half, stride=2), :
                    ].astype(jnp.bfloat16)
            partial_ref[...] = product(attended_ref[...], w_out_ref[...]).astype(jnp.bfloat16)

    return pl.pallas_call(
        body,
        grid=(pairs_of_heads,),
        in_specs=[IN_SMEM, fixed(count, width), fixed(6, half), fixed(1, count)] + [ANY] * 4,
        out_specs=[
            fixed(count, 3 * half),
            pl.BlockSpec((2, count, count), lambda h: (h, 0, 0)),
            fixed(count, half),
            fixed(count, width),
            fixed(width, UNIT_WIDTH),
            fixed(half, width),
        ],
        out_shape=[
            shaped((count, 3 * half), jnp.bfloat16),
            shaped((2 * pairs_of_heads, count, count), jnp.bfloat16),
            shaped((count, half), jnp.bfloat16),
            shaped((count, width), jnp.bfloat16),
            shaped((width, UNIT_WIDTH), jnp.bfloat16),
            shaped((half, width), jnp.bfloat16),
        ],
        scratch_shapes=[
            pltpu.VMEM((half // 128, width, 128), jnp.float32),
            pltpu.SemaphoreType.DMA((16,)),
        ],
        compiler_params=params(1),
        cost_estimate=cost(18),
        name="attention_forward",
    )(words, normed, split, column_bias, *pieces)


def mlp_all(words, rows_in, own, other, rep, split, grad_out, pieces_b, pieces_c):
    count, width = rows_in.shape
    half = split.shape[1]
    hidden_width = UNIT_WIDTH
    parts = hidden_width // half

    def body(
        words_ref, rep_ref, split_ref, in_any, own_any, other_any, grad_any,
        b0, b1, b2, b3, c0, c1, c2, c3,
        hidden_sum_ref, grad_sum_ref, middle_any, back_any, second_any,
        sent_b, kept_b, sent_c, kept_c,
        w_first, w_second, rows_ref, own_ref, other_ref, grad_ref, middle_ref, normed_ref,
        active_ref, slope_ref, grad_hidden_ref, back_ref, second_ref, whole_b, whole_c, semaphores,
    ):
        copies = Copies(semaphores)
        first_loads = copies.start(
            [(in_any, rows_ref), (own_any, own_ref), (other_any, other_ref)]
        )
        loads_b = copies.start(chunk_pairs(words_ref, (b0, b1, b2, b3), w_first))
        pairs = [(grad_any, grad_ref)]
        for piece, source in enumerate((c0, c1, c2, c3)):
            for entry in range(4):
                owner = owner_of(words_ref, piece, entry)
                for side in range(2):
                    pairs.append(
                        (
                            source.at[entry, :, pl.ds(side * width, width)],
                            w_second.at[unit_rows(owner * 2 + side), :],
                        )
                    )
        loads_c = copies.start(pairs)
        finish(first_loads)
        for block in range(count // BLOCK):
            rows = pl.ds(block * BLOCK, BLOCK)
            branch = own_ref[rows, :].astype(jnp.float32) + other_ref[rows, :].astype(jnp.float32)
            middle = rows_ref[rows, :].astype(jnp.float32) + branch + rep_ref[4:5, :]
            middle_ref[rows, :] = middle
            unit_signal, _ = norm_parts(middle)
            normed = unit_signal * rep_ref[2:3, :] + rep_ref[3:4, :]
            normed_ref[rows, :] = normed.astype(jnp.bfloat16)
        stores = copies.start([(middle_ref, middle_any)])
        finish(loads_b)
        for part in range(parts):
            columns = slice(part * half, (part + 1) * half)
            hidden = product(normed_ref[...], w_first[:, columns])
            hidden = hidden + split_ref[2 + part : 3 + part, :]
            spread = 0.5 + 0.5 * lax.erf(hidden * 0.7071067811865476)
            active_ref[:, columns] = (hidden * spread).astype(jnp.bfloat16)
            slope = spread + hidden * jnp.exp(-0.5 * hidden * hidden) * 0.3989422804014327
            slope_ref[:, columns] = slope.astype(jnp.bfloat16)
        finish(loads_c)
        second_ref[...] = product(active_ref[...], w_second[...]).astype(jnp.bfloat16)
        stores += copies.start([(second_ref, second_any)])
        grad_sum_ref[...] = jnp.sum(grad_ref[...].astype(jnp.float32), axis=0, keepdims=True)
        for part in range(parts):
            columns = slice(part * half, (part + 1) * half)
            grad_active = contract_last(grad_ref[...], w_second[columns, :])
            grad_hidden = grad_active * slope_ref[:, columns].astype(jnp.float32)
            grad_hidden = grad_hidden.astype(jnp.bfloat16)
            grad_hidden_ref[:, columns] = grad_hidden
            hidden_sum_ref[:, columns] = jnp.sum(
                grad_hidden.astype(jnp.float32), axis=0, keepdims=True
            )
        back_ref[...] = contract_last(grad_hidden_ref[...], w_first[...]).astype(jnp.bfloat16)
        stores += copies.start([(back_ref, back_any)])
        for part in range(parts):
            columns = slice(part * half, (part + 1) * half)
            whole_c[columns, :] = contract_rows(active_ref[:, columns], grad_ref[...]).astype(
                jnp.bfloat16
            )
        for target, owner in unit_targets(words_ref, sent_c, kept_c):
            stores += copies.start(
                [
                    (
                        whole_c.at[unit_rows(owner * 2 + side), :],
                        target.at[:, pl.ds(side * width, width)],
                    )
                    for side in range(2)
                ]
            )
        for part in range(width // half):
            columns = slice(part * half, (part + 1) * half)
            whole_b[columns, :] = contract_rows(normed_ref[:, columns], grad_hidden_ref[...]).astype(
                jnp.bfloat16
            )
        for target, owner in unit_targets(words_ref, sent_b, kept_b):
            stores += copies.start([(whole_b.at[unit_rows(owner), :], target)])
        finish(stores)

    low, full = jnp.bfloat16, jnp.float32
    return pl.pallas_call(
        body,
        in_specs=[IN_SMEM, IN_VMEM, IN_VMEM] + [ANY] * 12,
        out_specs=[IN_VMEM, IN_VMEM] + [ANY] * 7,
        out_shape=[
            shaped((1, hidden_width), full),
            shaped((1, width), full),
            shaped((count, width), full),
            shaped((count, width), low),
            shaped((count, width), low),
        ]
        + unit_shapes()
        + unit_shapes(),
        scratch_shapes=[
            pltpu.VMEM((width, hidden_width), low),
            pltpu.VMEM((hidden_width, width), low),
            pltpu.VMEM((count, width), low),
            pltpu.VMEM((count, width), low),
            pltpu.VMEM((count, width), low),
            pltpu.VMEM((count, width), low),
            pltpu.VMEM((count, width), full),
            pltpu.VMEM((count, width), low),
            pltpu.VMEM((count, hidden_width), low),
            pltpu.VMEM((count, hidden_width), low),
            pltpu.VMEM((count, hidden_width), low),
            pltpu.VMEM((count, width), low),
            pltpu.VMEM((count, width), low),
            pltpu.VMEM((width, hidden_width), low),
            pltpu.VMEM((hidden_width, width), low),
            pltpu.SemaphoreType.DMA((104,)),
        ],
        compiler_params=params(),
        cost_estimate=cost(18),
        name="mlp_all",
    )(words, rep, split, rows_in, own, other, grad_out, *pieces_b, *pieces_c)


def attention_back(
    words, rep, hidden_sum, grad_sum, mask_sum, middle, own, other, grad_out, w_out, attended, qkv,
    prob, normed, weights, rows_in,
):
    count, width = middle.shape
    half = qkv.shape[1] // 3
    span = 3 * half
    pairs_of_heads = half // (2 * HEAD)
    low, full = jnp.bfloat16, jnp.float32

    def body(
        words_ref, rep_ref, hidden_sum_ref, grad_sum_ref, mask_sum_ref,
        middle_any, own_any, other_any, grad_any, w_out_any, attended_any, qkv_any, prob_any,
        normed_any, weights_any, in_any,
        grad_middle_any, back_any, sent, kept,
        middle_ref, own_ref, other_ref, grad_ref, w_out_ref, attended_ref, qkv_ref, prob_ref,
        normed_ref, weights_ref, in_ref, grad_middle_ref, back_ref, branch, grad_attended,
        grad_qkv, spread, whole, vectors, low_vectors, semaphores,
    ):
        copies = Copies(semaphores)
        early = copies.start(
            [
                (middle_any, middle_ref), (own_any, own_ref), (other_any, other_ref),
                (grad_any, grad_ref),
            ]
        )
        outer = copies.start([(w_out_any, w_out_ref), (attended_any, attended_ref)])
        inner = copies.start([(qkv_any, qkv_ref)])
        probs = copies.start(
            [(prob_any.at[pl.ds(2 * pair, 2)], prob_ref.at[pair]) for pair in range(2)]
        )
        late = copies.start(
            [(normed_any, normed_ref), (weights_any, weights_ref), (in_any, in_ref)]
        )
        vectors[...] = jnp.zeros_like(vectors)
        finish(early)
        for block in range(count // BLOCK):
            rows = pl.ds(block * BLOCK, BLOCK)
            unit_signal, scale = norm_parts(middle_ref[rows, :])
            mine = own_ref[rows, :].astype(full)
            grad_normed = mine + other_ref[rows, :].astype(full)
            grad_middle = grad_ref[rows, :].astype(full) + norm_back(
                grad_normed, unit_signal, scale, rep_ref[2:3, :]
            )
            grad_middle_ref[rows, :] = grad_middle
            grad_branch = grad_middle.astype(low)
            branch[rows, :] = grad_branch
            vectors[1:2, :width] += jnp.sum(mine * unit_signal, axis=0, keepdims=True)
            vectors[1:2, width:] += jnp.sum(mine, axis=0, keepdims=True)
            vectors[2:3, :width] += 0.5 * jnp.sum(grad_branch.astype(full), axis=0, keepdims=True)
        stores = copies.start([(grad_middle_ref, grad_middle_any)])
        finish(outer)
        grad_attended[...] = contract_last(branch[...], w_out_ref[...]).astype(low)
        out_gradient = contract_rows(attended_ref[...], branch[...])
        for strip in range(half // 128):
            for side in range(2):
                start = side * half + strip * 128
                spread[strip, pl.ds(side, half, stride=2), :] = out_gradient[
                    :, start : start + 128
                ]
            start = span + strip * 128
            whole[:, start : start + 128] = spread[strip].astype(low)
        finish(inner)
        upper = lax.broadcasted_iota(jnp.int32, (1, 2 * HEAD), 1) >= HEAD
        for pair in range(pairs_of_heads):
            finish(probs[:1])
            probs = probs[1:]
            lanes = [slice(part * half + pair * 128, part * half + pair * 128 + 128) for part in range(3)]
            queries, keys, values = (qkv_ref[:, lane] for lane in lanes)
            grad = grad_attended[:, lanes[0]]
            found = []
            for side in range(2):
                chosen = upper if side else jnp.logical_not(upper)
                own_grad = jnp.where(chosen, grad, jnp.zeros_like(grad))
                low_probability = prob_ref[pair % 2, side]
                probability = low_probability.astype(full)
                weighted = probability * contract_last(own_grad, values)
                inner_sum = jnp.sum(weighted, axis=1, keepdims=True)
                grad_scores = (weighted - probability * inner_sum).astype(low)
                found.append(
                    (
                        product(grad_scores, keys),
                        contract_rows(queries, grad_scores)[side * HEAD : (side + 1) * HEAD],
                        contract_rows(grad, low_probability)[side * HEAD : (side + 1) * HEAD],
                    )
                )
            if pair + 2 < pairs_of_heads:
                probs += copies.start(
                    [(prob_any.at[pl.ds(2 * pair + 4, 2)], prob_ref.at[pair % 2])]
                )
            backs = (
                jnp.where(upper, found[1][0], found[0][0]) * HEAD ** (-0.5),
                jnp.transpose(jnp.concatenate([found[0][1], found[1][1]])) * HEAD ** (-0.5),
                jnp.transpose(jnp.concatenate([found[0][2], found[1][2]])),
            )
            for lane, value in zip(lanes, backs):
                grad_qkv[:, lane] = value.astype(low)
        finish(late)
        for part in range(width // half):
            columns = slice(part * half, (part + 1) * half)
            whole[columns, :span] = contract_rows(normed_ref[:, columns], grad_qkv[...]).astype(low)
        for target, owner in unit_targets(words_ref, sent, kept):
            stores += copies.start([(whole.at[unit_rows(owner), :], target)])
        for block in range(count // BLOCK):
            rows = pl.ds(block * BLOCK, BLOCK)
            back = contract_last(grad_qkv[rows, :], weights_ref[:, :span])
            back_ref[rows, :] = back.astype(low)
            unit_signal, _ = norm_parts(in_ref[rows, :].astype(full))
            vectors[0:1, :width] += jnp.sum(back * unit_signal, axis=0, keepdims=True)
            vectors[0:1, width:] += jnp.sum(back, axis=0, keepdims=True)
            for place, part in enumerate((0, 2)):
                sums = jnp.sum(
                    grad_qkv[rows, part * half : (part + 1) * half].astype(full),
                    axis=0,
                    keepdims=True,
                )
                vectors[3:4, place * half : (place + 1) * half] += sums
        stores += copies.start([(back_ref, back_any)])
        vectors[2:3, width:] = 0.5 * grad_sum_ref[...]
        vectors[3:4, 2 * half : span] = mask_sum_ref[...]
        vectors[4:5, :] = hidden_sum_ref[...]
        low_vectors[...] = vectors[...].astype(low)
        last = pl.ds(8 * UNIT_ROWS, 16)
        stores += copies.start([(low_vectors, sent.at[last, :]), (low_vectors, kept.at[last, :])])
        finish(stores)

    return pl.pallas_call(
        body,
        in_specs=[IN_SMEM] + [IN_VMEM] * 4 + [ANY] * 11,
        out_specs=[ANY] * 4,
        out_shape=[shaped((count, width), full), shaped((count, width), low)] + unit_shapes(16),
        scratch_shapes=[
            pltpu.VMEM((count, width), full),
            pltpu.VMEM((count, width), low),
            pltpu.VMEM((count, width), low),
            pltpu.VMEM((count, width), low),
            pltpu.VMEM((half, width), low),
            pltpu.VMEM((count, half), low),
            pltpu.VMEM((count, span), low),
            pltpu.VMEM((2, 2, count, count), low),
            pltpu.VMEM((count, width), low),
            pltpu.VMEM((width, UNIT_WIDTH), low),
            pltpu.VMEM((count, width), low),
            pltpu.VMEM((count, width), full),
            pltpu.VMEM((count, width), low),
            pltpu.VMEM((count, width), low),
            pltpu.VMEM((count, half), low),
            pltpu.VMEM((count, span), low),
            pltpu.VMEM((half // 128, width, 128), full),
            pltpu.VMEM((width, UNIT_WIDTH), low),
            pltpu.VMEM((16, UNIT_WIDTH), full),
            pltpu.VMEM((16, UNIT_WIDTH), low),
            pltpu.SemaphoreType.DMA((40,)),
        ],
        compiler_params=params(),
        cost_estimate=cost(22),
        name="attention_back",
    )(
        words, rep, hidden_sum, grad_sum, mask_sum, middle, own, other, grad_out, w_out, attended,
        qkv, prob, normed, weights, rows_in,
    )


def input_gradient(rows_in, own, other, grad_middle, rep):
    count, width = rows_in.shape

    def body(in_ref, own_ref, other_ref, middle_ref, rep_ref, out_ref):
        unit_signal, scale = norm_parts(in_ref[...].astype(jnp.float32))
        grad = own_ref[...].astype(jnp.float32) + other_ref[...].astype(jnp.float32)
        out_ref[...] = middle_ref[...] + norm_back(grad, unit_signal, scale, rep_ref[0:1, :])

    block = pl.BlockSpec((BLOCK, width), lambda i: (i, 0))
    return pl.pallas_call(
        body,
        grid=(count // BLOCK,),
        in_specs=[block, block, block, block, pl.BlockSpec(rep.shape, lambda i: (0, 0))],
        out_specs=block,
        out_shape=shaped((count, width), jnp.float32),
        compiler_params=params(1),
        cost_estimate=cost(5.7),
        name="input_gradient",
    )(rows_in, own, other, grad_middle, rep)


def adam_unit(units, states, strides):
    flat = [array.reshape(-1, 128) for state in states for array in state]
    terms = [array for unit in units for array in unit]
    counts = [len(unit) for unit in units]

    def body(*refs):
        terms_here, refs = refs[: len(terms)], refs[len(terms) :]
        inputs, outputs = refs[: len(flat)], refs[len(flat) :]
        for unit, column, state, start, step in strides:
            columns = slice(column * 128, (column + 1) * 128)
            skip = sum(counts[:unit])
            gradient = terms_here[skip][:, columns].astype(jnp.float32)
            for term in terms_here[skip + 1 : skip + counts[unit]]:
                gradient = gradient + term[:, columns].astype(jnp.float32)
            rows = pl.ds(start, UNIT_ROWS, stride=step)
            weight, one, two = (inputs[3 * state + i][rows, :] for i in range(3))
            updated = adam_step(weight, one, two, gradient, MATRIX_RATE, MATRIX_DECAY)
            for i in range(3):
                outputs[3 * state + i][rows, :] = updated[i]

    whole = [pl.BlockSpec(array.shape, lambda i: (0, 0)) for array in flat]
    results = pl.pallas_call(
        body,
        grid=(1,),
        in_specs=[
            pl.BlockSpec((UNIT_ROWS, term.shape[1]), lambda i: (0, 0)) for term in terms
        ]
        + whole,
        out_specs=whole,
        out_shape=[shaped(array.shape, jnp.float32) for array in flat],
        compiler_params=params(1),
        cost_estimate=cost(2.5),
        name="adam_unit",
    )(*terms, *flat)
    return [array.reshape(1, -1) for array in results]


def on_device(
    patch_rows,
    cotangent,
    mask_token,
    lengths,
    masked,
    dealing,
    qkv_master,
    qkv_first,
    qkv_second,
    out_master,
    out_first,
    out_second,
    fc1_master,
    fc1_first,
    fc1_second,
    fc2_master,
    fc2_first,
    fc2_second,
    rep_master,
    rep_first,
    rep_second,
    split_master,
    split_first,
    split_second,
):
    slot_count, capacity, feature_width = patch_rows.shape
    half_width = mask_token.shape[0]
    dp_count = lax.axis_size("dp")
    member = lax.axis_index("dp")
    core_index = lax.axis_index("mp")
    positions_here = cotangent.shape[1]
    position_span = positions_here * dp_count
    heads_here = half_width // HEAD
    row_count = slot_count * capacity
    strip_count = lengths.shape[0]
    position_rows = -(-positions_here // 4) * 4
    held_count = strip_count * positions_here
    dealt_count = strip_count * position_rows
    words = jnp.stack([member, 1 + core_index, 2 - core_index, core_index]).astype(jnp.int32)

    inputs = patch_rows.reshape(row_count, feature_width)
    split_rows = split_master[0]
    unit_a, unit_b, unit_c = pack_units(qkv_master, out_master, fc1_master, fc2_master)

    patch_index = jnp.arange(PATCHES, dtype=jnp.int32)
    visible_all = (patch_index[None, :] < lengths[:, None]) & (masked == 0)
    strips_here = lax.dynamic_slice_in_dim(dealing, member * slot_count, slot_count)
    visible_here = visible_all[strips_here]
    rank_here = jnp.cumsum(visible_here.astype(jnp.int32), axis=1) - 1
    counts_here = jnp.sum(visible_here.astype(jnp.int32), axis=1)
    valid_rows = jnp.arange(capacity, dtype=jnp.int32)[None, :] < counts_here[:, None]
    column_bias = jnp.where(valid_rows, 0.0, -1e30).astype(jnp.float32).reshape(1, row_count)
    padding = position_span - PATCHES
    visible_padded = jnp.pad(visible_here, ((0, 0), (0, padding)))
    rank_padded = jnp.pad(jnp.maximum(rank_here, 0), ((0, 0), (0, padding)))
    own_positions = jnp.arange(positions_here, dtype=jnp.int32) * dp_count + member
    inside = own_positions < PATCHES
    visible_own = visible_all[:, jnp.minimum(own_positions, PATCHES - 1)] & inside[None, :]
    row_time = jnp.arange(position_rows, dtype=jnp.int32)[None, :]
    strip_row = jnp.where(
        row_time < positions_here, row_time * strip_count + dealing[:, None], -1
    ).reshape(dealt_count)
    deal = (
        strip_row[:, None] == jnp.arange(held_count, dtype=jnp.int32)[None, :]
    ).astype(jnp.bfloat16)
    encoder_row = jnp.where(
        visible_padded,
        rank_padded + jnp.arange(slot_count, dtype=jnp.int32)[:, None] * capacity,
        -1,
    )
    encoder_row = jnp.transpose(
        encoder_row.reshape(slot_count, positions_here, dp_count), (2, 0, 1)
    )
    encoder_row = jnp.pad(
        encoder_row, ((0, 0), (0, 0), (0, position_rows - positions_here)), constant_values=-1
    ).reshape(dealt_count)
    pick = (
        jnp.arange(row_count, dtype=jnp.int32)[:, None] == encoder_row[None, :]
    ).astype(jnp.bfloat16)
    unseen = jnp.transpose(jnp.logical_not(visible_own) & inside[None, :]).reshape(held_count)

    cotangent_rows = jnp.transpose(
        cotangent.reshape(strip_count, positions_here, half_width), (1, 0, 2)
    ).reshape(held_count, half_width)

    def spread_out(array):
        return hop_by_core(array, 1, 2, dp_count), hop_by_core(array, 2, 1, dp_count)

    def exchanged(array):
        array = array.reshape(dp_count, slot_count * position_rows, half_width)
        array = lax.all_to_all(array, "dp", split_axis=0, concat_axis=0, tiled=True)
        return array.reshape(dealt_count, half_width)

    def columns_of(unit):
        return [hop(unit, distance, dp_count) for distance in Z_ORDER[1:]]

    column_a = columns_of(unit_a)
    normed = first_norm(inputs, rep_master)
    column_a, normed, unit_b, unit_c, cotangent_rows, deal, unseen = together(
        column_a, normed, unit_b, unit_c, cotangent_rows, deal, unseen
    )

    column_a = join_chunks([unit_a, *column_a])
    first_a, second_a = spread_out(column_a)
    column_b = columns_of(unit_b)
    dealt = product(deal, cotangent_rows).astype(jnp.bfloat16)
    mask_sum = product(unseen.astype(jnp.bfloat16)[None, :], cotangent_rows)
    first_a, second_a, column_b, dealt, mask_sum, column_bias, pick = together(
        first_a, second_a, column_b, dealt, mask_sum, column_bias, pick
    )

    third_a = hop_by_core(first_a, 2, 1, dp_count)
    column_c = columns_of(unit_c)
    returned = exchanged(dealt)
    column_b = join_chunks([unit_b, *column_b])
    third_a, column_c, normed, column_b = together(third_a, column_c, normed, column_b)

    first_b, second_b = spread_out(column_b)
    column_c = join_chunks([unit_c, *column_c])
    first_c, second_c = spread_out(column_c)
    qkv, prob, attended, branch, weights_a, w_output = attention_forward(
        words, normed, split_rows, column_bias, (column_a, first_a, second_a, third_a)
    )
    first_b, second_b, first_c, second_c = together(first_b, second_b, first_c, second_c)

    third_b = hop_by_core(first_b, 2, 1, dp_count)
    third_c = hop_by_core(first_c, 2, 1, dp_count)
    branch_other = swap_cores(branch)
    gathered = product(pick, returned).astype(jnp.bfloat16)
    gathered_other = swap_cores(gathered)
    grad_out = jnp.where(
        core_index == 0,
        jnp.concatenate([gathered, gathered_other], axis=1),
        jnp.concatenate([gathered_other, gathered], axis=1),
    )
    third_b, third_c, branch_other, grad_out = together(third_b, third_c, branch_other, grad_out)

    hidden_sum, grad_sum, middle, back_two, second, sent_b, kept_b, sent_c, kept_c = mlp_all(
        words, inputs, branch, branch_other, rep_master, split_rows, grad_out,
        (column_b, first_b, second_b, third_b), (column_c, first_c, second_c, third_c),
    )
    middle, back_two, second, sent_b, kept_b, sent_c, kept_c = together(
        middle, back_two, second, sent_b, kept_b, sent_c, kept_c
    )

    one_c = hop_by_core(sent_c, 2, 1, dp_count)
    back_two_other = swap_cores(back_two)
    second_other = swap_cores(second)
    total = second.astype(jnp.float32) + second_other.astype(jnp.float32) + rep_master[5]
    result = (middle + total).astype(jnp.bfloat16)
    result_half = lax.dynamic_slice_in_dim(result, core_index * half_width, half_width, 1)
    outgoing = contract_rows(pick, result_half).astype(jnp.bfloat16)
    one_c, back_two_other, outgoing = together(one_c, back_two_other, outgoing)

    half_unit, quarter, eighth = 4 * UNIT_ROWS, 2 * UNIT_ROWS, UNIT_ROWS
    one_b = hop_by_core(sent_b, 2, 1, dp_count)
    two_c = hop_by_core(
        added(half_unit, 2 * half_unit, (kept_c, 0), (one_c, 0)), 1, 2, dp_count
    )
    arrived = exchanged(outgoing)
    grad_middle, back_one, sent_a, kept_a = attention_back(
        words, rep_master, hidden_sum, grad_sum, mask_sum, middle, back_two, back_two_other,
        grad_out, w_output, attended, qkv, prob, normed, weights_a, inputs,
    )
    two_c, one_b, back_one, sent_a, kept_a, arrived = together(
        two_c, one_b, back_one, sent_a, kept_a, arrived
    )

    one_a = hop_by_core(sent_a, 2, 1, dp_count)
    back_one_other = swap_cores(back_one)
    two_b = hop_by_core(
        added(half_unit, 2 * half_unit, (kept_b, 0), (one_b, 0)), 1, 2, dp_count
    )
    three_c = hop(
        added(quarter, half_unit, (kept_c, 0), (one_c, 0), (two_c, 0)), 4, dp_count
    )
    full_out = contract_rows(deal, arrived)
    full_out = jnp.where(unseen[:, None], mask_token.astype(jnp.float32)[None, :], full_out)
    full_out = full_out.astype(jnp.bfloat16)
    one_a, three_c, two_b, back_one_other, full_out = together(
        one_a, three_c, two_b, back_one_other, full_out
    )

    two_a_sent = added(half_unit, 2 * half_unit + 16, (kept_a, 0), (one_a, 0))
    two_a = hop_by_core(two_a_sent, 1, 2, dp_count)
    three_b = hop(
        added(quarter, half_unit, (kept_b, 0), (one_b, 0), (two_b, 0)), 4, dp_count
    )
    four_c = hop(
        added(eighth, quarter, (kept_c, 0), (one_c, 0), (two_c, 0), (three_c, 0)), 12, dp_count
    )
    input_grad = input_gradient(inputs, back_one, back_one_other, grad_middle, rep_master)
    two_a_sent, two_a, four_c, three_b, input_grad = together(
        two_a_sent, two_a, four_c, three_b, input_grad
    )

    messages = last_messages(kept_a, one_a, two_a, two_a_sent)
    arrivals = [hop(message, k, dp_count) for message, k in zip(messages, Z_ORDER[1:])]
    four_b = hop(
        added(eighth, quarter, (kept_b, 0), (one_b, 0), (two_b, 0), (three_b, 0)), 12, dp_count
    )
    fc2_new = adam_unit(
        [(kept_c, one_c, two_c, three_c, four_c)],
        [(fc2_master, fc2_first, fc2_second)],
        [(0, side * 6 + j, 0, side * UNIT_ROWS * 6 + j, 6) for side in range(2) for j in range(6)],
    )
    arrivals, four_b, message, *fc2_new = together(arrivals, four_b, messages[0], *fc2_new)

    fc1_new = adam_unit(
        [(kept_b, one_b, two_b, three_b, four_b)],
        [(fc1_master, fc1_first, fc1_second)],
        [(0, j, 0, j, 12) for j in range(12)],
    )
    vectors = [array[eighth:].astype(jnp.float32) for array in (message, *arrivals)]
    vectors = (vectors[0] + vectors[1]) + (vectors[2] + vectors[3])
    rep_total = (vectors[:3] + swap_cores(vectors[:3])).reshape(rep_master.shape)
    split_total = jnp.concatenate(
        [vectors[3, : 2 * half_width], vectors[4]]
    ).reshape(split_master.shape)
    mask_total = vectors[3, 2 * half_width : 3 * half_width]
    qkv_out_new = adam_unit(
        [(kept_a, one_a, two_a, *arrivals)],
        [(qkv_master, qkv_first, qkv_second), (out_master, out_first, out_second)],
        [(0, j, 0, j, 9) for j in range(9)] + [(0, 9 + j, 1, j, 3) for j in range(3)],
    )
    full_out = full_out.reshape(positions_here, strip_count, half_width)
    full_out = jnp.transpose(full_out, (1, 0, 2))[:, :, None, :]
    input_grad = input_grad.reshape(slot_count, capacity, feature_width)
    rep_new = adam_step(rep_master, rep_first, rep_second, rep_total, VECTOR_RATE, 0.0)
    split_new = adam_step(split_master, split_first, split_second, split_total, VECTOR_RATE, 0.0)
    return (
        full_out,
        input_grad,
        mask_total,
        *qkv_out_new,
        *fc1_new,
        *fc2_new,
        *rep_new,
        *split_new,
    )


def solution(mesh):
    placed = (
        P("dp", None, None),
        P(None, None, "dp", "mp"),
        P("mp"),
        P(),
        P(),
        P(),
        P("mp", "dp"),
        P("mp", "dp"),
        P("mp", "dp"),
        P("mp", "dp"),
        P("mp", "dp"),
        P("mp", "dp"),
        P("mp", "dp"),
        P("mp", "dp"),
        P("mp", "dp"),
        P("mp", "dp"),
        P("mp", "dp"),
        P("mp", "dp"),
        P(),
        P(),
        P(),
        P("mp", None, None),
        P("mp", None, None),
        P("mp", None, None),
    )
    tuned = mesh.shape["dp"] == 16 and mesh.shape["mp"] == 2
    return jax.shard_map(
        on_device if tuned else on_device_general,
        mesh=mesh,
        in_specs=placed,
        out_specs=(
            P(None, None, "dp", "mp"),
            P("dp", None, None),
            P("mp"),
            P("mp", "dp"),
            P("mp", "dp"),
            P("mp", "dp"),
            P("mp", "dp"),
            P("mp", "dp"),
            P("mp", "dp"),
            P("mp", "dp"),
            P("mp", "dp"),
            P("mp", "dp"),
            P("mp", "dp"),
            P("mp", "dp"),
            P("mp", "dp"),
            P(),
            P(),
            P(),
            P("mp", None, None),
            P("mp", None, None),
            P("mp", None, None),
        ),
        check_vma=False,
    )
```

profile of v0, /device:TPU:0, one launch (start us, length us, event | category | flops | bytes accessed | tf_op | source)
XLA Modules:
  0.0 256.0 jit_solution(6052236109538873910)
XLA Ops:
  0.7 2.1 pack_units.1
  2.8 5.0 %collective-permute-start = (bf16[1,48,1536]{2,1,0:T(8,128)(2,1)}, bf16[1,48,1536]{2,1,0:T(8,128)(2,1)}, u32[]{:S(2)}, u32[]{:S(2)}) collective-permute-start(bf16[1,48,1536]{2,1,0:T(8,128)(2,1)} %get-tuple-element.124.refs_0_), channel_id=1, source_target_pairs={{0,24},{2,26},{4,28},{6,30},{8,16},{10,18},{12,20},{14,22},{16,8},... | collective-permute-start | bytes 442376 | tf_op jit(solution)/shard_map/ppermute | solution.py:116
  12.5 1.8 fusion.1
  14.3 2.7 %first_norm.1.normed_ref.normed_any = bf16[768,768]{1,0:T(8,128)(2,1)} custom-call(bf16[768,768]{1,0:T(8,128)(2,1)} %bitcast.79, f32[6,768]{1,0:T(8,128)} %rep_ref.7), custom_call_target="tpu_custom_call" | custom-call | flops 4024999936 | bytes 1000000 | tf_op jit(solution)/shard_map/first_norm/pallas_call | solution.py:644
  17.7 2.9 %collective-permute-done.2.refs_3_ = bf16[1,48,1536]{2,1,0:T(8,128)(2,1)} collective-permute-done((bf16[1,48,1536]{2,1,0:T(8,128)(2,1)}, bf16[1,48,1536]{2,1,0:T(8,128)(2,1)}, u32[]{:S(2)}, u32[]{:S(2)}) %collective-permute-start.2) | collective-permute-done | bytes 147488 | tf_op jit(solution)/shard_map/ppermute | solution.py:116
  20.7 2.0 join_chunks.3.p0
  22.7 1.5 collective-permute-start.3
  24.2 1.5 collective-permute-start.4
  25.7 2.5 collective-permute-start.5
  28.2 1.9 collective-permute-start.7
  30.1 2.6 %convolution_convert_fusion.1 = bf16[1152,384]{1,0:T(8,128)(2,1)} fusion(bf16[1152,1088]{1,0:T(8,128)(2,1)S(1)} %fusion, bf16[1088,384]{1,0:T(8,128)(2,1)S(1)} %bitcast.70), kind=kOutput, calls=%fused_computation.7 | convolution fusion | flops 963035136 | bytes 4227072 | tf_op jit(solution)/shard_map/dot_general | solution.py:34
  32.7 0.8 fusion.16.mask_sum_ref
  33.5 0.9 collective-permute-done.5.refs_1_
  35.0 4.4 %collective-permute-done.7.refs_3_ = bf16[1,48,1536]{2,1,0:T(8,128)(2,1)S(1)} collective-permute-done((bf16[1,48,1536]{2,1,0:T(8,128)(2,1)S(1)}, bf16[1,48,1536]{2,1,0:T(8,128)(2,1)S(1)}, u32[]{:S(2)}, u32[]{:S(2)}) %collective-permute-start.7) | collective-permute-done | bytes 147488 | tf_op jit(solution)/shard_map/ppermute | solution.py:116
  40.6 1.8 collective-permute-start.11
  42.4 2.5 collective-permute-start.9
  46.2 4.3 %all-to-all-start = ((bf16[16,72,384]{2,1,0:T(8,128)(2,1)}), bf16[16,72,384]{2,1,0:T(8,128)(2,1)}, u32[]{:S(2)}, u32[]{:S(2)}) async-start(bf16[16,72,384]{2,1,0:T(8,128)(2,1)} %bitcast.71), calls=%async_computation | async-start | bytes 1769472 | tf_op jit(solution)/shard_map/all_to_all | solution.py:1227
  50.5 2.0 join_chunks.4.b0
  52.5 8.6 %collective-permute-done.11.refs_3_ = bf16[1,48,1536]{2,1,0:T(8,128)(2,1)} collective-permute-done((bf16[1,48,1536]{2,1,0:T(8,128)(2,1)}, bf16[1,48,1536]{2,1,0:T(8,128)(2,1)}, u32[]{:S(2)}, u32[]{:S(2)}) %collective-permute-start.11) | collective-permute-done | bytes 147488 | tf_op jit(solution)/shard_map/ppermute | solution.py:116
  61.1 2.2 join_chunks.5.c0
  63.3 2.0 collective-permute-start.12
  65.3 2.0 collective-permute-start.13
  67.3 16.7 %attention_forward.1 = (bf16[768,1152]{1,0:T(8,128)(2,1)}, bf16[6,768,768]{2,1,0:T(8,128)(2,1)}, bf16[768,384]{1,0:T(8,128)(2,1)}, bf16[768,768]{1,0:T(8,128)(2,...) custom-call(s32[4]{0:T(128)} %pad_add_fusion.words_ref, bf16[768,768]{1,0:T(8,128)(2,1)} %first_norm.1.normed_ref.normed_any, ...), custom_call_target="tpu_custom_call" | custom-call | flops 20700000256 | bytes 1000000 | tf_op jit(solution)/shard_map/attention_forward/pallas_call | solution.py:758
  84.1 2.8 %convolution_convert_fusion.2 = bf16[768,384]{1,0:T(8,128)(2,1)S(1)} fusion(bf16[768,1152]{1,0:T(8,128)(2,1)} %fusion.1, bf16[1152,384]{1,0:T(8,128)(2,1)} %bitcast.15), kind=kOutput, calls=%fused_computation.9 | convolution fusion | flops 679772160 | bytes 3244032 | tf_op jit(solution)/shard_map/dot_general | solution.py:34
  87.5 1.7 collective-permute-done.12.b1
  89.8 1.5 collective-permute-start.17
  91.3 2.7 %maximum_select_fusion.grad_any = bf16[768,768]{1,0:T(8,128)(2,1)} fusion(bf16[768,384]{1,0:T(8,128)(2,1)} %collective-permute-done.19, bf16[768,384]{1,0:T(8,128)(2,1)S(1)} %convolution_convert_fusion.2, pred[]{:T(512)S(6)} %eq.46), kind=kLoop, calls=%fused_computation.13 | loop fusion | flops 5308416 | bytes 2359297 | tf_op jit(solution)/shard_map/jit(_where)/select_n | solution.py:1267
  94.0 5.4 %collective-permute-done.16.b3 = bf16[4,48,1536]{2,1,0:T(8,128)(2,1)} collective-permute-done((bf16[4,48,1536]{2,1,0:T(8,128)(2,1)}, bf16[4,48,1536]{2,1,0:T(8,128)(2,1)}, u32[]{:S(2)}, u32[]{:S(2)}) %collective-permute-start.16) | collective-permute-done | bytes 589856 | tf_op jit(solution)/shard_map/ppermute | solution.py:513
  99.5 6.3 %collective-permute-done.17.c3 = bf16[4,48,1536]{2,1,0:T(8,128)(2,1)} collective-permute-done((bf16[4,48,1536]{2,1,0:T(8,128)(2,1)}, bf16[4,48,1536]{2,1,0:T(8,128)(2,1)}, u32[]{:S(2)}, u32[]{:S(2)}) %collective-permute-start.17) | collective-permute-done | bytes 589856 | tf_op jit(solution)/shard_map/ppermute | solution.py:513
  105.8 31.5 %mlp_all.1 = (f32[1,1536]{1,0:T(1,128)}, f32[1,768]{1,0:T(1,128)}, f32[768,768]{1,0:T(8,128)}, bf16[768,768]{1,0:T(8,128)(2,1)}, bf16[768,768]{1,0:T(8,128)(2,1)...) custom-call(s32[4]{0:T(128)} %pad_add_fusion.words_ref, ...), custom_call_target="tpu_custom_call" | custom-call | flops 20700000256 | bytes 1000000 | tf_op jit(solution)/shard_map/mlp_all/pallas_call | solution.py:878
  137.9 1.1 collective-permute-start.21
  140.5 4.2 %convolution_convert_fusion = bf16[1152,384]{1,0:T(8,128)(2,1)} fusion(bf16[768,1152]{1,0:T(8,128)(2,1)} %fusion.1, f32[768,768]{1,0:T(8,128)} %get-tuple-element.169.middle_any, s32[]{:T(128)S(6)} %select_n.70, f32[384]{0:T(512)S(1)} %dynamic-slice, bf16[768,768]{1,0:T(8,128)(2,1)} %collective-permute-done.22, bf16[768,768]{1,0:T(8,128)(2,1)} %get-tuple-element.170), kind=kOutput, calls=%fused_computation.6 | convolution fusion | flops 681689088 | bytes 5015044 | tf_op jit(solution)/shard_map/dot_general | solution.py:44
  144.7 9.2 %collective-permute-done.20.refs_1_ = bf16[384,1536]{1,0:T(8,128)(2,1)} collective-permute-done((bf16[384,1536]{1,0:T(8,128)(2,1)}, bf16[384,1536]{1,0:T(8,128)(2,1)}, u32[]{:S(2)}, u32[]{:S(2)}) %collective-permute-start.20) | collective-permute-done | bytes 1179680 | tf_op jit(solution)/shard_map/ppermute | solution.py:513
  154.0 1.2 add_convert_fusion.2
  155.2 1.6 collective-permute-start.23
  156.7 6.3 %all-to-all-start.1 = ((bf16[16,72,384]{2,1,0:T(8,128)(2,1)}), bf16[16,72,384]{2,1,0:T(8,128)(2,1)}, u32[]{:S(2)}, u32[]{:S(2)}) async-start(bf16[16,72,384]{2,1,0:T(8,128)(2,1)} %bitcast.72), calls=%async_computation.1 | async-start | bytes 1769472 | tf_op jit(solution)/shard_map/all_to_all | solution.py:1227
  163.0 20.4 %attention_back.1 = (f32[768,768]{1,0:T(8,128)}, bf16[768,768]{1,0:T(8,128)(2,1)}, bf16[400,1536]{1,0:T(8,128)(2,1)}, bf16[400,1536]{1,0:T(8,128)(2,1)}) custom-call(s32[4]{0:T(128)} %pad_add_fusion.words_ref, f32[6,768]{1,0:T(8,128)} %rep_ref.7, f32[1,1536]{1,0:T(1,128)} %get-tuple-element.173.hidden_sum_ref, f32[1,768]{1,0:T(1,128)} %get-tuple-element.174.grad_sum_ref, ...), custom_call_target="tpu_custom_call" | custom-call | flops 25300000768 | bytes 1000000 | tf_op jit(solution)/shard_map/attention_back/pallas_call | solution.py:1041
  183.4 1.0 all-to-all-done.1
  184.5 1.7 collective-permute-start.25
  186.2 1.4 add_convert_fusion.1
  188.3 1.2 add_convert_fusion.4
  189.5 1.9 collective-permute-start.26
  191.4 3.8 %select_convert_fusion = bf16[1088,384]{1,0:T(8,128)(2,1)} fusion(bf16[384]{0:T(512)(128)(2,1)S(1)} %copy-done.31, pred[1088]{0:T(1024)(128)(4,1)S(1)} %reshape.314, bf16[1152,1088]{1,0:T(8,128)(2,1)S(1)} %fusion, bf16[1152,384]{1,0:T(8,128)(2,1)} %bitcast.17), kind=kOutput, calls=%fused_computation.8 | convolution fusion | flops 963010560 | bytes 4228928 | tf_op jit(solution)/shard_map/dot_general | solution.py:44
  195.2 4.2 %collective-permute-done.26.refs_3_ = bf16[96,1536]{1,0:T(8,128)(2,1)S(1)} collective-permute-done((bf16[96,1536]{1,0:T(8,128)(2,1)S(1)}, bf16[96,1536]{1,0:T(8,128)(2,1)S(1)}, u32[]{:S(2)}, u32[]{:S(2)}) %collective-permute-start.26) | collective-permute-done | bytes 294944 | tf_op jit(solution)/shard_map/ppermute | solution.py:116
  199.5 4.5 %collective-permute-done.27.refs_2_ = bf16[192,1536]{1,0:T(8,128)(2,1)S(1)} collective-permute-done((bf16[192,1536]{1,0:T(8,128)(2,1)S(1)}, bf16[192,1536]{1,0:T(8,128)(2,1)S(1)}, u32[]{:S(2)}, u32[]{:S(2)}) %collective-permute-start.27) | collective-permute-done | bytes 589856 | tf_op jit(solution)/shard_map/ppermute | solution.py:513
  204.0 3.8 %collective-permute-done.25.one_ref.refs_1_ = bf16[400,1536]{1,0:T(8,128)(2,1)S(1)} collective-permute-done((bf16[400,1536]{1,0:T(8,128)(2,1)}, bf16[400,1536]{1,0:T(8,128)(2,1)S(1)}, u32[]{:S(2)}, u32[]{:S(2)}) %collective-permute-start.25) | collective-permute-done | bytes 1228832 | tf_op jit(solution)/shard_map/ppermute | solution.py:513
  207.7 1.6 add_convert_fusion.3
  209.3 2.9 %collective-permute-start.31 = (bf16[96,1536]{1,0:T(8,128)(2,1)S(1)}, bf16[96,1536]{1,0:T(8,128)(2,1)S(1)}, u32[]{:S(2)}, u32[]{:S(2)}) collective-permute-start(bf16[96,1536]{1,0:T(8,128)(2,1)S(1)} %add_convert_fusion.3), channel_id=1, source_target_pairs={{0,8},{2,10},{4,12},{6,14},{8,0},{10,2},{12,4},{14,6},{16,24},{18,... | collective-permute-start | bytes 884744 | tf_op jit(solution)/shard_map/ppermute | solution.py:116
  212.7 1.1 add_convert_fusion.6
  213.8 2.6 %collective-permute-start.30 = (bf16[48,1536]{1,0:T(8,128)(2,1)S(1)}, bf16[48,1536]{1,0:T(8,128)(2,1)S(1)}, u32[]{:S(2)}, u32[]{:S(2)}) collective-permute-start(bf16[48,1536]{1,0:T(8,128)(2,1)S(1)} %add_convert_fusion.6), channel_id=1, source_target_pairs={{0,24},{2,26},{4,28},{6,30},{8,16},{10,18},{12,20},{14,22},{16,8},... | collective-permute-start | bytes 442376 | tf_op jit(solution)/shard_map/ppermute | solution.py:116
  216.4 4.8 %input_gradient.1 = f32[768,768]{1,0:T(8,128)} custom-call(bf16[768,768]{1,0:T(8,128)(2,1)} %bitcast.82, bf16[768,768]{1,0:T(8,128)(2,1)} %get-tuple-element.190.own_ref, bf16[768,768]{1,0:T(8,128)(2,1)} %copy-done.21, f32[768,768]{1,0:T(8,128)} %get-tuple-element.198.middle_ref, f32[6,768]{1,0:T(8,128)} %rep_ref.7), custom_call_target="tpu_custom_call" | custom-call | flops 6554999808 | bytes 1000000 | tf_op jit(solution)/shard_map/input_gradient/pallas_call | solution.py:1087
  221.2 1.2 collective-permute-done.30.refs_4_
  222.8 1.3 add_convert_fusion.5
  224.1 1.5 collective-permute-start.35
  225.6 2.3 last_messages.1
  227.9 2.5 collective-permute-start.32
  230.4 2.0 collective-permute-start.34
  232.3 2.6 %adam_unit.3 = (f32[576,128]{1,0:T(8,128)}, f32[576,128]{1,0:T(8,128)}, f32[576,128]{1,0:T(8,128)}) custom-call(bf16[384,1536]{1,0:T(8,128)(2,1)} %get-tuple-element.166.refs_0_, bf16[384,1536]{1,0:T(8,128)(2,1)} %collective-permute-done.20.refs_1_, bf16[192,1536]{1,0:T(8,128)(2,1)} %collective-permute-done.23.refs_2_, bf16[96,1536]{1,0:T(8,128)(2,1)} %copy-done.9, ...), custom_call_target="tpu_custom_call" | custom-call | flops 2875000064 | bytes 1000000 | tf_op jit(solution)/shard_map/adam_unit/pallas_call | solution.py:1120
  235.0 2.8 %collective-permute-done.32.refs_3_ = bf16[64,1536]{1,0:T(8,128)(2,1)S(1)} collective-permute-done((bf16[64,1536]{1,0:T(8,128)(2,1)}, bf16[64,1536]{1,0:T(8,128)(2,1)S(1)}, u32[]{:S(2)}, u32[]{:S(2)}) %collective-permute-start.32) | collective-permute-done | bytes 196640 | tf_op jit(solution)/shard_map/ppermute | solution.py:116
  237.8 2.6 %collective-permute-done.33.refs_4_ = bf16[64,1536]{1,0:T(8,128)(2,1)S(1)} collective-permute-done((bf16[64,1536]{1,0:T(8,128)(2,1)}, bf16[64,1536]{1,0:T(8,128)(2,1)S(1)}, u32[]{:S(2)}, u32[]{:S(2)}) %collective-permute-start.33) | collective-permute-done | bytes 196640 | tf_op jit(solution)/shard_map/ppermute | solution.py:116
  240.4 6.9 %collective-permute-done.34.refs_5_ = bf16[64,1536]{1,0:T(8,128)(2,1)S(1)} collective-permute-done((bf16[64,1536]{1,0:T(8,128)(2,1)}, bf16[64,1536]{1,0:T(8,128)(2,1)S(1)}, u32[]{:S(2)}, u32[]{:S(2)}) %collective-permute-start.34) | collective-permute-done | bytes 196640 | tf_op jit(solution)/shard_map/ppermute | solution.py:116
  247.3 0.8 add_add_fusion
  249.1 2.6 %adam_unit.5 = (f32[576,128]{1,0:T(8,128)}, f32[576,128]{1,0:T(8,128)}, f32[576,128]{1,0:T(8,128)}) custom-call(bf16[384,1536]{1,0:T(8,128)(2,1)} %get-tuple-element.188.refs_0_, bf16[384,1536]{1,0:T(8,128)(2,1)} %collective-permute-done.24.refs_1_, bf16[192,1536]{1,0:T(8,128)(2,1)} %copy-done.6, bf16[96,1536]{1,0:T(8,128)(2,1)} %copy-done.8, ...), custom_call_target="tpu_custom_call" | custom-call | flops 2875000064 | bytes 1000000 | tf_op jit(solution)/shard_map/adam_unit/pallas_call | solution.py:1120
  251.7 2.7 %adam_unit.4 = (f32[432,128]{1,0:T(8,128)}, f32[432,128]{1,0:T(8,128)}, f32[432,128]{1,0:T(8,128)}, f32[144,128]{1,0:T(8,128)}, f32[144,128]{1,0:T(8,128)}, /*index=5*/f32[144,128]{1,0:T(8,128)}) custom-call(bf16[400,1536]{1,0:T(8,128)(2,1)} %get-tuple-element.193.kept_ref.refs_0_, bf16[400,1536]{1,0:T(8,128)(2,1)} %copy-done.5, ...), custom_call_target="tpu_custom_call" | custom-call | flops 2875000064 | bytes 1000000 | tf_op jit(solution)/shard_map/adam_unit/pallas_call | solution.py:1120
  (155 shorter events, 15.3 us)
Async XLA Ops:
  0.7 20.0 %copy-start = (bf16[32,34,1,384]{3,0,2,1:T(8,128)(2,1)S(1)}, bf16[32,34,1,384]{3,0,2,1:T(8,128)(2,1)}, u32[]{:S(2)}) copy-start(bf16[32,34,1,384]{3,0,2,1:T(8,128)(2,1)} %param.25) | copy-start | bytes 2506756
  0.7 7.8 %copy-start.7 = (s32[32,529]{1,0:T(8,128)S(1)}, s32[32,529]{1,0:T(8,128)}, u32[]{:S(2)}) copy-start(s32[32,529]{1,0:T(8,128)} %param.28) | copy-start | bytes 203140
  0.7 7.8 %copy-start.19 = (s32[32]{0:T(128)S(1)}, s32[32]{0:T(128)}, u32[]{:S(2)}) copy-start(s32[32]{0:T(128)} %param.27) | copy-start | bytes 388
  0.7 8.1 %copy-start.20 = (s32[32]{0:T(128)S(1)}, s32[32]{0:T(128)}, u32[]{:S(2)}) copy-start(s32[32]{0:T(128)} %param.29) | copy-start | bytes 388
  2.8 14.9 %collective-permute-start = (bf16[1,48,1536]{2,1,0:T(8,128)(2,1)}, bf16[1,48,1536]{2,1,0:T(8,128)(2,1)}, u32[]{:S(2)}, u32[]{:S(2)}) collective-permute-start(bf16[1,48,1536]{2,1,0:T(8,128)(2,1)} %get-tuple-element.124.refs_0_), channel_id=1, source_target_pairs={{0,24},{2,26},{4,28},{6,30},{8,16},{10,18},{12,20},{14,22},{16,8},... | collective-permute-start | bytes 442376 | tf_op jit(solution)/shard_map/ppermute | solution.py:116
  7.9 9.8 %collective-permute-start.1 = (bf16[1,48,1536]{2,1,0:T(8,128)(2,1)}, bf16[1,48,1536]{2,1,0:T(8,128)(2,1)}, u32[]{:S(2)}, u32[]{:S(2)}) collective-permute-start(bf16[1,48,1536]{2,1,0:T(8,128)(2,1)} %get-tuple-element.124.refs_0_), channel_id=1, source_target_pairs={{0,8},{2,10},{4,12},{6,14},{8,0},{10,2},{12,4},{14,6},{16,24},{18,... | collective-permute-start | bytes 442376 | tf_op jit(solution)/shard_map/ppermute | solution.py:116
  7.9 12.8 %collective-permute-start.2 = (bf16[1,48,1536]{2,1,0:T(8,128)(2,1)}, bf16[1,48,1536]{2,1,0:T(8,128)(2,1)}, u32[]{:S(2)}, u32[]{:S(2)}) collective-permute-start(bf16[1,48,1536]{2,1,0:T(8,128)(2,1)} %get-tuple-element.124.refs_0_), channel_id=1, source_target_pairs={{0,16},{2,18},{4,20},{6,22},{8,24},{10,26},{12,28},{14,30},{16,0},... | collective-permute-start | bytes 442376 | tf_op jit(solution)/shard_map/ppermute | solution.py:116
  20.7 5.0 %copy-start.24 = (bf16[1,48,1536]{2,1,0:T(8,128)(2,1)S(1)}, bf16[1,48,1536]{2,1,0:T(8,128)(2,1)}, u32[]{:S(2)}) copy-start(bf16[1,48,1536]{2,1,0:T(8,128)(2,1)} %get-tuple-element.130.refs_0_) | copy-start | bytes 442372
  22.7 16.7 %collective-permute-start.3 = (bf16[4,48,1536]{2,1,0:T(8,128)(2,1)}, bf16[4,48,1536]{2,1,0:T(8,128)(2,1)}, u32[]{:S(2)}, u32[]{:S(2)}) collective-permute-start(bf16[4,48,1536]{2,1,0:T(8,128)(2,1)} %join_chunks.3.p0), channel_id=1, source_target_pairs={{0,2},{1,5},{2,0},{3,7},{4,6},{5,1},{6,4},{7,3},{8,10},{9,13},{10,... | collective-permute-start | bytes 1769480 | tf_op jit(solution)/shard_map/ppermute | solution.py:513
  24.2 15.2 %collective-permute-start.4 = (bf16[4,48,1536]{2,1,0:T(8,128)(2,1)}, bf16[4,48,1536]{2,1,0:T(8,128)(2,1)}, u32[]{:S(2)}, u32[]{:S(2)}) collective-permute-start(bf16[4,48,1536]{2,1,0:T(8,128)(2,1)} %join_chunks.3.p0), channel_id=1, source_target_pairs={{0,4},{1,3},{2,6},{3,1},{4,0},{5,7},{6,2},{7,5},{8,12},{9,11},{10,... | collective-permute-start | bytes 1769480 | tf_op jit(solution)/shard_map/ppermute | solution.py:513
  25.7 8.7 %collective-permute-start.5 = (bf16[1,48,1536]{2,1,0:T(8,128)(2,1)S(1)}, bf16[1,48,1536]{2,1,0:T(8,128)(2,1)S(1)}, u32[]{:S(2)}, u32[]{:S(2)}) collective-permute-start(bf16[1,48,1536]{2,1,0:T(8,128)(2,1)S(1)} %copy-done.24), channel_id=1, source_target_pairs={{0,24},{2,26},{4,28},{6,30},{8,16},{10,18},{12,20},{14,22},{16,8},... | collective-permute-start | bytes 442376 | tf_op jit(solution)/shard_map/ppermute | solution.py:116
  28.2 6.8 %collective-permute-start.6 = (bf16[1,48,1536]{2,1,0:T(8,128)(2,1)S(1)}, bf16[1,48,1536]{2,1,0:T(8,128)(2,1)S(1)}, u32[]{:S(2)}, u32[]{:S(2)}) collective-permute-start(bf16[1,48,1536]{2,1,0:T(8,128)(2,1)S(1)} %copy-done.24), channel_id=1, source_target_pairs={{0,8},{2,10},{4,12},{6,14},{8,0},{10,2},{12,4},{14,6},{16,24},{18,... | collective-permute-start | bytes 442376 | tf_op jit(solution)/shard_map/ppermute | solution.py:116
  28.2 11.2 %collective-permute-start.7 = (bf16[1,48,1536]{2,1,0:T(8,128)(2,1)S(1)}, bf16[1,48,1536]{2,1,0:T(8,128)(2,1)S(1)}, u32[]{:S(2)}, u32[]{:S(2)}) collective-permute-start(bf16[1,48,1536]{2,1,0:T(8,128)(2,1)S(1)} %copy-done.24), channel_id=1, source_target_pairs={{0,16},{2,18},{4,20},{6,22},{8,24},{10,26},{12,28},{14,30},{16,0},... | collective-permute-start | bytes 442376 | tf_op jit(solution)/shard_map/ppermute | solution.py:116
  30.1 15.5 %copy-start.10 = (f32[1,6,384]{2,0,1:T(1,128)S(1)}, f32[1,6,384]{2,0,1:T(1,128)}, u32[]{:S(2)}) copy-start(f32[1,6,384]{2,0,1:T(1,128)} %param.45) | copy-start | bytes 27652
  34.4 5.0 %copy-start.26 = (bf16[1,48,1536]{2,1,0:T(8,128)(2,1)}, bf16[1,48,1536]{2,1,0:T(8,128)(2,1)S(1)}, u32[]{:S(2)}) copy-start(bf16[1,48,1536]{2,1,0:T(8,128)(2,1)S(1)} %collective-permute-done.5.refs_1_) | copy-start | bytes 442372
  35.0 4.4 %copy-start.27 = (bf16[1,48,1536]{2,1,0:T(8,128)(2,1)}, bf16[1,48,1536]{2,1,0:T(8,128)(2,1)S(1)}, u32[]{:S(2)}) copy-start(bf16[1,48,1536]{2,1,0:T(8,128)(2,1)S(1)} %collective-permute-done.6.refs_2_) | copy-start | bytes 442372
  40.1 21.0 %collective-permute-start.8 = (bf16[4,48,1536]{2,1,0:T(8,128)(2,1)}, bf16[4,48,1536]{2,1,0:T(8,128)(2,1)S(1)}, u32[]{:S(2)}, u32[]{:S(2)}) collective-permute-start(bf16[4,48,1536]{2,1,0:T(8,128)(2,1)} %collective-permute-done.3.p1), channel_id=1, source_target_pairs={{0,4},{1,3},{2,6},{3,1},{4,0},{5,7},{6,2},{7,5},{8,12},{9,11},{10,... | collective-permute-start | bytes 1769480 | tf_op jit(solution)/shard_map/ppermute | solution.py:513
  40.6 11.9 %collective-permute-start.10 = (bf16[1,48,1536]{2,1,0:T(8,128)(2,1)}, bf16[1,48,1536]{2,1,0:T(8,128)(2,1)S(1)}, u32[]{:S(2)}, u32[]{:S(2)}) collective-permute-start(bf16[1,48,1536]{2,1,0:T(8,128)(2,1)} %get-tuple-element.135.refs_0_), channel_id=1, source_target_pairs={{0,8},{2,10},{4,12},{6,14},{8,0},{10,2},{12,4},{14,6},{16,24},{18,... | collective-permute-start | bytes 442376 | tf_op jit(solution)/shard_map/ppermute | solution.py:116
  40.6 20.5 %collective-permute-start.11 = (bf16[1,48,1536]{2,1,0:T(8,128)(2,1)}, bf16[1,48,1536]{2,1,0:T(8,128)(2,1)}, u32[]{:S(2)}, u32[]{:S(2)}) collective-permute-start(bf16[1,48,1536]{2,1,0:T(8,128)(2,1)} %get-tuple-element.135.refs_0_), channel_id=1, source_target_pairs={{0,16},{2,18},{4,20},{6,22},{8,24},{10,26},{12,28},{14,30},{16,0},... | collective-permute-start | bytes 442376 | tf_op jit(solution)/shard_map/ppermute | solution.py:116
  42.4 18.7 %collective-permute-start.9 = (bf16[1,48,1536]{2,1,0:T(8,128)(2,1)}, bf16[1,48,1536]{2,1,0:T(8,128)(2,1)}, u32[]{:S(2)}, u32[]{:S(2)}) collective-permute-start(bf16[1,48,1536]{2,1,0:T(8,128)(2,1)} %get-tuple-element.135.refs_0_), channel_id=1, source_target_pairs={{0,24},{2,26},{4,28},{6,30},{8,16},{10,18},{12,20},{14,22},{16,8},... | collective-permute-start | bytes 442376 | tf_op jit(solution)/shard_map/ppermute | solution.py:116
  46.2 38.0 %all-to-all-start = ((bf16[16,72,384]{2,1,0:T(8,128)(2,1)}), bf16[16,72,384]{2,1,0:T(8,128)(2,1)}, u32[]{:S(2)}, u32[]{:S(2)}) async-start(bf16[16,72,384]{2,1,0:T(8,128)(2,1)} %bitcast.71), calls=%async_computation | async-start | bytes 1769472 | tf_op jit(solution)/shard_map/all_to_all | solution.py:1227
  52.5 8.6 %copy-start.30 = (bf16[1,48,1536]{2,1,0:T(8,128)(2,1)}, bf16[1,48,1536]{2,1,0:T(8,128)(2,1)S(1)}, u32[]{:S(2)}) copy-start(bf16[1,48,1536]{2,1,0:T(8,128)(2,1)S(1)} %collective-permute-done.10.refs_2_) | copy-start | bytes 442372
  63.3 23.6 %collective-permute-start.14 = (bf16[4,48,1536]{2,1,0:T(8,128)(2,1)}, bf16[4,48,1536]{2,1,0:T(8,128)(2,1)}, u32[]{:S(2)}, u32[]{:S(2)}) collective-permute-start(bf16[4,48,1536]{2,1,0:T(8,128)(2,1)} %join_chunks.5.c0), channel_id=1, source_target_pairs={{0,2},{1,5},{2,0},{3,7},{4,6},{5,1},{6,4},{7,3},{8,10},{9,13},{10,... | collective-permute-start | bytes 1769480 | tf_op jit(solution)/shard_map/ppermute | solution.py:513
  63.3 24.2 %collective-permute-start.15 = (bf16[4,48,1536]{2,1,0:T(8,128)(2,1)}, bf16[4,48,1536]{2,1,0:T(8,128)(2,1)}, u32[]{:S(2)}, u32[]{:S(2)}) collective-permute-start(bf16[4,48,1536]{2,1,0:T(8,128)(2,1)} %join_chunks.5.c0), channel_id=1, source_target_pairs={{0,4},{1,3},{2,6},{3,1},{4,0},{5,7},{6,2},{7,5},{8,12},{9,11},{10,... | collective-permute-start | bytes 1769480 | tf_op jit(solution)/shard_map/ppermute | solution.py:513
  63.3 25.9 %collective-permute-start.12 = (bf16[4,48,1536]{2,1,0:T(8,128)(2,1)}, bf16[4,48,1536]{2,1,0:T(8,128)(2,1)}, u32[]{:S(2)}, u32[]{:S(2)}) collective-permute-start(bf16[4,48,1536]{2,1,0:T(8,128)(2,1)} %join_chunks.4.b0), channel_id=1, source_target_pairs={{0,2},{1,5},{2,0},{3,7},{4,6},{5,1},{6,4},{7,3},{8,10},{9,13},{10,... | collective-permute-start | bytes 1769480 | tf_op jit(solution)/shard_map/ppermute | solution.py:513
  65.3 23.9 %collective-permute-start.13 = (bf16[4,48,1536]{2,1,0:T(8,128)(2,1)}, bf16[4,48,1536]{2,1,0:T(8,128)(2,1)}, u32[]{:S(2)}, u32[]{:S(2)}) collective-permute-start(bf16[4,48,1536]{2,1,0:T(8,128)(2,1)} %join_chunks.4.b0), channel_id=1, source_target_pairs={{0,4},{1,3},{2,6},{3,1},{4,0},{5,7},{6,2},{7,5},{8,12},{9,11},{10,... | collective-permute-start | bytes 1769480 | tf_op jit(solution)/shard_map/ppermute | solution.py:513
  84.0 21.7 %collective-permute-start.18 = (bf16[768,768]{1,0:T(8,128)(2,1)}, bf16[768,768]{1,0:T(8,128)(2,1)}, u32[]{:S(2)}, u32[]{:S(2)}) collective-permute-start(bf16[768,768]{1,0:T(8,128)(2,1)} %get-tuple-element.144.own_any), channel_id=1, source_target_pairs={{0,1},{1,0},{2,3},{3,2},{4,5},{5,4},{6,7},{7,6},{8,9},{9,8},{10,11... | collective-permute-start | bytes 3538952 | tf_op jit(solution)/shard_map/ppermute | solution.py:120
  87.0 4.3 %collective-permute-start.19 = (bf16[768,384]{1,0:T(8,128)(2,1)S(1)}, bf16[768,384]{1,0:T(8,128)(2,1)}, u32[]{:S(2)}, u32[]{:S(2)}) collective-permute-start(bf16[768,384]{1,0:T(8,128)(2,1)S(1)} %convolution_convert_fusion.2), channel_id=1, source_target_pairs={{0,1},{1,0},{2,3},{3,2},{4,5},{5,4},{6,7},{7,6},{8,9},{9,8},{10,11... | collective-permute-start | bytes 1769480 | tf_op jit(solution)/shard_map/ppermute | solution.py:120
  89.2 10.2 %collective-permute-start.16 = (bf16[4,48,1536]{2,1,0:T(8,128)(2,1)}, bf16[4,48,1536]{2,1,0:T(8,128)(2,1)}, u32[]{:S(2)}, u32[]{:S(2)}) collective-permute-start(bf16[4,48,1536]{2,1,0:T(8,128)(2,1)} %collective-permute-done.12.b1), channel_id=1, source_target_pairs={{0,4},{1,3},{2,6},{3,1},{4,0},{5,7},{6,2},{7,5},{8,12},{9,11},{10,... | collective-permute-start | bytes 1769480 | tf_op jit(solution)/shard_map/ppermute | solution.py:513
  89.8 16.0 %collective-permute-start.17 = (bf16[4,48,1536]{2,1,0:T(8,128)(2,1)}, bf16[4,48,1536]{2,1,0:T(8,128)(2,1)}, u32[]{:S(2)}, u32[]{:S(2)}) collective-permute-start(bf16[4,48,1536]{2,1,0:T(8,128)(2,1)} %collective-permute-done.14.c1), channel_id=1, source_target_pairs={{0,4},{1,3},{2,6},{3,1},{4,0},{5,7},{6,2},{7,5},{8,12},{9,11},{10,... | collective-permute-start | bytes 1769480 | tf_op jit(solution)/shard_map/ppermute | solution.py:513
  137.3 3.3 %collective-permute-start.22 = (bf16[768,768]{1,0:T(8,128)(2,1)}, bf16[768,768]{1,0:T(8,128)(2,1)}, u32[]{:S(2)}, u32[]{:S(2)}) collective-permute-start(bf16[768,768]{1,0:T(8,128)(2,1)} %get-tuple-element.170), channel_id=1, source_target_pairs={{0,1},{1,0},{2,3},{3,2},{4,5},{5,4},{6,7},{7,6},{8,9},{9,8},{10,11... | collective-permute-start | bytes 3538952 | tf_op jit(solution)/shard_map/ppermute | solution.py:120
  137.4 16.6 %collective-permute-start.20 = (bf16[384,1536]{1,0:T(8,128)(2,1)}, bf16[384,1536]{1,0:T(8,128)(2,1)}, u32[]{:S(2)}, u32[]{:S(2)}) collective-permute-start(bf16[384,1536]{1,0:T(8,128)(2,1)} %get-tuple-element.167), channel_id=1, source_target_pairs={{0,4},{1,3},{2,6},{3,1},{4,0},{5,7},{6,2},{7,5},{8,12},{9,11},{10,... | collective-permute-start | bytes 3538952 | tf_op jit(solution)/shard_map/ppermute | solution.py:513
  137.9 16.0 %collective-permute-start.21 = (bf16[768,768]{1,0:T(8,128)(2,1)}, bf16[768,768]{1,0:T(8,128)(2,1)}, u32[]{:S(2)}, u32[]{:S(2)}) collective-permute-start(bf16[768,768]{1,0:T(8,128)(2,1)} %get-tuple-element.168.own_any), channel_id=1, source_target_pairs={{0,1},{1,0},{2,3},{3,2},{4,5},{5,4},{6,7},{7,6},{8,9},{9,8},{10,11... | collective-permute-start | bytes 3538952 | tf_op jit(solution)/shard_map/ppermute | solution.py:120
  139.9 14.0 %copy-start.2 = (bf16[384,1536]{1,0:T(8,128)(2,1)S(1)}, bf16[384,1536]{1,0:T(8,128)(2,1)}, u32[]{:S(2)}) copy-start(bf16[384,1536]{1,0:T(8,128)(2,1)} %get-tuple-element.166.refs_0_) | copy-start | bytes 3538948
  139.9 43.5 %collective-permute-start.24 = (bf16[384,1536]{1,0:T(8,128)(2,1)}, bf16[384,1536]{1,0:T(8,128)(2,1)}, u32[]{:S(2)}, u32[]{:S(2)}) collective-permute-start(bf16[384,1536]{1,0:T(8,128)(2,1)} %get-tuple-element.172), channel_id=1, source_target_pairs={{0,4},{1,3},{2,6},{3,1},{4,0},{5,7},{6,2},{7,5},{8,12},{9,11},{10,... | collective-permute-start | bytes 3538952 | tf_op jit(solution)/shard_map/ppermute | solution.py:513
  155.2 28.3 %collective-permute-start.23 = (bf16[192,1536]{1,0:T(8,128)(2,1)S(1)}, bf16[192,1536]{1,0:T(8,128)(2,1)}, u32[]{:S(2)}, u32[]{:S(2)}) collective-permute-start(bf16[192,1536]{1,0:T(8,128)(2,1)S(1)} %add_convert_fusion.2), channel_id=1, source_target_pairs={{0,2},{1,5},{2,0},{3,7},{4,6},{5,1},{6,4},{7,3},{8,10},{9,13},{10,... | collective-permute-start | bytes 1769480 | tf_op jit(solution)/shard_map/ppermute | solution.py:513
  156.7 27.7 %all-to-all-start.1 = ((bf16[16,72,384]{2,1,0:T(8,128)(2,1)}), bf16[16,72,384]{2,1,0:T(8,128)(2,1)}, u32[]{:S(2)}, u32[]{:S(2)}) async-start(bf16[16,72,384]{2,1,0:T(8,128)(2,1)} %bitcast.72), calls=%async_computation.1 | async-start | bytes 1769472 | tf_op jit(solution)/shard_map/all_to_all | solution.py:1227
  184.5 7.0 %copy-start.31 = (bf16[384]{0:T(512)(128)(2,1)S(1)}, bf16[384]{0:T(512)(128)(2,1)}, u32[]{:S(2)}) copy-start(bf16[384]{0:T(512)(128)(2,1)} %param.26) | copy-start | bytes 2308
  184.5 23.3 %collective-permute-start.25 = (bf16[400,1536]{1,0:T(8,128)(2,1)}, bf16[400,1536]{1,0:T(8,128)(2,1)S(1)}, u32[]{:S(2)}, u32[]{:S(2)}) collective-permute-start(bf16[400,1536]{1,0:T(8,128)(2,1)} %get-tuple-element.186), channel_id=1, source_target_pairs={{0,4},{1,3},{2,6},{3,1},{4,0},{5,7},{6,2},{7,5},{8,12},{9,11},{10,... | collective-permute-start | bytes 3686408 | tf_op jit(solution)/shard_map/ppermute | solution.py:513
  186.2 17.7 %collective-permute-start.28 = (bf16[768,768]{1,0:T(8,128)(2,1)}, bf16[768,768]{1,0:T(8,128)(2,1)S(1)}, u32[]{:S(2)}, u32[]{:S(2)}) collective-permute-start(bf16[768,768]{1,0:T(8,128)(2,1)} %get-tuple-element.190.own_ref), channel_id=1, source_target_pairs={{0,1},{1,0},{2,3},{3,2},{4,5},{5,4},{6,7},{7,6},{8,9},{9,8},{10,11... | collective-permute-start | bytes 3538952 | tf_op jit(solution)/shard_map/ppermute | solution.py:120
  187.6 16.3 %collective-permute-start.27 = (bf16[192,1536]{1,0:T(8,128)(2,1)S(1)}, bf16[192,1536]{1,0:T(8,128)(2,1)S(1)}, u32[]{:S(2)}, u32[]{:S(2)}) collective-permute-start(bf16[192,1536]{1,0:T(8,128)(2,1)S(1)} %add_convert_fusion.1), channel_id=1, source_target_pairs={{0,2},{1,5},{2,0},{3,7},{4,6},{5,1},{6,4},{7,3},{8,10},{9,13},{10,... | collective-permute-start | bytes 1769480 | tf_op jit(solution)/shard_map/ppermute | solution.py:513
  189.5 9.9 %collective-permute-start.26 = (bf16[96,1536]{1,0:T(8,128)(2,1)S(1)}, bf16[96,1536]{1,0:T(8,128)(2,1)S(1)}, u32[]{:S(2)}, u32[]{:S(2)}) collective-permute-start(bf16[96,1536]{1,0:T(8,128)(2,1)S(1)} %add_convert_fusion.4), channel_id=1, source_target_pairs={{0,8},{2,10},{4,12},{6,14},{8,0},{10,2},{12,4},{14,6},{16,24},{18,... | collective-permute-start | bytes 884744 | tf_op jit(solution)/shard_map/ppermute | solution.py:116
  191.4 20.7 %copy-start.4 = (bf16[400,1536]{1,0:T(8,128)(2,1)S(1)}, bf16[400,1536]{1,0:T(8,128)(2,1)}, u32[]{:S(2)}) copy-start(bf16[400,1536]{1,0:T(8,128)(2,1)} %get-tuple-element.193.kept_ref.refs_0_) | copy-start | bytes 3686404
  199.5 13.2 %copy-start.9 = (bf16[96,1536]{1,0:T(8,128)(2,1)}, bf16[96,1536]{1,0:T(8,128)(2,1)S(1)}, u32[]{:S(2)}) copy-start(bf16[96,1536]{1,0:T(8,128)(2,1)S(1)} %collective-permute-done.26.refs_3_) | copy-start | bytes 884740
  204.0 18.9 %copy-start.6 = (bf16[192,1536]{1,0:T(8,128)(2,1)}, bf16[192,1536]{1,0:T(8,128)(2,1)S(1)}, u32[]{:S(2)}) copy-start(bf16[192,1536]{1,0:T(8,128)(2,1)S(1)} %collective-permute-done.27.refs_2_) | copy-start | bytes 1769476
  204.0 12.4 %copy-start.21 = (bf16[768,768]{1,0:T(8,128)(2,1)}, bf16[768,768]{1,0:T(8,128)(2,1)S(1)}, u32[]{:S(2)}) copy-start(bf16[768,768]{1,0:T(8,128)(2,1)S(1)} %collective-permute-done.28.other_ref) | copy-start | bytes 3538948
  207.7 4.6 %copy-start.5 = (bf16[400,1536]{1,0:T(8,128)(2,1)}, bf16[400,1536]{1,0:T(8,128)(2,1)S(1)}, u32[]{:S(2)}) copy-start(bf16[400,1536]{1,0:T(8,128)(2,1)S(1)} %collective-permute-done.25.one_ref.refs_1_) | copy-start | bytes 3686404
  209.3 13.0 %collective-permute-start.31 = (bf16[96,1536]{1,0:T(8,128)(2,1)S(1)}, bf16[96,1536]{1,0:T(8,128)(2,1)S(1)}, u32[]{:S(2)}, u32[]{:S(2)}) collective-permute-start(bf16[96,1536]{1,0:T(8,128)(2,1)S(1)} %add_convert_fusion.3), channel_id=1, source_target_pairs={{0,8},{2,10},{4,12},{6,14},{8,0},{10,2},{12,4},{14,6},{16,24},{18,... | collective-permute-start | bytes 884744 | tf_op jit(solution)/shard_map/ppermute | solution.py:116
  212.3 8.8 %copy-start.3 = (bf16[208,1536]{1,0:T(8,128)(2,1)}, bf16[208,1536]{1,0:T(8,128)(2,1)S(1)}, u32[]{:S(2)}) copy-start(bf16[208,1536]{1,0:T(8,128)(2,1)S(1)} %add_convert_fusion.carried_ref) | copy-start | bytes 1916932
  212.3 10.5 %collective-permute-start.29 = (bf16[208,1536]{1,0:T(8,128)(2,1)S(1)}, bf16[208,1536]{1,0:T(8,128)(2,1)S(1)}, u32[]{:S(2)}, u32[]{:S(2)}) collective-permute-start(bf16[208,1536]{1,0:T(8,128)(2,1)S(1)} %add_convert_fusion.carried_ref), channel_id=1, source_target_pairs={{0,2},{1,5},{2,0},{3,7},{4,6},{5,1},{6,4},{7,3},{8,10},{9,13},{10,... | collective-permute-start | bytes 1916936 | tf_op jit(solution)/shard_map/ppermute | solution.py:513
  213.8 8.5 %collective-permute-start.30 = (bf16[48,1536]{1,0:T(8,128)(2,1)S(1)}, bf16[48,1536]{1,0:T(8,128)(2,1)S(1)}, u32[]{:S(2)}, u32[]{:S(2)}) collective-permute-start(bf16[48,1536]{1,0:T(8,128)(2,1)S(1)} %add_convert_fusion.6), channel_id=1, source_target_pairs={{0,24},{2,26},{4,28},{6,30},{8,16},{10,18},{12,20},{14,22},{16,8},... | collective-permute-start | bytes 442376 | tf_op jit(solution)/shard_map/ppermute | solution.py:116
  222.3 5.6 %copy-start.29 = (bf16[48,1536]{1,0:T(8,128)(2,1)}, bf16[48,1536]{1,0:T(8,128)(2,1)S(1)}, u32[]{:S(2)}) copy-start(bf16[48,1536]{1,0:T(8,128)(2,1)S(1)} %collective-permute-done.30.refs_4_) | copy-start | bytes 442372
  222.3 5.6 %copy-start.8 = (bf16[96,1536]{1,0:T(8,128)(2,1)}, bf16[96,1536]{1,0:T(8,128)(2,1)S(1)}, u32[]{:S(2)}) copy-start(bf16[96,1536]{1,0:T(8,128)(2,1)S(1)} %collective-permute-done.31.refs_3_) | copy-start | bytes 884740
  224.1 10.9 %collective-permute-start.35 = (bf16[48,1536]{1,0:T(8,128)(2,1)S(1)}, bf16[48,1536]{1,0:T(8,128)(2,1)S(1)}, u32[]{:S(2)}, u32[]{:S(2)}) collective-permute-start(bf16[48,1536]{1,0:T(8,128)(2,1)S(1)} %add_convert_fusion.5), channel_id=1, source_target_pairs={{0,24},{2,26},{4,28},{6,30},{8,16},{10,18},{12,20},{14,22},{16,8},... | collective-permute-start | bytes 442376 | tf_op jit(solution)/shard_map/ppermute | solution.py:116
  227.9 9.9 %collective-permute-start.32 = (bf16[64,1536]{1,0:T(8,128)(2,1)}, bf16[64,1536]{1,0:T(8,128)(2,1)S(1)}, u32[]{:S(2)}, u32[]{:S(2)}) collective-permute-start(bf16[64,1536]{1,0:T(8,128)(2,1)} %get-tuple-element.210), channel_id=1, source_target_pairs={{0,24},{2,26},{4,28},{6,30},{8,16},{10,18},{12,20},{14,22},{16,8},... | collective-permute-start | bytes 589832 | tf_op jit(solution)/shard_map/ppermute | solution.py:116
  230.4 10.0 %collective-permute-start.33 = (bf16[64,1536]{1,0:T(8,128)(2,1)}, bf16[64,1536]{1,0:T(8,128)(2,1)S(1)}, u32[]{:S(2)}, u32[]{:S(2)}) collective-permute-start(bf16[64,1536]{1,0:T(8,128)(2,1)} %get-tuple-element.203), channel_id=1, source_target_pairs={{0,8},{2,10},{4,12},{6,14},{8,0},{10,2},{12,4},{14,6},{16,24},{18,... | collective-permute-start | bytes 589832 | tf_op jit(solution)/shard_map/ppermute | solution.py:116
  230.4 17.0 %collective-permute-start.34 = (bf16[64,1536]{1,0:T(8,128)(2,1)}, bf16[64,1536]{1,0:T(8,128)(2,1)S(1)}, u32[]{:S(2)}, u32[]{:S(2)}) collective-permute-start(bf16[64,1536]{1,0:T(8,128)(2,1)} %get-tuple-element.204), channel_id=1, source_target_pairs={{0,16},{2,18},{4,20},{6,22},{8,24},{10,26},{12,28},{14,30},{16,0},... | collective-permute-start | bytes 589832 | tf_op jit(solution)/shard_map/ppermute | solution.py:116
  232.3 16.0 %copy-start.17 = (f32[1,6,384]{2,0,1:T(1,128)S(1)}, f32[1,6,384]{2,0,1:T(1,128)}, u32[]{:S(2)}) copy-start(f32[1,6,384]{2,0,1:T(1,128)} %param.46) | copy-start | bytes 27652
  232.3 16.0 %copy-start.18 = (f32[1,6,384]{2,0,1:T(1,128)S(1)}, f32[1,6,384]{2,0,1:T(1,128)}, u32[]{:S(2)}) copy-start(f32[1,6,384]{2,0,1:T(1,128)} %param.47) | copy-start | bytes 27652
  235.0 14.1 %copy-start.25 = (bf16[48,1536]{1,0:T(8,128)(2,1)}, bf16[48,1536]{1,0:T(8,128)(2,1)S(1)}, u32[]{:S(2)}) copy-start(bf16[48,1536]{1,0:T(8,128)(2,1)S(1)} %collective-permute-done.35.refs_4_) | copy-start | bytes 442372
  237.8 13.9 %copy-start.14 = (bf16[64,1536]{1,0:T(8,128)(2,1)}, bf16[64,1536]{1,0:T(8,128)(2,1)S(1)}, u32[]{:S(2)}) copy-start(bf16[64,1536]{1,0:T(8,128)(2,1)S(1)} %collective-permute-done.32.refs_3_) | copy-start | bytes 589828
  240.4 11.3 %copy-start.15 = (bf16[64,1536]{1,0:T(8,128)(2,1)}, bf16[64,1536]{1,0:T(8,128)(2,1)S(1)}, u32[]{:S(2)}) copy-start(bf16[64,1536]{1,0:T(8,128)(2,1)S(1)} %collective-permute-done.33.refs_4_) | copy-start | bytes 589828
  247.3 4.4 %copy-start.16 = (bf16[64,1536]{1,0:T(8,128)(2,1)}, bf16[64,1536]{1,0:T(8,128)(2,1)S(1)}, u32[]{:S(2)}) copy-start(bf16[64,1536]{1,0:T(8,128)(2,1)S(1)} %collective-permute-done.34.refs_5_) | copy-start | bytes 589828
  248.3 6.8 %collective-permute-start.36 = (f32[3,1536]{1,0:T(4,128)S(1)}, f32[3,1536]{1,0:T(4,128)S(1)}, u32[]{:S(2)}, u32[]{:S(2)}) collective-permute-start(f32[3,1536]{1,0:T(4,128)S(1)} %slice.136), channel_id=1, source_target_pairs={{0,1},{1,0},{2,3},{3,2},{4,5},{5,4},{6,7},{7,6},{8,9},{9,8},{10,11... | collective-permute-start | bytes 55304 | tf_op jit(solution)/shard_map/ppermute | solution.py:120
  (7 other events, 19.9 us)
where the time goes:
time: 259 us; the launch traced here: 256 us
  Pallas kernels  94.7 us (37%)
  waiting for transfers between devices  68 us (26%)
  starting transfers between devices  55 us (21%)
  other arithmetic  17.2 us (7%)
  matrix products  14.2 us (5%)
  local copies, waits for them, and re-layouts  5.52 us (2%)
    ppermute x16, waiting for transfers between devices, hop(): lax.ppermute(array, 'dp', [(i, i ^ distance) for i in range(axis_count)])  35.3 us
    pallas_call x1, Pallas kernels, mlp_all(): pl.pallas_call(body, in_specs=[IN_SMEM, IN_VMEM, IN_VMEM] + [ANY] * 12, o...  31.5 us
    ppermute x15, waiting for transfers between devices, hop_by_core(): return lax.ppermute(array, ('dp', 'mp'), pairs)  31.5 us
    ppermute x16, starting transfers between devices, hop(): lax.ppermute(array, 'dp', [(i, i ^ distance) for i in range(axis_count)])  27.7 us
    pallas_call x1, Pallas kernels, attention_back(): pl.pallas_call(body, in_specs=[IN_SMEM] + [IN_VMEM] * 4 + [ANY] * 11, out...  20.4 us
    pallas_call x1, Pallas kernels, attention_forward(): pl.pallas_call(body, grid=(pairs_of_heads,), in_specs=[IN_SMEM, fixed(cou...  16.7 us
    ppermute x15, starting transfers between devices, hop_by_core(): return lax.ppermute(array, ('dp', 'mp'), pairs)  14.8 us
    all_to_all x2, starting transfers between devices, exchanged(): array = lax.all_to_all(array, 'dp', split_axis=0, concat_axis=0, tiled=True)  10.6 us
  transfers between devices with their start and end apart: 39, of which 19 were waited for; matrix products, arithmetic and copies ran while one was open for 12% of the time, Pallas kernels for 23%

commit v1 on v0

--- a/solution.py
+++ b/solution.py
@@ -479,6 +479,7 @@
 BLOCK = 384
 UNIT_ROWS = 48
 UNIT_WIDTH = 1536
+BLOCK_WIDTH = 256
 Z_ORDER = (0, 12, 4, 8)
 VMEM_BYTES = 60 * 1024 * 1024
 ANY = pl.BlockSpec(memory_space=pl.ANY)
@@ -514,25 +515,30 @@
 
 
 def pack_units(qkv, out, fc1, fc2):
-    def body(qkv_ref, out_ref, fc1_ref, fc2_ref, unit_a, unit_b, unit_c):
+    def body(qkv_ref, out_ref, fc1_ref, fc2_ref, units, unit_a, units_later):
         def put(unit, column, rows):
-            unit[0, :, column * 128 : (column + 1) * 128] = rows.astype(jnp.bfloat16)
+            units[unit, :, column * 128 : (column + 1) * 128] = rows.astype(jnp.bfloat16)
 
         for j in range(9):
-            put(unit_a, j, qkv_ref[pl.ds(j, UNIT_ROWS, stride=9), :])
+            put(0, j, qkv_ref[pl.ds(j, UNIT_ROWS, stride=9), :])
         for j in range(3):
-            put(unit_a, 9 + j, out_ref[pl.ds(j, UNIT_ROWS, stride=3), :])
+            put(0, 9 + j, out_ref[pl.ds(j, UNIT_ROWS, stride=3), :])
         for j in range(12):
-            put(unit_b, j, fc1_ref[pl.ds(j, UNIT_ROWS, stride=12), :])
+            put(1, j, fc1_ref[pl.ds(j, UNIT_ROWS, stride=12), :])
         for half in range(2):
             for j in range(6):
                 start = half * UNIT_ROWS * 6 + j
-                put(unit_c, half * 6 + j, fc2_ref[pl.ds(start, UNIT_ROWS, stride=6), :])
-
-    unit = shaped((1, UNIT_ROWS, UNIT_WIDTH), jnp.bfloat16)
+                put(2, half * 6 + j, fc2_ref[pl.ds(start, UNIT_ROWS, stride=6), :])
+        unit_a[0] = units[0]
+        units_later[0] = units[1]
+        units_later[1] = units[2]
+
+    def unit_array(count):
+        return shaped((count, UNIT_ROWS, UNIT_WIDTH), jnp.bfloat16)
+
     return pl.pallas_call(
         body,
-        out_shape=[unit, unit, unit],
+        out_shape=[unit_array(3), unit_array(1), unit_array(2)],
         compiler_params=params(),
         cost_estimate=cost(2),
         name="pack_units",
@@ -541,53 +547,68 @@
     )
 
 
-def owner_of(words, piece, entry):
-    extra = (0, words[1], words[2], 3)[piece]
-    return words[0] ^ Z_ORDER[entry] ^ extra
+def chunk_sources(words, own, pieces, unit):
+    step, offset = (1, 0) if unit == 0 else (2, unit - 1)
+    found = []
+    for place, extra in enumerate((0, words[1], words[2], 3)):
+        found.append((own[place].at[unit], words[0] ^ extra))
+        for entry, distance in enumerate(Z_ORDER[1:]):
+            source = pieces[place].at[entry * step + offset]
+            found.append((source, words[0] ^ distance ^ extra))
+    return found
 
 
 def join_chunks(chunks):
+    size = chunks[0].shape[0]
+
     def body(*refs):
         for entry, ref in enumerate(refs[:-1]):
-            refs[-1][entry] = ref[0]
+            refs[-1][entry * size : (entry + 1) * size] = ref[...]
 
     return pl.pallas_call(
         body,
-        out_shape=shaped((len(chunks),) + chunks[0].shape[1:], chunks[0].dtype),
+        out_shape=shaped((len(chunks) * size,) + chunks[0].shape[1:], chunks[0].dtype),
         compiler_params=params(),
-        cost_estimate=cost(1.3),
+        cost_estimate=cost(1.5 * size),
         name="join_chunks",
     )(*chunks)
 
 
-def last_messages(kept, one, two, carried):
-    def body(kept_ref, one_ref, two_ref, carried_ref, *targets):
-        vectors = carried_ref[...].astype(jnp.float32)
-        vectors = (vectors + two_ref[4 * UNIT_ROWS :, :].astype(jnp.float32)).astype(jnp.bfloat16)
+def last_messages(kept, one, two, carried=None):
+    extra = 0 if carried is None else 16
+    inputs = [kept, one, two] + ([] if carried is None else [carried])
+
+    def body(kept_ref, one_ref, two_ref, *refs):
+        targets = refs[-3:]
+        if extra:
+            vectors = refs[0][...].astype(jnp.float32)
+            vectors = vectors + two_ref[4 * UNIT_ROWS :, :].astype(jnp.float32)
+            vectors = vectors.astype(jnp.bfloat16)
         for entry, target in enumerate(targets):
             rows = slice((entry + 1) * UNIT_ROWS, (entry + 2) * UNIT_ROWS)
             total = kept_ref[rows, :].astype(jnp.float32) + one_ref[rows, :].astype(jnp.float32)
             total = total + two_ref[rows, :].astype(jnp.float32)
             target[:UNIT_ROWS, :] = total.astype(jnp.bfloat16)
-            target[UNIT_ROWS:, :] = vectors
+            if extra:
+                target[UNIT_ROWS:, :] = vectors
 
     def rows(count, start=0):
         return pl.BlockSpec((count, UNIT_WIDTH), lambda i: (start, 0))
 
-    message = shaped((UNIT_ROWS + 16, UNIT_WIDTH), jnp.bfloat16)
+    specs = [rows(4 * UNIT_ROWS), rows(4 * UNIT_ROWS), rows(4 * UNIT_ROWS + extra)]
+    if extra:
+        specs.append(rows(16, 4 * UNIT_ROWS // 16))
+    message = shaped((UNIT_ROWS + extra, UNIT_WIDTH), jnp.bfloat16)
     return pl.pallas_call(
         body,
         grid=(1,),
-        in_specs=[
-            rows(4 * UNIT_ROWS), rows(4 * UNIT_ROWS), rows(4 * UNIT_ROWS + 16),
-            rows(16, 4 * UNIT_ROWS // 16),
-        ],
-        out_specs=[rows(UNIT_ROWS + 16)] * 3,
+        in_specs=specs,
+        out_specs=[rows(UNIT_ROWS + extra)] * 3,
         out_shape=[message] * 3,
         compiler_params=params(1),
         cost_estimate=cost(1.5),
         name="last_messages",
-    )(kept, one, two, carried)
+    )(*inputs)
 
 
 def added(start, stop, *arrays):
@@ -615,6 +636,10 @@
     return places
 
 
+def lanes_of(part, size):
+    return pl.ds(pl.multiple_of(part * size, 128), size)
+
+
 def unit_rows(owner, rows=UNIT_ROWS):
     return pl.ds(pl.multiple_of(owner * rows, 16), rows)
 
@@ -631,29 +656,6 @@
     mean_one = jnp.mean(scaled, axis=1, keepdims=True)
     mean_two = jnp.mean(scaled * unit_signal, axis=1, keepdims=True)
     return scale * (scaled - mean_one - unit_signal * mean_two)
-
-
-def first_norm(rows, rep):
-    count, width = rows.shape
-
-    def body(rows_ref, rep_ref, normed_ref):
-        unit_signal, _ = norm_parts(rows_ref[...].astype(jnp.float32))
-        normed = unit_signal * rep_ref[0:1, :] + rep_ref[1:2, :]
-        normed_ref[...] = normed.astype(jnp.bfloat16)
-
-    return pl.pallas_call(
-        body,
-        grid=(count // BLOCK,),
-        in_specs=[
-            pl.BlockSpec((BLOCK, width), lambda i: (i, 0)),
-            pl.BlockSpec(rep.shape, lambda i: (0, 0)),
-        ],
-        out_specs=pl.BlockSpec((BLOCK, width), lambda i: (i, 0)),
-        out_shape=shaped((count, width), jnp.bfloat16),
-        compiler_params=params(1),
-        cost_estimate=cost(3.5),
-        name="first_norm",
-    )(rows, rep)
 
 
 def fixed(*shape):
@@ -690,38 +692,48 @@
         copy.wait()
 
 
-def chunk_pairs(words_ref, pieces, target):
-    pairs = []
-    for piece, source in enumerate(pieces):
-        for entry in range(4):
-            owner = owner_of(words_ref, piece, entry)
-            pairs.append((source.at[entry], target.at[unit_rows(owner), :]))
-    return pairs
-
-
-def attention_forward(words, normed, split, column_bias, pieces):
-    count, width = normed.shape
+def chunk_pairs(words, own, pieces, unit, target):
+    return [
+        (source, target.at[unit_rows(owner), :])
+        for source, owner in chunk_sources(words, own, pieces, unit)
+    ]
+
+
+def attention_forward(words, rows_in, rep, split, column_bias, own_pieces, pieces):
+    count, width = rows_in.shape
     half = split.shape[1]
     pairs_of_heads = half // (2 * HEAD)
 
     def body(
-        words_ref, normed_ref, split_ref, bias_ref, p0, p1, p2, p3,
-        qkv_ref, prob_ref, attended_ref, partial_ref, weights_ref, w_out_ref, spread, semaphores,
+        words_ref, in_ref, rep_ref, split_ref, bias_ref, o0, o1, o2, o3, p0, p1, p2, p3,
+        normed_ref, qkv_ref, prob_ref, attended_ref, partial_ref, weights_ref, w_out_ref, spread, semaphores,
     ):
         pair = pl.program_id(0)
 
         @pl.when(pair == 0)
         def _():
             copies = Copies(semaphores)
-            finish(copies.start(chunk_pairs(words_ref, (p0, p1, p2, p3), weights_ref)))
-            for block in range(count // BLOCK):
+            pairs = chunk_pairs(words_ref, (o0, o1, o2, o3), (p0, p1, p2, p3), 0, weights_ref)
+            loads = copies.start(pairs)
+
+            @pl.loop(0, count // BLOCK)
+            def _(block):
                 rows = pl.ds(block * BLOCK, BLOCK)
-                for part in range(3):
-                    columns = slice(part * half, (part + 1) * half)
-                    projected = product(normed_ref[rows, :], weights_ref[:, columns])
-                    if part != 1:
-                        projected = projected + split_ref[part // 2 : part // 2 + 1, :]
-                    qkv_ref[rows, columns] = projected.astype(jnp.bfloat16)
+                unit_signal, _ = norm_parts(in_ref[rows, :].astype(jnp.float32))
+                normed = unit_signal * rep_ref[0:1, :] + rep_ref[1:2, :]
+                normed_ref[rows, :] = normed.astype(jnp.bfloat16)
+
+            finish(loads)
+
+            @pl.loop(0, count // BLOCK)
+            def _(block):
+                rows = pl.ds(block * BLOCK, BLOCK)
+                projected = product(normed_ref[rows, :], weights_ref[:, : 3 * half])
+                queries = projected[:, :half] + split_ref[0:1, :]
+                values = projected[:, 2 * half :] + split_ref[1:2, :]
+                qkv_ref[rows, :half] = queries.astype(jnp.bfloat16)
+                qkv_ref[rows, half : 2 * half] = projected[:, half : 2 * half].astype(jnp.bfloat16)
+                qkv_ref[rows, 2 * half :] = values.astype(jnp.bfloat16)
 
         lane = pl.multiple_of(pair * (2 * HEAD), 2 * HEAD)
         upper = lax.broadcasted_iota(jnp.int32, (1, 2 * HEAD), 1) >= HEAD
@@ -758,8 +770,10 @@
     return pl.pallas_call(
         body,
         grid=(pairs_of_heads,),
-        in_specs=[IN_SMEM, fixed(count, width), fixed(6, half), fixed(1, count)] + [ANY] * 4,
+        in_specs=[IN_SMEM, fixed(count, width), fixed(6, width), fixed(6, half), fixed(1, count)]
+        + [ANY] * 8,
         out_specs=[
+            fixed(count, width),
             fixed(count, 3 * half),
             pl.BlockSpec((2, count, count), lambda h: (h, 0, 0)),
             fixed(count, half),
@@ -768,6 +782,7 @@
             fixed(half, width),
         ],
         out_shape=[
+            shaped((count, width), jnp.bfloat16),
             shaped((count, 3 * half), jnp.bfloat16),
             shaped((2 * pairs_of_heads, count, count), jnp.bfloat16),
             shaped((count, half), jnp.bfloat16),
@@ -782,18 +797,20 @@
         compiler_params=params(1),
         cost_estimate=cost(18),
         name="attention_forward",
-    )(words, normed, split, column_bias, *pieces)
-
-
-def mlp_all(words, rows_in, own, other, rep, split, grad_out, pieces_b, pieces_c):
+    )(words, rows_in, rep, split, column_bias, *own_pieces, *pieces)
+
+
+def mlp_all(
+    words, rows_in, own, other, rep, hidden_bias, grad_out, own_pieces, pieces
+):
     count, width = rows_in.shape
-    half = split.shape[1]
     hidden_width = UNIT_WIDTH
-    parts = hidden_width // half
+    half, wide = width // 2, 2 * BLOCK_WIDTH
+    parts = hidden_width // wide
 
     def body(
-        words_ref, rep_ref, split_ref, in_any, own_any, other_any, grad_any,
-        b0, b1, b2, b3, c0, c1, c2, c3,
+        words_ref, rep_ref, bias_ref, in_any, own_any, other_any, grad_any,
+        o0, o1, o2, o3, p0, p1, p2, p3,
         hidden_sum_ref, grad_sum_ref, middle_any, back_any, second_any,
         sent_b, kept_b, sent_c, kept_c,
         w_first, w_second, rows_ref, own_ref, other_ref, grad_ref, middle_ref, normed_ref,
@@ -803,21 +820,22 @@
         first_loads = copies.start(
             [(in_any, rows_ref), (own_any, own_ref), (other_any, other_ref)]
         )
-        loads_b = copies.start(chunk_pairs(words_ref, (b0, b1, b2, b3), w_first))
+        own_refs, later = (o0, o1, o2, o3), (p0, p1, p2, p3)
+        loads_b = copies.start(chunk_pairs(words_ref, own_refs, later, 1, w_first))
         pairs = [(grad_any, grad_ref)]
-        for piece, source in enumerate((c0, c1, c2, c3)):
-            for entry in range(4):
-                owner = owner_of(words_ref, piece, entry)
-                for side in range(2):
-                    pairs.append(
-                        (
-                            source.at[entry, :, pl.ds(side * width, width)],
-                            w_second.at[unit_rows(owner * 2 + side), :],
-                        )
+        for source, owner in chunk_sources(words_ref, own_refs, later, 2):
+            for side in range(2):
+                pairs.append(
+                    (
+                        source.at[:, pl.ds(side * width, width)],
+                        w_second.at[unit_rows(owner * 2 + side), :],
                     )
+                )
         loads_c = copies.start(pairs)
         finish(first_loads)
-        for block in range(count // BLOCK):
+
+        @pl.loop(0, count // BLOCK)
+        def _(block):
             rows = pl.ds(block * BLOCK, BLOCK)
             branch = own_ref[rows, :].astype(jnp.float32) + other_ref[rows, :].astype(jnp.float32)
             middle = rows_ref[rows, :].astype(jnp.float32) + branch + rep_ref[4:5, :]
@@ -825,22 +843,23 @@
             unit_signal, _ = norm_parts(middle)
             normed = unit_signal * rep_ref[2:3, :] + rep_ref[3:4, :]
             normed_ref[rows, :] = normed.astype(jnp.bfloat16)
+
         stores = copies.start([(middle_ref, middle_any)])
         finish(loads_b)
         for part in range(parts):
-            columns = slice(part * half, (part + 1) * half)
-            hidden = product(normed_ref[...], w_first[:, columns])
-            hidden = hidden + split_ref[2 + part : 3 + part, :]
+            columns = slice(part * wide, (part + 1) * wide)
+            hidden = product(normed_ref[...], w_first[:, columns]) + bias_ref[:, columns]
             spread = 0.5 + 0.5 * lax.erf(hidden * 0.7071067811865476)
             active_ref[:, columns] = (hidden * spread).astype(jnp.bfloat16)
             slope = spread + hidden * jnp.exp(-0.5 * hidden * hidden) * 0.3989422804014327
             slope_ref[:, columns] = slope.astype(jnp.bfloat16)
+
         finish(loads_c)
         second_ref[...] = product(active_ref[...], w_second[...]).astype(jnp.bfloat16)
         stores += copies.start([(second_ref, second_any)])
         grad_sum_ref[...] = jnp.sum(grad_ref[...].astype(jnp.float32), axis=0, keepdims=True)
         for part in range(parts):
-            columns = slice(part * half, (part + 1) * half)
+            columns = slice(part * wide, (part + 1) * wide)
             grad_active = contract_last(grad_ref[...], w_second[columns, :])
             grad_hidden = grad_active * slope_ref[:, columns].astype(jnp.float32)
             grad_hidden = grad_hidden.astype(jnp.bfloat16)
@@ -848,13 +867,17 @@
             hidden_sum_ref[:, columns] = jnp.sum(
                 grad_hidden.astype(jnp.float32), axis=0, keepdims=True
             )
+
         back_ref[...] = contract_last(grad_hidden_ref[...], w_first[...]).astype(jnp.bfloat16)
         stores += copies.start([(back_ref, back_any)])
-        for part in range(parts):
-            columns = slice(part * half, (part + 1) * half)
+
+        @pl.loop(0, hidden_width // half)
+        def _(part):
+            columns = lanes_of(part, half)
             whole_c[columns, :] = contract_rows(active_ref[:, columns], grad_ref[...]).astype(
                 jnp.bfloat16
             )
+
         for target, owner in unit_targets(words_ref, sent_c, kept_c):
             stores += copies.start(
                 [
@@ -865,11 +888,14 @@
                     for side in range(2)
                 ]
             )
-        for part in range(width // half):
-            columns = slice(part * half, (part + 1) * half)
+
+        @pl.loop(0, width // half)
+        def _(part):
+            columns = lanes_of(part, half)
             whole_b[columns, :] = contract_rows(normed_ref[:, columns], grad_hidden_ref[...]).astype(
                 jnp.bfloat16
             )
+
         for target, owner in unit_targets(words_ref, sent_b, kept_b):
             stores += copies.start([(whole_b.at[unit_rows(owner), :], target)])
         finish(stores)
@@ -909,7 +935,7 @@
         compiler_params=params(),
         cost_estimate=cost(18),
         name="mlp_all",
-    )(words, rep, split, rows_in, own, other, grad_out, *pieces_b, *pieces_c)
+    )(words, rep, hidden_bias, rows_in, own, other, grad_out, *own_pieces, *pieces)
 
 
 def attention_back(
@@ -941,14 +967,16 @@
         outer = copies.start([(w_out_any, w_out_ref), (attended_any, attended_ref)])
         inner = copies.start([(qkv_any, qkv_ref)])
         probs = copies.start(
-            [(prob_any.at[pl.ds(2 * pair, 2)], prob_ref.at[pair]) for pair in range(2)]
+            [(prob_any.at[pl.ds(2 * i, 2)], prob_ref.at[i]) for i in range(pairs_of_heads)]
         )
         late = copies.start(
             [(normed_any, normed_ref), (weights_any, weights_ref), (in_any, in_ref)]
         )
         vectors[...] = jnp.zeros_like(vectors)
         finish(early)
-        for block in range(count // BLOCK):
+
+        @pl.loop(0, count // BLOCK)
+        def _(block):
             rows = pl.ds(block * BLOCK, BLOCK)
             unit_signal, scale = norm_parts(middle_ref[rows, :])
             mine = own_ref[rows, :].astype(full)
@@ -962,6 +990,7 @@
             vectors[1:2, :width] += jnp.sum(mine * unit_signal, axis=0, keepdims=True)
             vectors[1:2, width:] += jnp.sum(mine, axis=0, keepdims=True)
             vectors[2:3, :width] += 0.5 * jnp.sum(grad_branch.astype(full), axis=0, keepdims=True)
+
         stores = copies.start([(grad_middle_ref, grad_middle_any)])
         finish(outer)
         grad_attended[...] = contract_last(branch[...], w_out_ref[...]).astype(low)
@@ -976,17 +1005,21 @@
             whole[:, start : start + 128] = spread[strip].astype(low)
         finish(inner)
         upper = lax.broadcasted_iota(jnp.int32, (1, 2 * HEAD), 1) >= HEAD
-        for pair in range(pairs_of_heads):
-            finish(probs[:1])
-            probs = probs[1:]
-            lanes = [slice(part * half + pair * 128, part * half + pair * 128 + 128) for part in range(3)]
+        finish(probs)
+
+        @pl.loop(0, pairs_of_heads)
+        def _(pair):
+            lanes = [
+                pl.ds(pl.multiple_of(part * half + pair * (2 * HEAD), 2 * HEAD), 2 * HEAD)
+                for part in range(3)
+            ]
             queries, keys, values = (qkv_ref[:, lane] for lane in lanes)
             grad = grad_attended[:, lanes[0]]
             found = []
             for side in range(2):
                 chosen = upper if side else jnp.logical_not(upper)
                 own_grad = jnp.where(chosen, grad, jnp.zeros_like(grad))
-                low_probability = prob_ref[pair % 2, side]
+                low_probability = prob_ref[pair, side]
                 probability = low_probability.astype(full)
                 weighted = probability * contract_last(own_grad, values)
                 inner_sum = jnp.sum(weighted, axis=1, keepdims=True)
@@ -998,10 +1031,6 @@
                         contract_rows(grad, low_probability)[side * HEAD : (side + 1) * HEAD],
                     )
                 )
-            if pair + 2 < pairs_of_heads:
-                probs += copies.start(
-                    [(prob_any.at[pl.ds(2 * pair + 4, 2)], prob_ref.at[pair % 2])]
-                )
             backs = (
                 jnp.where(upper, found[1][0], found[0][0]) * HEAD ** (-0.5),
                 jnp.transpose(jnp.concatenate([found[0][1], found[1][1]])) * HEAD ** (-0.5),
@@ -1009,13 +1038,19 @@
             )
             for lane, value in zip(lanes, backs):
                 grad_qkv[:, lane] = value.astype(low)
+
         finish(late)
-        for part in range(width // half):
-            columns = slice(part * half, (part + 1) * half)
+
+        @pl.loop(0, width // half)
+        def _(part):
+            columns = lanes_of(part, half)
             whole[columns, :span] = contract_rows(normed_ref[:, columns], grad_qkv[...]).astype(low)
+
         for target, owner in unit_targets(words_ref, sent, kept):
             stores += copies.start([(whole.at[unit_rows(owner), :], target)])
-        for block in range(count // BLOCK):
+
+        @pl.loop(0, count // BLOCK)
+        def _(block):
             rows = pl.ds(block * BLOCK, BLOCK)
             back = contract_last(grad_qkv[rows, :], weights_ref[:, :span])
             back_ref[rows, :] = back.astype(low)
@@ -1029,6 +1064,7 @@
                     keepdims=True,
                 )
                 vectors[3:4, place * half : (place + 1) * half] += sums
+
         stores += copies.start([(back_ref, back_any)])
         vectors[2:3, width:] = 0.5 * grad_sum_ref[...]
         vectors[3:4, 2 * half : span] = mask_sum_ref[...]
@@ -1051,7 +1087,7 @@
             pltpu.VMEM((half, width), low),
             pltpu.VMEM((count, half), low),
             pltpu.VMEM((count, span), low),
-            pltpu.VMEM((2, 2, count, count), low),
+            pltpu.VMEM((pairs_of_heads, 2, count, count), low),
             pltpu.VMEM((count, width), low),
             pltpu.VMEM((width, UNIT_WIDTH), low),
             pltpu.VMEM((count, width), low),
@@ -1176,7 +1212,8 @@
 
     inputs = patch_rows.reshape(row_count, feature_width)
     split_rows = split_master[0]
-    unit_a, unit_b, unit_c = pack_units(qkv_master, out_master, fc1_master, fc2_master)
+    hidden_bias = split_rows[2:].reshape(1, -1)
+    units, unit_a, units_later = pack_units(qkv_master, out_master, fc1_master, fc2_master)
 
     patch_index = jnp.arange(PATCHES, dtype=jnp.int32)
     visible_all = (patch_index[None, :] < lengths[:, None]) & (masked == 0)
@@ -1230,37 +1267,43 @@
     def columns_of(unit):
         return [hop(unit, distance, dp_count) for distance in Z_ORDER[1:]]
 
+    def along_z(messages):
+        return [hop(message, k, dp_count) for message, k in zip(messages, Z_ORDER[1:])]
+
+    own_first, own_second = spread_out(units)
     column_a = columns_of(unit_a)
-    normed = first_norm(inputs, rep_master)
-    column_a, normed, unit_b, unit_c, cotangent_rows, deal, unseen = together(
-        column_a, normed, unit_b, unit_c, cotangent_rows, deal, unseen
-    )
-
-    column_a = join_chunks([unit_a, *column_a])
+    column_a, own_first, own_second, units_later, cotangent_rows, deal, unseen = together(
+        column_a, own_first, own_second, units_later, cotangent_rows, deal, unseen
+    )
+
+    column_a = join_chunks(column_a)
     first_a, second_a = spread_out(column_a)
-    column_b = columns_of(unit_b)
+    own_third = hop_by_core(own_first, 2, 1, dp_count)
+    column_far = hop(units_later, 12, dp_count)
     dealt = product(deal, cotangent_rows).astype(jnp.bfloat16)
     mask_sum = product(unseen.astype(jnp.bfloat16)[None, :], cotangent_rows)
-    first_a, second_a, column_b, dealt, mask_sum, column_bias, pick = together(
-        first_a, second_a, column_b, dealt, mask_sum, column_bias, pick
+    first_a, second_a, own_third, dealt, mask_sum, column_bias, pick, column_far, units_later = (
+        together(
+            first_a, second_a, own_third, dealt, mask_sum, column_bias, pick, column_far,
+            units_later,
+        )
     )
 
     third_a = hop_by_core(first_a, 2, 1, dp_count)
-    column_c = columns_of(unit_c)
+    column = [hop(units_later, distance, dp_count) for distance in (4, 8)]
+    third_a, column, inputs_here, dealt = together(third_a, column, inputs, dealt)
+
+    column = join_chunks([column_far, *column])
+    first, last = spread_out(column)
     returned = exchanged(dealt)
-    column_b = join_chunks([unit_b, *column_b])
-    third_a, column_c, normed, column_b = together(third_a, column_c, normed, column_b)
-
-    first_b, second_b = spread_out(column_b)
-    column_c = join_chunks([unit_c, *column_c])
-    first_c, second_c = spread_out(column_c)
-    qkv, prob, attended, branch, weights_a, w_output = attention_forward(
-        words, normed, split_rows, column_bias, (column_a, first_a, second_a, third_a)
-    )
-    first_b, second_b, first_c, second_c = together(first_b, second_b, first_c, second_c)
-
-    third_b = hop_by_core(first_b, 2, 1, dp_count)
-    third_c = hop_by_core(first_c, 2, 1, dp_count)
+    own_pieces = (units, own_first, own_second, own_third)
+    normed, qkv, prob, attended, branch, weights_a, w_output = attention_forward(
+        words, inputs_here, rep_master, split_rows, column_bias, own_pieces,
+        (column_a, first_a, second_a, third_a),
+    )
+    first, last = together(first, last)
+
+    third = hop_by_core(first, 2, 1, dp_count)
     branch_other = swap_cores(branch)
     gathered = product(pick, returned).astype(jnp.bfloat16)
     gathered_other = swap_cores(gathered)
@@ -1269,11 +1312,11 @@
         jnp.concatenate([gathered, gathered_other], axis=1),
         jnp.concatenate([gathered_other, gathered], axis=1),
     )
-    third_b, third_c, branch_other, grad_out = together(third_b, third_c, branch_other, grad_out)
+    third, branch_other, grad_out = together(third, branch_other, grad_out)
 
     hidden_sum, grad_sum, middle, back_two, second, sent_b, kept_b, sent_c, kept_c = mlp_all(
-        words, inputs, branch, branch_other, rep_master, split_rows, grad_out,
-        (column_b, first_b, second_b, third_b), (column_c, first_c, second_c, third_c),
+        words, inputs, branch, branch_other, rep_master, hidden_bias, grad_out, own_pieces,
+        (column, first, last, third),
     )
     middle, back_two, second, sent_b, kept_b, sent_c, kept_c = together(
         middle, back_two, second, sent_b, kept_b, sent_c, kept_c
@@ -1288,7 +1331,7 @@
     outgoing = contract_rows(pick, result_half).astype(jnp.bfloat16)
     one_c, back_two_other, outgoing = together(one_c, back_two_other, outgoing)
 
-    half_unit, quarter, eighth = 4 * UNIT_ROWS, 2 * UNIT_ROWS, UNIT_ROWS
+    half_unit = 4 * UNIT_ROWS
     one_b = hop_by_core(sent_b, 2, 1, dp_count)
     two_c = hop_by_core(
         added(half_unit, 2 * half_unit, (kept_c, 0), (one_c, 0)), 1, 2, dp_count
@@ -1303,51 +1346,43 @@
     )
 
     one_a = hop_by_core(sent_a, 2, 1, dp_count)
-    back_one_other = swap_cores(back_one)
     two_b = hop_by_core(
         added(half_unit, 2 * half_unit, (kept_b, 0), (one_b, 0)), 1, 2, dp_count
     )
-    three_c = hop(
-        added(quarter, half_unit, (kept_c, 0), (one_c, 0), (two_c, 0)), 4, dp_count
-    )
+    arrivals_c = along_z(last_messages(kept_c, one_c, two_c))
     full_out = contract_rows(deal, arrived)
     full_out = jnp.where(unseen[:, None], mask_token.astype(jnp.float32)[None, :], full_out)
     full_out = full_out.astype(jnp.bfloat16)
-    one_a, three_c, two_b, back_one_other, full_out = together(
-        one_a, three_c, two_b, back_one_other, full_out
+    one_a, arrivals_c, two_b, full_out, back_one = together(
+        one_a, arrivals_c, two_b, full_out, back_one
     )
 
     two_a_sent = added(half_unit, 2 * half_unit + 16, (kept_a, 0), (one_a, 0))
     two_a = hop_by_core(two_a_sent, 1, 2, dp_count)
-    three_b = hop(
-        added(quarter, half_unit, (kept_b, 0), (one_b, 0), (two_b, 0)), 4, dp_count
-    )
-    four_c = hop(
-        added(eighth, quarter, (kept_c, 0), (one_c, 0), (two_c, 0), (three_c, 0)), 12, dp_count
-    )
-    input_grad = input_gradient(inputs, back_one, back_one_other, grad_middle, rep_master)
-    two_a_sent, two_a, four_c, three_b, input_grad = together(
-        two_a_sent, two_a, four_c, three_b, input_grad
-    )
-
-    messages = last_messages(kept_a, one_a, two_a, two_a_sent)
-    arrivals = [hop(message, k, dp_count) for message, k in zip(messages, Z_ORDER[1:])]
-    four_b = hop(
-        added(eighth, quarter, (kept_b, 0), (one_b, 0), (two_b, 0), (three_b, 0)), 12, dp_count
-    )
+    arrivals_b = along_z(last_messages(kept_b, one_b, two_b))
     fc2_new = adam_unit(
-        [(kept_c, one_c, two_c, three_c, four_c)],
+        [(kept_c, one_c, two_c, *arrivals_c)],
         [(fc2_master, fc2_first, fc2_second)],
         [(0, side * 6 + j, 0, side * UNIT_ROWS * 6 + j, 6) for side in range(2) for j in range(6)],
     )
-    arrivals, four_b, message, *fc2_new = together(arrivals, four_b, messages[0], *fc2_new)
-
+    back_one_other = swap_cores(back_one)
+    two_a_sent, two_a, arrivals_b, back_one_other, *fc2_new = together(
+        two_a_sent, two_a, arrivals_b, back_one_other, *fc2_new
+    )
+
+    messages = last_messages(kept_a, one_a, two_a, two_a_sent)
+    arrivals = along_z(messages)
     fc1_new = adam_unit(
-        [(kept_b, one_b, two_b, three_b, four_b)],
+        [(kept_b, one_b, two_b, *arrivals_b)],
         [(fc1_master, fc1_first, fc1_second)],
         [(0, j, 0, j, 12) for j in range(12)],
     )
-    vectors = [array[eighth:].astype(jnp.float32) for array in (message, *arrivals)]
+    input_grad = input_gradient(inputs, back_one, back_one_other, grad_middle, rep_master)
+    arrivals, message, input_grad, *fc1_new = together(
+        arrivals, messages[0], input_grad, *fc1_new
+    )
+
+    vectors = [array[UNIT_ROWS:].astype(jnp.float32) for array in (message, *arrivals)]
     vectors = (vectors[0] + vectors[1]) + (vectors[2] + vectors[3])
     rep_total = (vectors[:3] + swap_cores(vectors[:3])).reshape(rep_master.shape)
     split_total = jnp.concatenate(

time: 259 us -> 245 us (0.946)
  Pallas kernels: 94.7 us -> 85.2 us
  other arithmetic: 17.2 us -> 14.1 us
    pallas_call x1, Pallas kernels: 31.5 us -> 21.7 us  [mlp_all(): pl.pallas_call(body, in_specs=[IN_SMEM, IN_VMEM, IN_VMEM] + [ANY] * 12, o...]
    ppermute x15, waiting for transfers between devices: 31.5 us -> 24.1 us  [hop_by_core(): return lax.ppermute(array, ('dp', 'mp'), pairs)]
    ppermute x15, starting transfers between devices: 14.8 us -> 21.2 us  [hop_by_core(): return lax.ppermute(array, ('dp', 'mp'), pairs)]
    ppermute x16 -> x15, waiting for transfers between devices: 35.3 us -> 40.7 us  [hop(): lax.ppermute(array, 'dp', [(i, i ^ distance) for i in range(axis_count)])]
    ppermute x16 -> x15, starting transfers between devices: 27.7 us -> 23.1 us  [hop(): lax.ppermute(array, 'dp', [(i, i ^ distance) for i in range(axis_count)])]
    convert_element_type x7 -> x3, other arithmetic: 7.97 us -> 3.82 us  [added(): return total.astype(jnp.bfloat16)]
  transfers between devices with their start and end apart: 39 -> 38, of which waited for: 19 -> 21; matrix products, arithmetic and copies ran while one was open for 12% -> 14% of each run, Pallas kernels for 23% -> 23%
where the time goes in v1:
time: 245 us; the launch traced here: 244 us
  Pallas kernels  85.2 us (35%)
  waiting for transfers between devices  67.4 us (28%)
  starting transfers between devices  53.9 us (22%)
  other arithmetic  14.1 us (6%)
  matrix products  14.1 us (6%)
  local copies, waits for them, and re-layouts  7.87 us (3%)
    ppermute x15, waiting for transfers between devices, hop(): lax.ppermute(array, 'dp', [(i, i ^ distance) for i in range(axis_count)])  40.7 us
    ppermute x15, waiting for transfers between devices, hop_by_core(): return lax.ppermute(array, ('dp', 'mp'), pairs)  24.1 us
    ppermute x15, starting transfers between devices, hop(): lax.ppermute(array, 'dp', [(i, i ^ distance) for i in range(axis_count)])  23.1 us
    pallas_call x1, Pallas kernels, mlp_all(): pl.pallas_call(body, in_specs=[IN_SMEM, IN_VMEM, IN_VMEM] + [ANY] * 12, o...  21.7 us
    ppermute x15, starting transfers between devices, hop_by_core(): return lax.ppermute(array, ('dp', 'mp'), pairs)  21.2 us
    pallas_call x1, Pallas kernels, attention_back(): pl.pallas_call(body, in_specs=[IN_SMEM] + [IN_VMEM] * 4 + [ANY] * 11, out...  20.7 us
    pallas_call x1, Pallas kernels, attention_forward(): pl.pallas_call(body, grid=(pairs_of_heads,), in_specs=[IN_SMEM, fixed(cou...  16.8 us
    all_to_all x2, starting transfers between devices, exchanged(): array = lax.all_to_all(array, 'dp', split_axis=0, concat_axis=0, tiled=True)  9.05 us
  transfers between devices with their start and end apart: 38, of which 21 were waited for; matrix products, arithmetic and copies ran while one was open for 14% of the time, Pallas kernels for 23%

profile of v1, /device:TPU:0, one launch (start us, length us, event | category | flops | bytes accessed | tf_op | source)
XLA Modules:
  0.0 243.8 jit_solution(7402786805171225574)
XLA Ops:
  0.7 2.2 pack_units.1
  2.9 2.9 %collective-permute-start.3 = (bf16[3,48,1536]{2,1,0:T(8,128)(2,1)}, bf16[3,48,1536]{2,1,0:T(8,128)(2,1)}, u32[]{:S(2)}, u32[]{:S(2)}) collective-permute-start(bf16[3,48,1536]{2,1,0:T(8,128)(2,1)} %get-tuple-element.134.o0), channel_id=1, source_target_pairs={{0,2},{1,5},{2,0},{3,7},{4,6},{5,1},{6,4},{7,3},{8,10},{9,13},{10,... | collective-permute-start | bytes 1327112 | tf_op jit(solution)/shard_map/ppermute | solution.py:514
  5.9 1.5 collective-permute-start.4
  7.4 3.6 %collective-permute-start = (bf16[1,48,1536]{2,1,0:T(8,128)(2,1)}, bf16[1,48,1536]{2,1,0:T(8,128)(2,1)}, u32[]{:S(2)}, u32[]{:S(2)}) collective-permute-start(bf16[1,48,1536]{2,1,0:T(8,128)(2,1)} %get-tuple-element.133), channel_id=1, source_target_pairs={{0,24},{2,26},{4,28},{6,30},{8,16},{10,18},{12,20},{14,22},{16,8},... | collective-permute-start | bytes 442376 | tf_op jit(solution)/shard_map/ppermute | solution.py:116
  16.1 1.8 fusion.1
  17.9 1.5 gather_fusion
  21.0 2.3 collective-permute-done.2.refs_2_
  23.2 1.9 join_chunks.2.p0
  26.1 1.5 collective-permute-start.7
  27.7 2.6 %collective-permute-start.8 = (bf16[2,48,1536]{2,1,0:T(8,128)(2,1)}, bf16[2,48,1536]{2,1,0:T(8,128)(2,1)S(1)}, u32[]{:S(2)}, u32[]{:S(2)}) collective-permute-start(bf16[2,48,1536]{2,1,0:T(8,128)(2,1)} %get-tuple-element.145), channel_id=1, source_target_pairs={{0,24},{2,26},{4,28},{6,30},{8,16},{10,18},{12,20},{14,22},{16,8},... | collective-permute-start | bytes 884744 | tf_op jit(solution)/shard_map/ppermute | solution.py:116
  30.3 2.6 %convolution_convert_fusion.1 = bf16[1152,384]{1,0:T(8,128)(2,1)} fusion(bf16[1152,1088]{1,0:T(8,128)(2,1)S(1)} %fusion, bf16[1088,384]{1,0:T(8,128)(2,1)S(1)} %bitcast.71), kind=kOutput, calls=%fused_computation.7 | convolution fusion | flops 963035136 | bytes 4227072 | tf_op jit(solution)/shard_map/dot_general | solution.py:34
  33.7 3.2 %collective-permute-done.8.refs_0_ = bf16[2,48,1536]{2,1,0:T(8,128)(2,1)S(1)} collective-permute-done((bf16[2,48,1536]{2,1,0:T(8,128)(2,1)}, bf16[2,48,1536]{2,1,0:T(8,128)(2,1)S(1)}, u32[]{:S(2)}, u32[]{:S(2)}) %collective-permute-start.8) | collective-permute-done | bytes 294944 | tf_op jit(solution)/shard_map/ppermute | solution.py:116
  36.9 1.6 collective-permute-done.5.p1
  38.5 2.8 %collective-permute-done.7.o3 = bf16[3,48,1536]{2,1,0:T(8,128)(2,1)} collective-permute-done((bf16[3,48,1536]{2,1,0:T(8,128)(2,1)}, bf16[3,48,1536]{2,1,0:T(8,128)(2,1)}, u32[]{:S(2)}, u32[]{:S(2)}) %collective-permute-start.7) | collective-permute-done | bytes 442400 | tf_op jit(solution)/shard_map/ppermute | solution.py:514
  42.2 2.5 %collective-permute-start.11 = (bf16[2,48,1536]{2,1,0:T(8,128)(2,1)}, bf16[2,48,1536]{2,1,0:T(8,128)(2,1)}, u32[]{:S(2)}, u32[]{:S(2)}) collective-permute-start(bf16[2,48,1536]{2,1,0:T(8,128)(2,1)} %get-tuple-element.145), channel_id=1, source_target_pairs={{0,16},{2,18},{4,20},{6,22},{8,24},{10,26},{12,28},{14,30},{16,0},... | collective-permute-start | bytes 884744 | tf_op jit(solution)/shard_map/ppermute | solution.py:116
  45.9 10.9 %collective-permute-done.10.refs_1_ = bf16[2,48,1536]{2,1,0:T(8,128)(2,1)S(1)} collective-permute-done((bf16[2,48,1536]{2,1,0:T(8,128)(2,1)}, bf16[2,48,1536]{2,1,0:T(8,128)(2,1)S(1)}, u32[]{:S(2)}, u32[]{:S(2)}) %collective-permute-start.10) | collective-permute-done | bytes 294944 | tf_op jit(solution)/shard_map/ppermute | solution.py:116
  56.9 1.3 collective-permute-done.11.refs_2_
  58.2 2.3 join_chunks.3.p0
  60.5 1.5 collective-permute-start.12
  62.0 1.5 collective-permute-start.13
  63.5 4.3 %all-to-all-start = ((bf16[16,72,384]{2,1,0:T(8,128)(2,1)}), bf16[16,72,384]{2,1,0:T(8,128)(2,1)}, u32[]{:S(2)}, u32[]{:S(2)}) async-start(bf16[16,72,384]{2,1,0:T(8,128)(2,1)} %bitcast.72), calls=%async_computation | async-start | bytes 1769472 | tf_op jit(solution)/shard_map/all_to_all | solution.py:1264
  67.8 16.8 %attention_forward.1 = (bf16[768,768]{1,0:T(8,128)(2,1)}, bf16[768,1152]{1,0:T(8,128)(2,1)}, bf16[6,768,768]{2,1,0:T(8,128)(2,1)}, bf16[768,384]{1,0:T(8,128)(2,...) custom-call(s32[4]{0:T(128)} %pad_add_fusion.words_ref, ...), custom_call_target="tpu_custom_call" | custom-call | flops 20700000256 | bytes 1000000 | tf_op jit(solution)/shard_map/attention_forward/pallas_call | solution.py:770
  84.7 5.8 %collective-permute-done.12.p1 = bf16[6,48,1536]{2,1,0:T(8,128)(2,1)} collective-permute-done((bf16[6,48,1536]{2,1,0:T(8,128)(2,1)}, bf16[6,48,1536]{2,1,0:T(8,128)(2,1)}, u32[]{:S(2)}, u32[]{:S(2)}) %collective-permute-start.12) | collective-permute-done | bytes 884768 | tf_op jit(solution)/shard_map/ppermute | solution.py:514
  90.5 1.3 collective-permute-start.14
  92.7 2.8 %convolution_convert_fusion.2 = bf16[768,384]{1,0:T(8,128)(2,1)S(1)} fusion(bf16[768,1152]{1,0:T(8,128)(2,1)} %fusion.1, bf16[1152,384]{1,0:T(8,128)(2,1)} %bitcast.16), kind=kOutput, calls=%fused_computation.9 | convolution fusion | flops 679772160 | bytes 3244032 | tf_op jit(solution)/shard_map/dot_general | solution.py:34
  96.2 1.5 collective-permute-done.16
  97.7 2.6 %maximum_select_fusion.grad_any = bf16[768,768]{1,0:T(8,128)(2,1)} fusion(bf16[768,384]{1,0:T(8,128)(2,1)} %collective-permute-done.16, bf16[768,384]{1,0:T(8,128)(2,1)S(1)} %convolution_convert_fusion.2, pred[]{:T(512)S(6)} %eq.46), kind=kLoop, calls=%fused_computation.13 | loop fusion | flops 5308416 | bytes 2359297 | tf_op jit(solution)/shard_map/jit(_where)/select_n | solution.py:1310
  100.3 3.5 %collective-permute-done.14.p3 = bf16[6,48,1536]{2,1,0:T(8,128)(2,1)} collective-permute-done((bf16[6,48,1536]{2,1,0:T(8,128)(2,1)}, bf16[6,48,1536]{2,1,0:T(8,128)(2,1)}, u32[]{:S(2)}, u32[]{:S(2)}) %collective-permute-start.14) | collective-permute-done | bytes 884768 | tf_op jit(solution)/shard_map/ppermute | solution.py:514
  103.8 21.7 %mlp_all.1 = (f32[1,1536]{1,0:T(1,128)}, f32[1,768]{1,0:T(1,128)}, f32[768,768]{1,0:T(8,128)}, bf16[768,768]{1,0:T(8,128)(2,1)}, bf16[768,768]{1,0:T(8,128)(2,1)...) custom-call(s32[4]{0:T(128)} %pad_add_fusion.words_ref, ...), custom_call_target="tpu_custom_call" | custom-call | flops 20700000256 | bytes 1000000 | tf_op jit(solution)/shard_map/mlp_all/pallas_call | solution.py:904
  125.6 1.4 collective-permute-start.17
  128.0 1.6 collective-permute-start.21
  129.6 4.2 %convolution_convert_fusion = bf16[1152,384]{1,0:T(8,128)(2,1)} fusion(bf16[768,1152]{1,0:T(8,128)(2,1)} %fusion.1, f32[768,768]{1,0:T(8,128)} %get-tuple-element.174.middle_any, s32[]{:T(128)S(6)} %select_n.70, f32[384]{0:T(512)S(1)} %dynamic-slice, bf16[768,768]{1,0:T(8,128)(2,1)} %collective-permute-done.19, bf16[768,768]{1,0:T(8,128)(2,1)} %get-tuple-element.175), kind=kOutput, calls=%fused_computation.6 | convolution fusion | flops 681689088 | bytes 5015044 | tf_op jit(solution)/shard_map/dot_general | solution.py:44
  133.8 8.4 %collective-permute-done.17.one_ref.refs_1_ = bf16[384,1536]{1,0:T(8,128)(2,1)} collective-permute-done((bf16[384,1536]{1,0:T(8,128)(2,1)}, bf16[384,1536]{1,0:T(8,128)(2,1)}, u32[]{:S(2)}, u32[]{:S(2)}) %collective-permute-start.17) | collective-permute-done | bytes 1179680 | tf_op jit(solution)/shard_map/ppermute | solution.py:514
  142.2 1.2 add_convert_fusion.2
  143.4 1.5 collective-permute-start.20
  144.8 4.8 %all-to-all-start.1 = ((bf16[16,72,384]{2,1,0:T(8,128)(2,1)}), bf16[16,72,384]{2,1,0:T(8,128)(2,1)}, u32[]{:S(2)}, u32[]{:S(2)}) async-start(bf16[16,72,384]{2,1,0:T(8,128)(2,1)} %bitcast.73), calls=%async_computation.1 | async-start | bytes 1769472 | tf_op jit(solution)/shard_map/all_to_all | solution.py:1264
  149.6 20.7 %attention_back.1 = (f32[768,768]{1,0:T(8,128)}, bf16[768,768]{1,0:T(8,128)(2,1)}, bf16[400,1536]{1,0:T(8,128)(2,1)}, bf16[400,1536]{1,0:T(8,128)(2,1)}) custom-call(s32[4]{0:T(128)} %pad_add_fusion.words_ref, f32[6,768]{1,0:T(8,128)} %rep_ref.7, f32[1,1536]{1,0:T(1,128)} %get-tuple-element.178.hidden_sum_ref, f32[1,768]{1,0:T(1,128)} %get-tuple-element.179.grad_sum_ref, ...), custom_call_target="tpu_custom_call" | custom-call | flops 25300000768 | bytes 1000000 | tf_op jit(solution)/shard_map/attention_back/pallas_call | solution.py:1077
  170.6 1.7 collective-permute-start.22
  172.3 1.4 add_convert_fusion.1
  173.7 1.5 collective-permute-start.26
  175.2 2.2 last_messages.3
  177.5 3.3 %collective-permute-start.23 = (bf16[48,1536]{1,0:T(8,128)(2,1)}, bf16[48,1536]{1,0:T(8,128)(2,1)S(1)}, u32[]{:S(2)}, u32[]{:S(2)}) collective-permute-start(bf16[48,1536]{1,0:T(8,128)(2,1)} %get-tuple-element.194), channel_id=1, source_target_pairs={{0,24},{2,26},{4,28},{6,30},{8,16},{10,18},{12,20},{14,22},{16,8},... | collective-permute-start | bytes 442376 | tf_op jit(solution)/shard_map/ppermute | solution.py:116
  180.7 1.1 collective-permute-start.25
  181.9 3.7 %select_convert_fusion = bf16[1088,384]{1,0:T(8,128)(2,1)} fusion(bf16[384]{0:T(512)(128)(2,1)S(1)} %copy-done.28, pred[1088]{0:T(1024)(128)(4,1)S(1)} %reshape.320, bf16[1152,1088]{1,0:T(8,128)(2,1)S(1)} %fusion, bf16[1152,384]{1,0:T(8,128)(2,1)} %bitcast.18), kind=kOutput, calls=%fused_computation.8 | convolution fusion | flops 963010560 | bytes 4228928 | tf_op jit(solution)/shard_map/dot_general | solution.py:44
  186.4 2.3 collective-permute-done.24.refs_4_
  188.7 3.3 %collective-permute-done.25.refs_5_ = bf16[48,1536]{1,0:T(8,128)(2,1)S(1)} collective-permute-done((bf16[48,1536]{1,0:T(8,128)(2,1)}, bf16[48,1536]{1,0:T(8,128)(2,1)S(1)}, u32[]{:S(2)}, u32[]{:S(2)}) %collective-permute-start.25) | collective-permute-done | bytes 147488 | tf_op jit(solution)/shard_map/ppermute | solution.py:116
  192.0 2.0 collective-permute-done.22.one_ref.refs_1_
  194.0 1.2 add_convert_fusion.refs_0_
  195.2 1.8 collective-permute-start.27
  197.0 2.2 last_messages.4
  199.3 2.6 %collective-permute-start.28 = (bf16[48,1536]{1,0:T(8,128)(2,1)}, bf16[48,1536]{1,0:T(8,128)(2,1)S(1)}, u32[]{:S(2)}, u32[]{:S(2)}) collective-permute-start(bf16[48,1536]{1,0:T(8,128)(2,1)} %get-tuple-element.205), channel_id=1, source_target_pairs={{0,24},{2,26},{4,28},{6,30},{8,16},{10,18},{12,20},{14,22},{16,8},... | collective-permute-start | bytes 442376 | tf_op jit(solution)/shard_map/ppermute | solution.py:116
  201.9 1.8 collective-permute-start.30
  203.7 2.7 %adam_unit.3 = (f32[576,128]{1,0:T(8,128)}, f32[576,128]{1,0:T(8,128)}, f32[576,128]{1,0:T(8,128)}) custom-call(bf16[384,1536]{1,0:T(8,128)(2,1)} %get-tuple-element.171.kept_ref.refs_0_, bf16[384,1536]{1,0:T(8,128)(2,1)} %collective-permute-done.17.one_ref.refs_1_, bf16[192,1536]{1,0:T(8,128)(2,1)} %collective-permute-done.20.two_ref.refs_2_, ...), custom_call_target="tpu_custom_call" | custom-call | flops 2875000064 | bytes 1000000 | tf_op jit(solution)/shard_map/adam_unit/pallas_call | solution.py:1156
  206.4 1.6 collective-permute-done.28.refs_3_
  208.1 3.4 %collective-permute-done.29.refs_4_ = bf16[48,1536]{1,0:T(8,128)(2,1)S(1)} collective-permute-done((bf16[48,1536]{1,0:T(8,128)(2,1)}, bf16[48,1536]{1,0:T(8,128)(2,1)S(1)}, u32[]{:S(2)}, u32[]{:S(2)}) %collective-permute-start.29) | collective-permute-done | bytes 147488 | tf_op jit(solution)/shard_map/ppermute | solution.py:116
  211.5 4.6 %collective-permute-done.30.refs_5_ = bf16[48,1536]{1,0:T(8,128)(2,1)S(1)} collective-permute-done((bf16[48,1536]{1,0:T(8,128)(2,1)}, bf16[48,1536]{1,0:T(8,128)(2,1)S(1)}, u32[]{:S(2)}, u32[]{:S(2)}) %collective-permute-start.30) | collective-permute-done | bytes 147488 | tf_op jit(solution)/shard_map/ppermute | solution.py:116
  217.0 2.3 last_messages.5
  219.3 2.2 collective-permute-start.32
  221.5 2.2 collective-permute-start.34
  223.7 4.7 %input_gradient.1 = f32[768,768]{1,0:T(8,128)} custom-call(bf16[768,768]{1,0:T(8,128)(2,1)} %bitcast.83, bf16[768,768]{1,0:T(8,128)(2,1)} %get-tuple-element.208.own_ref, bf16[768,768]{1,0:T(8,128)(2,1)} %copy-done.17, f32[768,768]{1,0:T(8,128)} %get-tuple-element.221.middle_ref, f32[6,768]{1,0:T(8,128)} %rep_ref.7), custom_call_target="tpu_custom_call" | custom-call | flops 6554999808 | bytes 1000000 | tf_op jit(solution)/shard_map/input_gradient/pallas_call | solution.py:1123
  228.5 2.7 %adam_unit.4 = (f32[576,128]{1,0:T(8,128)}, f32[576,128]{1,0:T(8,128)}, f32[576,128]{1,0:T(8,128)}) custom-call(bf16[384,1536]{1,0:T(8,128)(2,1)} %get-tuple-element.197.kept_ref.refs_0_, bf16[384,1536]{1,0:T(8,128)(2,1)} %collective-permute-done.21.one_ref.refs_1_, bf16[192,1536]{1,0:T(8,128)(2,1)} %collective-permute-done.26.two_ref.refs_2_, ...), custom_call_target="tpu_custom_call" | custom-call | flops 2875000064 | bytes 1000000 | tf_op jit(solution)/shard_map/adam_unit/pallas_call | solution.py:1156
  231.2 4.4 %collective-permute-done.33.refs_4_ = bf16[64,1536]{1,0:T(8,128)(2,1)S(1)} collective-permute-done((bf16[64,1536]{1,0:T(8,128)(2,1)}, bf16[64,1536]{1,0:T(8,128)(2,1)S(1)}, u32[]{:S(2)}, u32[]{:S(2)}) %collective-permute-start.33) | collective-permute-done | bytes 196640 | tf_op jit(solution)/shard_map/ppermute | solution.py:116
  235.6 2.4 collective-permute-done.34.refs_5_
  239.8 2.7 %adam_unit.5 = (f32[432,128]{1,0:T(8,128)}, f32[432,128]{1,0:T(8,128)}, f32[432,128]{1,0:T(8,128)}, f32[144,128]{1,0:T(8,128)}, f32[144,128]{1,0:T(8,128)}, /*index=5*/f32[144,128]{1,0:T(8,128)}) custom-call(bf16[400,1536]{1,0:T(8,128)(2,1)} %get-tuple-element.202.kept_ref.refs_0_, bf16[400,1536]{1,0:T(8,128)(2,1)} %collective-permute-done.22.one_ref.refs_1_, ...), custom_call_target="tpu_custom_call" | custom-call | flops 2875000064 | bytes 1000000 | tf_op jit(solution)/shard_map/adam_unit/pallas_call | solution.py:1156
  (144 shorter events, 18.3 us)
Async XLA Ops:
  0.7 22.6 %copy-start = (bf16[32,34,1,384]{3,0,2,1:T(8,128)(2,1)S(1)}, bf16[32,34,1,384]{3,0,2,1:T(8,128)(2,1)}, u32[]{:S(2)}) copy-start(bf16[32,34,1,384]{3,0,2,1:T(8,128)(2,1)} %param.25) | copy-start | bytes 2506756
  0.7 11.7 %copy-start.5 = (s32[32,529]{1,0:T(8,128)S(1)}, s32[32,529]{1,0:T(8,128)}, u32[]{:S(2)}) copy-start(s32[32,529]{1,0:T(8,128)} %param.28) | copy-start | bytes 203140
  0.7 11.7 %copy-start.15 = (s32[32]{0:T(128)S(1)}, s32[32]{0:T(128)}, u32[]{:S(2)}) copy-start(s32[32]{0:T(128)} %param.27) | copy-start | bytes 388
  0.7 12.5 %copy-start.16 = (s32[32]{0:T(128)S(1)}, s32[32]{0:T(128)}, u32[]{:S(2)}) copy-start(s32[32]{0:T(128)} %param.29) | copy-start | bytes 388
  2.9 20.3 %collective-permute-start.3 = (bf16[3,48,1536]{2,1,0:T(8,128)(2,1)}, bf16[3,48,1536]{2,1,0:T(8,128)(2,1)}, u32[]{:S(2)}, u32[]{:S(2)}) collective-permute-start(bf16[3,48,1536]{2,1,0:T(8,128)(2,1)} %get-tuple-element.134.o0), channel_id=1, source_target_pairs={{0,2},{1,5},{2,0},{3,7},{4,6},{5,1},{6,4},{7,3},{8,10},{9,13},{10,... | collective-permute-start | bytes 1327112 | tf_op jit(solution)/shard_map/ppermute | solution.py:514
  5.9 17.4 %collective-permute-start.4 = (bf16[3,48,1536]{2,1,0:T(8,128)(2,1)}, bf16[3,48,1536]{2,1,0:T(8,128)(2,1)}, u32[]{:S(2)}, u32[]{:S(2)}) collective-permute-start(bf16[3,48,1536]{2,1,0:T(8,128)(2,1)} %get-tuple-element.134.o0), channel_id=1, source_target_pairs={{0,4},{1,3},{2,6},{3,1},{4,0},{5,7},{6,2},{7,5},{8,12},{9,11},{10,... | collective-permute-start | bytes 1327112 | tf_op jit(solution)/shard_map/ppermute | solution.py:514
  7.4 13.6 %collective-permute-start = (bf16[1,48,1536]{2,1,0:T(8,128)(2,1)}, bf16[1,48,1536]{2,1,0:T(8,128)(2,1)}, u32[]{:S(2)}, u32[]{:S(2)}) collective-permute-start(bf16[1,48,1536]{2,1,0:T(8,128)(2,1)} %get-tuple-element.133), channel_id=1, source_target_pairs={{0,24},{2,26},{4,28},{6,30},{8,16},{10,18},{12,20},{14,22},{16,8},... | collective-permute-start | bytes 442376 | tf_op jit(solution)/shard_map/ppermute | solution.py:116
  11.0 10.0 %collective-permute-start.1 = (bf16[1,48,1536]{2,1,0:T(8,128)(2,1)}, bf16[1,48,1536]{2,1,0:T(8,128)(2,1)}, u32[]{:S(2)}, u32[]{:S(2)}) collective-permute-start(bf16[1,48,1536]{2,1,0:T(8,128)(2,1)} %get-tuple-element.133), channel_id=1, source_target_pairs={{0,8},{2,10},{4,12},{6,14},{8,0},{10,2},{12,4},{14,6},{16,24},{18,... | collective-permute-start | bytes 442376 | tf_op jit(solution)/shard_map/ppermute | solution.py:116
  11.0 12.2 %collective-permute-start.2 = (bf16[1,48,1536]{2,1,0:T(8,128)(2,1)}, bf16[1,48,1536]{2,1,0:T(8,128)(2,1)}, u32[]{:S(2)}, u32[]{:S(2)}) collective-permute-start(bf16[1,48,1536]{2,1,0:T(8,128)(2,1)} %get-tuple-element.133), channel_id=1, source_target_pairs={{0,16},{2,18},{4,20},{6,22},{8,24},{10,26},{12,28},{14,30},{16,0},... | collective-permute-start | bytes 442376 | tf_op jit(solution)/shard_map/ppermute | solution.py:116
  25.1 19.7 %copy-start.6 = (f32[1,6,384]{2,0,1:T(1,128)S(1)}, f32[1,6,384]{2,0,1:T(1,128)}, u32[]{:S(2)}) copy-start(f32[1,6,384]{2,0,1:T(1,128)} %param.45) | copy-start | bytes 27652
  25.1 13.4 %collective-permute-start.5 = (bf16[3,48,1536]{2,1,0:T(8,128)(2,1)}, bf16[3,48,1536]{2,1,0:T(8,128)(2,1)}, u32[]{:S(2)}, u32[]{:S(2)}) collective-permute-start(bf16[3,48,1536]{2,1,0:T(8,128)(2,1)} %join_chunks.2.p0), channel_id=1, source_target_pairs={{0,2},{1,5},{2,0},{3,7},{4,6},{5,1},{6,4},{7,3},{8,10},{9,13},{10,... | collective-permute-start | bytes 1327112 | tf_op jit(solution)/shard_map/ppermute | solution.py:514
  25.6 12.9 %collective-permute-start.6 = (bf16[3,48,1536]{2,1,0:T(8,128)(2,1)}, bf16[3,48,1536]{2,1,0:T(8,128)(2,1)}, u32[]{:S(2)}, u32[]{:S(2)}) collective-permute-start(bf16[3,48,1536]{2,1,0:T(8,128)(2,1)} %join_chunks.2.p0), channel_id=1, source_target_pairs={{0,4},{1,3},{2,6},{3,1},{4,0},{5,7},{6,2},{7,5},{8,12},{9,11},{10,... | collective-permute-start | bytes 1327112 | tf_op jit(solution)/shard_map/ppermute | solution.py:514
  26.1 15.2 %collective-permute-start.7 = (bf16[3,48,1536]{2,1,0:T(8,128)(2,1)}, bf16[3,48,1536]{2,1,0:T(8,128)(2,1)}, u32[]{:S(2)}, u32[]{:S(2)}) collective-permute-start(bf16[3,48,1536]{2,1,0:T(8,128)(2,1)} %collective-permute-done.3.o1), channel_id=1, source_target_pairs={{0,4},{1,3},{2,6},{3,1},{4,0},{5,7},{6,2},{7,5},{8,12},{9,11},{10,... | collective-permute-start | bytes 1327112 | tf_op jit(solution)/shard_map/ppermute | solution.py:514
  27.7 9.3 %collective-permute-start.8 = (bf16[2,48,1536]{2,1,0:T(8,128)(2,1)}, bf16[2,48,1536]{2,1,0:T(8,128)(2,1)S(1)}, u32[]{:S(2)}, u32[]{:S(2)}) collective-permute-start(bf16[2,48,1536]{2,1,0:T(8,128)(2,1)} %get-tuple-element.145), channel_id=1, source_target_pairs={{0,24},{2,26},{4,28},{6,30},{8,16},{10,18},{12,20},{14,22},{16,8},... | collective-permute-start | bytes 884744 | tf_op jit(solution)/shard_map/ppermute | solution.py:116
  36.9 4.4 %copy-start.20 = (bf16[2,48,1536]{2,1,0:T(8,128)(2,1)}, bf16[2,48,1536]{2,1,0:T(8,128)(2,1)S(1)}, u32[]{:S(2)}) copy-start(bf16[2,48,1536]{2,1,0:T(8,128)(2,1)S(1)} %collective-permute-done.8.refs_0_) | copy-start | bytes 884740
  41.3 16.9 %collective-permute-start.9 = (bf16[3,48,1536]{2,1,0:T(8,128)(2,1)}, bf16[3,48,1536]{2,1,0:T(8,128)(2,1)S(1)}, u32[]{:S(2)}, u32[]{:S(2)}) collective-permute-start(bf16[3,48,1536]{2,1,0:T(8,128)(2,1)} %collective-permute-done.5.p1), channel_id=1, source_target_pairs={{0,4},{1,3},{2,6},{3,1},{4,0},{5,7},{6,2},{7,5},{8,12},{9,11},{10,... | collective-permute-start | bytes 1327112 | tf_op jit(solution)/shard_map/ppermute | solution.py:514
  41.8 15.0 %collective-permute-start.10 = (bf16[2,48,1536]{2,1,0:T(8,128)(2,1)}, bf16[2,48,1536]{2,1,0:T(8,128)(2,1)S(1)}, u32[]{:S(2)}, u32[]{:S(2)}) collective-permute-start(bf16[2,48,1536]{2,1,0:T(8,128)(2,1)} %get-tuple-element.145), channel_id=1, source_target_pairs={{0,8},{2,10},{4,12},{6,14},{8,0},{10,2},{12,4},{14,6},{16,24},{18,... | collective-permute-start | bytes 884744 | tf_op jit(solution)/shard_map/ppermute | solution.py:116
  42.2 16.0 %collective-permute-start.11 = (bf16[2,48,1536]{2,1,0:T(8,128)(2,1)}, bf16[2,48,1536]{2,1,0:T(8,128)(2,1)}, u32[]{:S(2)}, u32[]{:S(2)}) collective-permute-start(bf16[2,48,1536]{2,1,0:T(8,128)(2,1)} %get-tuple-element.145), channel_id=1, source_target_pairs={{0,16},{2,18},{4,20},{6,22},{8,24},{10,26},{12,28},{14,30},{16,0},... | collective-permute-start | bytes 884744 | tf_op jit(solution)/shard_map/ppermute | solution.py:116
  58.2 2.3 copy-start.19
  60.5 29.9 %collective-permute-start.12 = (bf16[6,48,1536]{2,1,0:T(8,128)(2,1)}, bf16[6,48,1536]{2,1,0:T(8,128)(2,1)}, u32[]{:S(2)}, u32[]{:S(2)}) collective-permute-start(bf16[6,48,1536]{2,1,0:T(8,128)(2,1)} %join_chunks.3.p0), channel_id=1, source_target_pairs={{0,2},{1,5},{2,0},{3,7},{4,6},{5,1},{6,4},{7,3},{8,10},{9,13},{10,... | collective-permute-start | bytes 2654216 | tf_op jit(solution)/shard_map/ppermute | solution.py:514
  62.0 28.5 %collective-permute-start.13 = (bf16[6,48,1536]{2,1,0:T(8,128)(2,1)}, bf16[6,48,1536]{2,1,0:T(8,128)(2,1)}, u32[]{:S(2)}, u32[]{:S(2)}) collective-permute-start(bf16[6,48,1536]{2,1,0:T(8,128)(2,1)} %join_chunks.3.p0), channel_id=1, source_target_pairs={{0,4},{1,3},{2,6},{3,1},{4,0},{5,7},{6,2},{7,5},{8,12},{9,11},{10,... | collective-permute-start | bytes 2654216 | tf_op jit(solution)/shard_map/ppermute | solution.py:514
  63.5 29.3 %all-to-all-start = ((bf16[16,72,384]{2,1,0:T(8,128)(2,1)}), bf16[16,72,384]{2,1,0:T(8,128)(2,1)}, u32[]{:S(2)}, u32[]{:S(2)}) async-start(bf16[16,72,384]{2,1,0:T(8,128)(2,1)} %bitcast.72), calls=%async_computation | async-start | bytes 1769472 | tf_op jit(solution)/shard_map/all_to_all | solution.py:1264
  84.6 15.7 %collective-permute-start.15 = (bf16[768,768]{1,0:T(8,128)(2,1)}, bf16[768,768]{1,0:T(8,128)(2,1)}, u32[]{:S(2)}, u32[]{:S(2)}) collective-permute-start(bf16[768,768]{1,0:T(8,128)(2,1)} %get-tuple-element.153.own_any), channel_id=1, source_target_pairs={{0,1},{1,0},{2,3},{3,2},{4,5},{5,4},{6,7},{7,6},{8,9},{9,8},{10,11... | collective-permute-start | bytes 3538952 | tf_op jit(solution)/shard_map/ppermute | solution.py:120
  90.5 13.4 %collective-permute-start.14 = (bf16[6,48,1536]{2,1,0:T(8,128)(2,1)}, bf16[6,48,1536]{2,1,0:T(8,128)(2,1)}, u32[]{:S(2)}, u32[]{:S(2)}) collective-permute-start(bf16[6,48,1536]{2,1,0:T(8,128)(2,1)} %collective-permute-done.12.p1), channel_id=1, source_target_pairs={{0,4},{1,3},{2,6},{3,1},{4,0},{5,7},{6,2},{7,5},{8,12},{9,11},{10,... | collective-permute-start | bytes 2654216 | tf_op jit(solution)/shard_map/ppermute | solution.py:514
  95.5 2.2 collective-permute-start.16
  125.5 4.1 %collective-permute-start.19 = (bf16[768,768]{1,0:T(8,128)(2,1)}, bf16[768,768]{1,0:T(8,128)(2,1)}, u32[]{:S(2)}, u32[]{:S(2)}) collective-permute-start(bf16[768,768]{1,0:T(8,128)(2,1)} %get-tuple-element.175), channel_id=1, source_target_pairs={{0,1},{1,0},{2,3},{3,2},{4,5},{5,4},{6,7},{7,6},{8,9},{9,8},{10,11... | collective-permute-start | bytes 3538952 | tf_op jit(solution)/shard_map/ppermute | solution.py:120
  125.6 16.6 %collective-permute-start.17 = (bf16[384,1536]{1,0:T(8,128)(2,1)}, bf16[384,1536]{1,0:T(8,128)(2,1)}, u32[]{:S(2)}, u32[]{:S(2)}) collective-permute-start(bf16[384,1536]{1,0:T(8,128)(2,1)} %get-tuple-element.172), channel_id=1, source_target_pairs={{0,4},{1,3},{2,6},{3,1},{4,0},{5,7},{6,2},{7,5},{8,12},{9,11},{10,... | collective-permute-start | bytes 3538952 | tf_op jit(solution)/shard_map/ppermute | solution.py:514
  127.0 15.2 %collective-permute-start.18 = (bf16[768,768]{1,0:T(8,128)(2,1)}, bf16[768,768]{1,0:T(8,128)(2,1)}, u32[]{:S(2)}, u32[]{:S(2)}) collective-permute-start(bf16[768,768]{1,0:T(8,128)(2,1)} %get-tuple-element.173.own_any), channel_id=1, source_target_pairs={{0,1},{1,0},{2,3},{3,2},{4,5},{5,4},{6,7},{7,6},{8,9},{9,8},{10,11... | collective-permute-start | bytes 3538952 | tf_op jit(solution)/shard_map/ppermute | solution.py:120
  128.0 14.1 %copy-start.4 = (bf16[384,1536]{1,0:T(8,128)(2,1)S(1)}, bf16[384,1536]{1,0:T(8,128)(2,1)}, u32[]{:S(2)}) copy-start(bf16[384,1536]{1,0:T(8,128)(2,1)} %get-tuple-element.171.kept_ref.refs_0_) | copy-start | bytes 3538948
  128.0 42.3 %collective-permute-start.21 = (bf16[384,1536]{1,0:T(8,128)(2,1)}, bf16[384,1536]{1,0:T(8,128)(2,1)}, u32[]{:S(2)}, u32[]{:S(2)}) collective-permute-start(bf16[384,1536]{1,0:T(8,128)(2,1)} %get-tuple-element.177), channel_id=1, source_target_pairs={{0,4},{1,3},{2,6},{3,1},{4,0},{5,7},{6,2},{7,5},{8,12},{9,11},{10,... | collective-permute-start | bytes 3538952 | tf_op jit(solution)/shard_map/ppermute | solution.py:514
  143.4 27.0 %collective-permute-start.20 = (bf16[192,1536]{1,0:T(8,128)(2,1)S(1)}, bf16[192,1536]{1,0:T(8,128)(2,1)}, u32[]{:S(2)}, u32[]{:S(2)}) collective-permute-start(bf16[192,1536]{1,0:T(8,128)(2,1)S(1)} %add_convert_fusion.2), channel_id=1, source_target_pairs={{0,2},{1,5},{2,0},{3,7},{4,6},{5,1},{6,4},{7,3},{8,10},{9,13},{10,... | collective-permute-start | bytes 1769480 | tf_op jit(solution)/shard_map/ppermute | solution.py:514
  144.8 25.8 %all-to-all-start.1 = ((bf16[16,72,384]{2,1,0:T(8,128)(2,1)}), bf16[16,72,384]{2,1,0:T(8,128)(2,1)}, u32[]{:S(2)}, u32[]{:S(2)}) async-start(bf16[16,72,384]{2,1,0:T(8,128)(2,1)} %bitcast.73), calls=%async_computation.1 | async-start | bytes 1769472 | tf_op jit(solution)/shard_map/all_to_all | solution.py:1264
  170.6 23.4 %collective-permute-start.22 = (bf16[400,1536]{1,0:T(8,128)(2,1)}, bf16[400,1536]{1,0:T(8,128)(2,1)}, u32[]{:S(2)}, u32[]{:S(2)}) collective-permute-start(bf16[400,1536]{1,0:T(8,128)(2,1)} %get-tuple-element.192), channel_id=1, source_target_pairs={{0,4},{1,3},{2,6},{3,1},{4,0},{5,7},{6,2},{7,5},{8,12},{9,11},{10,... | collective-permute-start | bytes 3686408 | tf_op jit(solution)/shard_map/ppermute | solution.py:514
  173.7 8.1 %copy-start.28 = (bf16[384]{0:T(512)(128)(2,1)S(1)}, bf16[384]{0:T(512)(128)(2,1)}, u32[]{:S(2)}) copy-start(bf16[384]{0:T(512)(128)(2,1)} %param.26) | copy-start | bytes 2308
  173.7 18.3 %collective-permute-start.26 = (bf16[192,1536]{1,0:T(8,128)(2,1)S(1)}, bf16[192,1536]{1,0:T(8,128)(2,1)}, u32[]{:S(2)}, u32[]{:S(2)}) collective-permute-start(bf16[192,1536]{1,0:T(8,128)(2,1)S(1)} %add_convert_fusion.1), channel_id=1, source_target_pairs={{0,2},{1,5},{2,0},{3,7},{4,6},{5,1},{6,4},{7,3},{8,10},{9,13},{10,... | collective-permute-start | bytes 1769480 | tf_op jit(solution)/shard_map/ppermute | solution.py:514
  177.5 8.9 %collective-permute-start.23 = (bf16[48,1536]{1,0:T(8,128)(2,1)}, bf16[48,1536]{1,0:T(8,128)(2,1)S(1)}, u32[]{:S(2)}, u32[]{:S(2)}) collective-permute-start(bf16[48,1536]{1,0:T(8,128)(2,1)} %get-tuple-element.194), channel_id=1, source_target_pairs={{0,24},{2,26},{4,28},{6,30},{8,16},{10,18},{12,20},{14,22},{16,8},... | collective-permute-start | bytes 442376 | tf_op jit(solution)/shard_map/ppermute | solution.py:116
  180.7 7.9 %collective-permute-start.24 = (bf16[48,1536]{1,0:T(8,128)(2,1)}, bf16[48,1536]{1,0:T(8,128)(2,1)S(1)}, u32[]{:S(2)}, u32[]{:S(2)}) collective-permute-start(bf16[48,1536]{1,0:T(8,128)(2,1)} %get-tuple-element.195), channel_id=1, source_target_pairs={{0,8},{2,10},{4,12},{6,14},{8,0},{10,2},{12,4},{14,6},{16,24},{18,... | collective-permute-start | bytes 442376 | tf_op jit(solution)/shard_map/ppermute | solution.py:116
  180.7 13.2 %copy-start.3 = (bf16[400,1536]{1,0:T(8,128)(2,1)S(1)}, bf16[400,1536]{1,0:T(8,128)(2,1)}, u32[]{:S(2)}) copy-start(bf16[400,1536]{1,0:T(8,128)(2,1)} %get-tuple-element.202.kept_ref.refs_0_) | copy-start | bytes 3686404
  180.7 11.2 %collective-permute-start.25 = (bf16[48,1536]{1,0:T(8,128)(2,1)}, bf16[48,1536]{1,0:T(8,128)(2,1)S(1)}, u32[]{:S(2)}, u32[]{:S(2)}) collective-permute-start(bf16[48,1536]{1,0:T(8,128)(2,1)} %get-tuple-element.196), channel_id=1, source_target_pairs={{0,16},{2,18},{4,20},{6,22},{8,24},{10,26},{12,28},{14,30},{16,0},... | collective-permute-start | bytes 442376 | tf_op jit(solution)/shard_map/ppermute | solution.py:116
  186.4 12.9 %copy-start.23 = (bf16[48,1536]{1,0:T(8,128)(2,1)}, bf16[48,1536]{1,0:T(8,128)(2,1)S(1)}, u32[]{:S(2)}) copy-start(bf16[48,1536]{1,0:T(8,128)(2,1)S(1)} %collective-permute-done.23.refs_3_) | copy-start | bytes 442372
  188.7 10.6 %copy-start.25 = (bf16[48,1536]{1,0:T(8,128)(2,1)}, bf16[48,1536]{1,0:T(8,128)(2,1)S(1)}, u32[]{:S(2)}) copy-start(bf16[48,1536]{1,0:T(8,128)(2,1)S(1)} %collective-permute-done.24.refs_4_) | copy-start | bytes 442372
  192.0 7.3 %copy-start.27 = (bf16[48,1536]{1,0:T(8,128)(2,1)}, bf16[48,1536]{1,0:T(8,128)(2,1)S(1)}, u32[]{:S(2)}) copy-start(bf16[48,1536]{1,0:T(8,128)(2,1)S(1)} %collective-permute-done.25.refs_5_) | copy-start | bytes 442372
  194.0 22.1 %collective-permute-start.31 = (bf16[768,768]{1,0:T(8,128)(2,1)}, bf16[768,768]{1,0:T(8,128)(2,1)S(1)}, u32[]{:S(2)}, u32[]{:S(2)}) collective-permute-start(bf16[768,768]{1,0:T(8,128)(2,1)} %get-tuple-element.208.own_ref), channel_id=1, source_target_pairs={{0,1},{1,0},{2,3},{3,2},{4,5},{5,4},{6,7},{7,6},{8,9},{9,8},{10,11... | collective-permute-start | bytes 3538952 | tf_op jit(solution)/shard_map/ppermute | solution.py:120
  195.2 4.0 %copy-start.2 = (bf16[208,1536]{1,0:T(8,128)(2,1)}, bf16[208,1536]{1,0:T(8,128)(2,1)S(1)}, u32[]{:S(2)}) copy-start(bf16[208,1536]{1,0:T(8,128)(2,1)S(1)} %add_convert_fusion.refs_0_) | copy-start | bytes 1916932
  195.2 20.9 %collective-permute-start.27 = (bf16[208,1536]{1,0:T(8,128)(2,1)S(1)}, bf16[208,1536]{1,0:T(8,128)(2,1)S(1)}, u32[]{:S(2)}, u32[]{:S(2)}) collective-permute-start(bf16[208,1536]{1,0:T(8,128)(2,1)S(1)} %add_convert_fusion.refs_0_), channel_id=1, source_target_pairs={{0,2},{1,5},{2,0},{3,7},{4,6},{5,1},{6,4},{7,3},{8,10},{9,13},{10,... | collective-permute-start | bytes 1916936 | tf_op jit(solution)/shard_map/ppermute | solution.py:514
  199.3 8.8 %collective-permute-start.28 = (bf16[48,1536]{1,0:T(8,128)(2,1)}, bf16[48,1536]{1,0:T(8,128)(2,1)S(1)}, u32[]{:S(2)}, u32[]{:S(2)}) collective-permute-start(bf16[48,1536]{1,0:T(8,128)(2,1)} %get-tuple-element.205), channel_id=1, source_target_pairs={{0,24},{2,26},{4,28},{6,30},{8,16},{10,18},{12,20},{14,22},{16,8},... | collective-permute-start | bytes 442376 | tf_op jit(solution)/shard_map/ppermute | solution.py:116
  201.9 9.6 %collective-permute-start.29 = (bf16[48,1536]{1,0:T(8,128)(2,1)}, bf16[48,1536]{1,0:T(8,128)(2,1)S(1)}, u32[]{:S(2)}, u32[]{:S(2)}) collective-permute-start(bf16[48,1536]{1,0:T(8,128)(2,1)} %get-tuple-element.206), channel_id=1, source_target_pairs={{0,8},{2,10},{4,12},{6,14},{8,0},{10,2},{12,4},{14,6},{16,24},{18,... | collective-permute-start | bytes 442376 | tf_op jit(solution)/shard_map/ppermute | solution.py:116
  201.9 14.2 %collective-permute-start.30 = (bf16[48,1536]{1,0:T(8,128)(2,1)}, bf16[48,1536]{1,0:T(8,128)(2,1)S(1)}, u32[]{:S(2)}, u32[]{:S(2)}) collective-permute-start(bf16[48,1536]{1,0:T(8,128)(2,1)} %get-tuple-element.207), channel_id=1, source_target_pairs={{0,16},{2,18},{4,20},{6,22},{8,24},{10,26},{12,28},{14,30},{16,0},... | collective-permute-start | bytes 442376 | tf_op jit(solution)/shard_map/ppermute | solution.py:116
  208.1 20.4 %copy-start.22 = (bf16[48,1536]{1,0:T(8,128)(2,1)}, bf16[48,1536]{1,0:T(8,128)(2,1)S(1)}, u32[]{:S(2)}) copy-start(bf16[48,1536]{1,0:T(8,128)(2,1)S(1)} %collective-permute-done.28.refs_3_) | copy-start | bytes 442372
  211.5 16.9 %copy-start.24 = (bf16[48,1536]{1,0:T(8,128)(2,1)}, bf16[48,1536]{1,0:T(8,128)(2,1)S(1)}, u32[]{:S(2)}) copy-start(bf16[48,1536]{1,0:T(8,128)(2,1)S(1)} %collective-permute-done.29.refs_4_) | copy-start | bytes 442372
  216.1 12.3 %copy-start.26 = (bf16[48,1536]{1,0:T(8,128)(2,1)}, bf16[48,1536]{1,0:T(8,128)(2,1)S(1)}, u32[]{:S(2)}) copy-start(bf16[48,1536]{1,0:T(8,128)(2,1)S(1)} %collective-permute-done.30.refs_5_) | copy-start | bytes 442372
  216.1 3.2 %copy-start.17 = (bf16[768,768]{1,0:T(8,128)(2,1)}, bf16[768,768]{1,0:T(8,128)(2,1)S(1)}, u32[]{:S(2)}) copy-start(bf16[768,768]{1,0:T(8,128)(2,1)S(1)} %collective-permute-done.31.other_ref) | copy-start | bytes 3538948
  219.3 11.9 %collective-permute-start.32 = (bf16[64,1536]{1,0:T(8,128)(2,1)}, bf16[64,1536]{1,0:T(8,128)(2,1)S(1)}, u32[]{:S(2)}, u32[]{:S(2)}) collective-permute-start(bf16[64,1536]{1,0:T(8,128)(2,1)} %get-tuple-element.229), channel_id=1, source_target_pairs={{0,24},{2,26},{4,28},{6,30},{8,16},{10,18},{12,20},{14,22},{16,8},... | collective-permute-start | bytes 589832 | tf_op jit(solution)/shard_map/ppermute | solution.py:116
  221.5 14.1 %collective-permute-start.33 = (bf16[64,1536]{1,0:T(8,128)(2,1)}, bf16[64,1536]{1,0:T(8,128)(2,1)S(1)}, u32[]{:S(2)}, u32[]{:S(2)}) collective-permute-start(bf16[64,1536]{1,0:T(8,128)(2,1)} %get-tuple-element.218), channel_id=1, source_target_pairs={{0,8},{2,10},{4,12},{6,14},{8,0},{10,2},{12,4},{14,6},{16,24},{18,... | collective-permute-start | bytes 589832 | tf_op jit(solution)/shard_map/ppermute | solution.py:116
  221.5 16.4 %collective-permute-start.34 = (bf16[64,1536]{1,0:T(8,128)(2,1)}, bf16[64,1536]{1,0:T(8,128)(2,1)S(1)}, u32[]{:S(2)}, u32[]{:S(2)}) collective-permute-start(bf16[64,1536]{1,0:T(8,128)(2,1)} %get-tuple-element.219), channel_id=1, source_target_pairs={{0,16},{2,18},{4,20},{6,22},{8,24},{10,26},{12,28},{14,30},{16,0},... | collective-permute-start | bytes 589832 | tf_op jit(solution)/shard_map/ppermute | solution.py:116
  228.4 10.6 %copy-start.13 = (f32[1,6,384]{2,0,1:T(1,128)S(1)}, f32[1,6,384]{2,0,1:T(1,128)}, u32[]{:S(2)}) copy-start(f32[1,6,384]{2,0,1:T(1,128)} %param.46) | copy-start | bytes 27652
  228.4 10.6 %copy-start.14 = (f32[1,6,384]{2,0,1:T(1,128)S(1)}, f32[1,6,384]{2,0,1:T(1,128)}, u32[]{:S(2)}) copy-start(f32[1,6,384]{2,0,1:T(1,128)} %param.47) | copy-start | bytes 27652
  231.2 8.5 %copy-start.10 = (bf16[64,1536]{1,0:T(8,128)(2,1)}, bf16[64,1536]{1,0:T(8,128)(2,1)S(1)}, u32[]{:S(2)}) copy-start(bf16[64,1536]{1,0:T(8,128)(2,1)S(1)} %collective-permute-done.32.refs_3_) | copy-start | bytes 589828
  235.6 4.1 %copy-start.11 = (bf16[64,1536]{1,0:T(8,128)(2,1)}, bf16[64,1536]{1,0:T(8,128)(2,1)S(1)}, u32[]{:S(2)}) copy-start(bf16[64,1536]{1,0:T(8,128)(2,1)S(1)} %collective-permute-done.33.refs_4_) | copy-start | bytes 589828
  238.9 4.2 %collective-permute-start.35 = (f32[3,1536]{1,0:T(4,128)S(1)}, f32[3,1536]{1,0:T(4,128)S(1)}, u32[]{:S(2)}, u32[]{:S(2)}) collective-permute-start(f32[3,1536]{1,0:T(4,128)S(1)} %slice.85), channel_id=1, source_target_pairs={{0,1},{1,0},{2,3},{3,2},{4,5},{5,4},{6,7},{7,6},{8,9},{9,8},{10,11... | collective-permute-start | bytes 55304 | tf_op jit(solution)/shard_map/ppermute | solution.py:120
  239.7 3.4 %copy-start.7 = (f32[6,768]{1,0:T(8,128)S(1)}, f32[6,768]{1,0:T(8,128)}, u32[]{:S(2)}) copy-start(f32[6,768]{1,0:T(8,128)} %rep_ref.7) | copy-start | bytes 55300
  239.7 3.4 %copy-start.8 = (f32[6,768]{1,0:T(8,128)S(1)}, f32[6,768]{1,0:T(8,128)}, u32[]{:S(2)}) copy-start(f32[6,768]{1,0:T(8,128)} %param.43) | copy-start | bytes 55300
  239.7 3.4 %copy-start.9 = (f32[6,768]{1,0:T(8,128)S(1)}, f32[6,768]{1,0:T(8,128)}, u32[]{:S(2)}) copy-start(f32[6,768]{1,0:T(8,128)} %param.44) | copy-start | bytes 55300
  239.7 4.1 %copy-start.1 = (bf16[32,34,1,384]{3,0,2,1:T(8,128)(2,1)S(1)}, bf16[32,34,1,384]{3,0,2,1:T(8,128)(2,1)}, u32[]{:S(2)}) copy-start(bf16[32,34,1,384]{3,0,2,1:T(8,128)(2,1)} %param.25) | copy-start | bytes 2506756
  (3 other events, 4.0 us)

commit v2 on v1

--- a/solution.py
+++ b/solution.py
@@ -1366,8 +1366,8 @@
         [(0, side * 6 + j, 0, side * UNIT_ROWS * 6 + j, 6) for side in range(2) for j in range(6)],
     )
     back_one_other = swap_cores(back_one)
-    two_a_sent, two_a, arrivals_b, back_one_other, *fc2_new = together(
-        two_a_sent, two_a, arrivals_b, back_one_other, *fc2_new
+    two_a_sent, two_a, arrivals_b[0], back_one_other = together(
+        two_a_sent, two_a, arrivals_b[0], back_one_other
     )
 
     messages = last_messages(kept_a, one_a, two_a, two_a_sent)

time: 245 us -> 240 us (0.980)
  waiting for transfers between devices: 67.4 us -> 61.3 us
    ppermute x15, waiting for transfers between devices: 40.7 us -> 34.6 us  [hop(): lax.ppermute(array, 'dp', [(i, i ^ distance) for i in range(axis_count)])]
  transfers between devices with their start and end apart: 38 -> 38, of which waited for: 21 -> 19; matrix products, arithmetic and copies ran while one was open for 14% -> 14% of each run, Pallas kernels for 23% -> 24%
where the time goes in v2:
time: 240 us; the launch traced here: 239 us
  Pallas kernels  85.7 us (36%)
  waiting for transfers between devices  61.3 us (26%)
  starting transfers between devices  54 us (22%)
  other arithmetic  14.1 us (6%)
  matrix products  14.1 us (6%)
  local copies, waits for them, and re-layouts  8.56 us (4%)
    ppermute x15, waiting for transfers between devices, hop(): lax.ppermute(array, 'dp', [(i, i ^ distance) for i in range(axis_count)])  34.6 us
    ppermute x15, waiting for transfers between devices, hop_by_core(): return lax.ppermute(array, ('dp', 'mp'), pairs)  24.1 us
    ppermute x15, starting transfers between devices, hop(): lax.ppermute(array, 'dp', [(i, i ^ distance) for i in range(axis_count)])  23.1 us
    pallas_call x1, Pallas kernels, mlp_all(): pl.pallas_call(body, in_specs=[IN_SMEM, IN_VMEM, IN_VMEM] + [ANY] * 12, o...  21.7 us
    ppermute x15, starting transfers between devices, hop_by_core(): return lax.ppermute(array, ('dp', 'mp'), pairs)  21.2 us
    pallas_call x1, Pallas kernels, attention_back(): pl.pallas_call(body, in_specs=[IN_SMEM] + [IN_VMEM] * 4 + [ANY] * 11, out...  20.7 us
    pallas_call x1, Pallas kernels, attention_forward(): pl.pallas_call(body, grid=(pairs_of_heads,), in_specs=[IN_SMEM, fixed(cou...  16.8 us
    all_to_all x2, starting transfers between devices, exchanged(): array = lax.all_to_all(array, 'dp', split_axis=0, concat_axis=0, tiled=True)  9.05 us
  transfers between devices with their start and end apart: 38, of which 19 were waited for; matrix products, arithmetic and copies ran while one was open for 14% of the time, Pallas kernels for 24%

profile of v2, /device:TPU:0, one launch (start us, length us, event | category | flops | bytes accessed | tf_op | source)
XLA Modules:
  0.0 238.9 jit_solution(16909094383955609395)
XLA Ops:
  0.7 2.2 pack_units.1
  2.9 2.9 %collective-permute-start.3 = (bf16[3,48,1536]{2,1,0:T(8,128)(2,1)}, bf16[3,48,1536]{2,1,0:T(8,128)(2,1)}, u32[]{:S(2)}, u32[]{:S(2)}) collective-permute-start(bf16[3,48,1536]{2,1,0:T(8,128)(2,1)} %get-tuple-element.129.o0), channel_id=1, source_target_pairs={{0,2},{1,5},{2,0},{3,7},{4,6},{5,1},{6,4},{7,3},{8,10},{9,13},{10,... | collective-permute-start | bytes 1327112 | tf_op jit(solution)/shard_map/ppermute | solution.py:514
  5.9 1.5 collective-permute-start.4
  7.4 3.6 %collective-permute-start = (bf16[1,48,1536]{2,1,0:T(8,128)(2,1)}, bf16[1,48,1536]{2,1,0:T(8,128)(2,1)}, u32[]{:S(2)}, u32[]{:S(2)}) collective-permute-start(bf16[1,48,1536]{2,1,0:T(8,128)(2,1)} %get-tuple-element.128), channel_id=1, source_target_pairs={{0,24},{2,26},{4,28},{6,30},{8,16},{10,18},{12,20},{14,22},{16,8},... | collective-permute-start | bytes 442376 | tf_op jit(solution)/shard_map/ppermute | solution.py:116
  16.1 1.8 fusion.1
  17.9 1.5 gather_fusion
  21.0 2.3 collective-permute-done.2.refs_2_
  23.2 1.9 join_chunks.2.p0
  26.1 1.5 collective-permute-start.7
  27.7 2.6 %collective-permute-start.8 = (bf16[2,48,1536]{2,1,0:T(8,128)(2,1)}, bf16[2,48,1536]{2,1,0:T(8,128)(2,1)S(1)}, u32[]{:S(2)}, u32[]{:S(2)}) collective-permute-start(bf16[2,48,1536]{2,1,0:T(8,128)(2,1)} %get-tuple-element.140), channel_id=1, source_target_pairs={{0,24},{2,26},{4,28},{6,30},{8,16},{10,18},{12,20},{14,22},{16,8},... | collective-permute-start | bytes 884744 | tf_op jit(solution)/shard_map/ppermute | solution.py:116
  30.3 2.6 %convolution_convert_fusion.1 = bf16[1152,384]{1,0:T(8,128)(2,1)} fusion(bf16[1152,1088]{1,0:T(8,128)(2,1)S(1)} %fusion, bf16[1088,384]{1,0:T(8,128)(2,1)S(1)} %bitcast.71), kind=kOutput, calls=%fused_computation.7 | convolution fusion | flops 963035136 | bytes 4227072 | tf_op jit(solution)/shard_map/dot_general | solution.py:34
  33.7 3.2 %collective-permute-done.8.refs_0_ = bf16[2,48,1536]{2,1,0:T(8,128)(2,1)S(1)} collective-permute-done((bf16[2,48,1536]{2,1,0:T(8,128)(2,1)}, bf16[2,48,1536]{2,1,0:T(8,128)(2,1)S(1)}, u32[]{:S(2)}, u32[]{:S(2)}) %collective-permute-start.8) | collective-permute-done | bytes 294944 | tf_op jit(solution)/shard_map/ppermute | solution.py:116
  36.9 1.6 collective-permute-done.5.p1
  38.5 2.8 %collective-permute-done.7.o3 = bf16[3,48,1536]{2,1,0:T(8,128)(2,1)} collective-permute-done((bf16[3,48,1536]{2,1,0:T(8,128)(2,1)}, bf16[3,48,1536]{2,1,0:T(8,128)(2,1)}, u32[]{:S(2)}, u32[]{:S(2)}) %collective-permute-start.7) | collective-permute-done | bytes 442400 | tf_op jit(solution)/shard_map/ppermute | solution.py:514
  42.2 2.5 %collective-permute-start.11 = (bf16[2,48,1536]{2,1,0:T(8,128)(2,1)}, bf16[2,48,1536]{2,1,0:T(8,128)(2,1)}, u32[]{:S(2)}, u32[]{:S(2)}) collective-permute-start(bf16[2,48,1536]{2,1,0:T(8,128)(2,1)} %get-tuple-element.140), channel_id=1, source_target_pairs={{0,16},{2,18},{4,20},{6,22},{8,24},{10,26},{12,28},{14,30},{16,0},... | collective-permute-start | bytes 884744 | tf_op jit(solution)/shard_map/ppermute | solution.py:116
  45.9 10.9 %collective-permute-done.10.refs_1_ = bf16[2,48,1536]{2,1,0:T(8,128)(2,1)S(1)} collective-permute-done((bf16[2,48,1536]{2,1,0:T(8,128)(2,1)}, bf16[2,48,1536]{2,1,0:T(8,128)(2,1)S(1)}, u32[]{:S(2)}, u32[]{:S(2)}) %collective-permute-start.10) | collective-permute-done | bytes 294944 | tf_op jit(solution)/shard_map/ppermute | solution.py:116
  56.9 1.3 collective-permute-done.11.refs_2_
  58.2 2.3 join_chunks.3.p0
  60.5 1.5 collective-permute-start.12
  62.0 1.5 collective-permute-start.13
  63.5 4.3 %all-to-all-start = ((bf16[16,72,384]{2,1,0:T(8,128)(2,1)}), bf16[16,72,384]{2,1,0:T(8,128)(2,1)}, u32[]{:S(2)}, u32[]{:S(2)}) async-start(bf16[16,72,384]{2,1,0:T(8,128)(2,1)} %bitcast.72), calls=%async_computation | async-start | bytes 1769472 | tf_op jit(solution)/shard_map/all_to_all | solution.py:1264
  67.8 16.8 %attention_forward.1 = (bf16[768,768]{1,0:T(8,128)(2,1)}, bf16[768,1152]{1,0:T(8,128)(2,1)}, bf16[6,768,768]{2,1,0:T(8,128)(2,1)}, bf16[768,384]{1,0:T(8,128)(2,...) custom-call(s32[4]{0:T(128)} %pad_add_fusion.words_ref, ...), custom_call_target="tpu_custom_call" | custom-call | flops 20700000256 | bytes 1000000 | tf_op jit(solution)/shard_map/attention_forward/pallas_call | solution.py:770
  84.7 5.8 %collective-permute-done.12.p1 = bf16[6,48,1536]{2,1,0:T(8,128)(2,1)} collective-permute-done((bf16[6,48,1536]{2,1,0:T(8,128)(2,1)}, bf16[6,48,1536]{2,1,0:T(8,128)(2,1)}, u32[]{:S(2)}, u32[]{:S(2)}) %collective-permute-start.12) | collective-permute-done | bytes 884768 | tf_op jit(solution)/shard_map/ppermute | solution.py:514
  90.5 1.3 collective-permute-start.14
  91.8 0.9 all-to-all-done
  92.7 2.8 %convolution_convert_fusion.2 = bf16[768,384]{1,0:T(8,128)(2,1)S(1)} fusion(bf16[768,1152]{1,0:T(8,128)(2,1)} %fusion.1, bf16[1152,384]{1,0:T(8,128)(2,1)} %bitcast.16), kind=kOutput, calls=%fused_computation.9 | convolution fusion | flops 679772160 | bytes 3244032 | tf_op jit(solution)/shard_map/dot_general | solution.py:34
  96.2 1.5 collective-permute-done.16
  97.7 2.6 %maximum_select_fusion.grad_any = bf16[768,768]{1,0:T(8,128)(2,1)} fusion(bf16[768,384]{1,0:T(8,128)(2,1)} %collective-permute-done.16, bf16[768,384]{1,0:T(8,128)(2,1)S(1)} %convolution_convert_fusion.2, pred[]{:T(512)S(6)} %eq.46), kind=kLoop, calls=%fused_computation.13 | loop fusion | flops 5308416 | bytes 2359297 | tf_op jit(solution)/shard_map/jit(_where)/select_n | solution.py:1310
  100.3 3.5 %collective-permute-done.14.p3 = bf16[6,48,1536]{2,1,0:T(8,128)(2,1)} collective-permute-done((bf16[6,48,1536]{2,1,0:T(8,128)(2,1)}, bf16[6,48,1536]{2,1,0:T(8,128)(2,1)}, u32[]{:S(2)}, u32[]{:S(2)}) %collective-permute-start.14) | collective-permute-done | bytes 884768 | tf_op jit(solution)/shard_map/ppermute | solution.py:514
  103.8 21.7 %mlp_all.1 = (f32[1,1536]{1,0:T(1,128)}, f32[1,768]{1,0:T(1,128)}, f32[768,768]{1,0:T(8,128)}, bf16[768,768]{1,0:T(8,128)(2,1)}, bf16[768,768]{1,0:T(8,128)(2,1)...) custom-call(s32[4]{0:T(128)} %pad_add_fusion.words_ref, ...), custom_call_target="tpu_custom_call" | custom-call | flops 20700000256 | bytes 1000000 | tf_op jit(solution)/shard_map/mlp_all/pallas_call | solution.py:904
  125.6 1.4 collective-permute-start.17
  128.0 1.6 collective-permute-start.21
  129.6 4.2 %convolution_convert_fusion = bf16[1152,384]{1,0:T(8,128)(2,1)} fusion(bf16[768,1152]{1,0:T(8,128)(2,1)} %fusion.1, f32[768,768]{1,0:T(8,128)} %get-tuple-element.169.middle_any, s32[]{:T(128)S(6)} %select_n.70, f32[384]{0:T(512)S(1)} %dynamic-slice, bf16[768,768]{1,0:T(8,128)(2,1)} %collective-permute-done.19, bf16[768,768]{1,0:T(8,128)(2,1)} %get-tuple-element.170), kind=kOutput, calls=%fused_computation.6 | convolution fusion | flops 681689088 | bytes 5015044 | tf_op jit(solution)/shard_map/dot_general | solution.py:44
  133.8 8.4 %collective-permute-done.17.one_ref.refs_1_ = bf16[384,1536]{1,0:T(8,128)(2,1)} collective-permute-done((bf16[384,1536]{1,0:T(8,128)(2,1)}, bf16[384,1536]{1,0:T(8,128)(2,1)}, u32[]{:S(2)}, u32[]{:S(2)}) %collective-permute-start.17) | collective-permute-done | bytes 1179680 | tf_op jit(solution)/shard_map/ppermute | solution.py:514
  142.2 1.2 add_convert_fusion.2
  143.4 1.5 collective-permute-start.20
  144.8 4.8 %all-to-all-start.1 = ((bf16[16,72,384]{2,1,0:T(8,128)(2,1)}), bf16[16,72,384]{2,1,0:T(8,128)(2,1)}, u32[]{:S(2)}, u32[]{:S(2)}) async-start(bf16[16,72,384]{2,1,0:T(8,128)(2,1)} %bitcast.73), calls=%async_computation.1 | async-start | bytes 1769472 | tf_op jit(solution)/shard_map/all_to_all | solution.py:1264
  149.6 20.7 %attention_back.1 = (f32[768,768]{1,0:T(8,128)}, bf16[768,768]{1,0:T(8,128)(2,1)}, bf16[400,1536]{1,0:T(8,128)(2,1)}, bf16[400,1536]{1,0:T(8,128)(2,1)}) custom-call(s32[4]{0:T(128)} %pad_add_fusion.words_ref, f32[6,768]{1,0:T(8,128)} %rep_ref.7, f32[1,1536]{1,0:T(1,128)} %get-tuple-element.173.hidden_sum_ref, f32[1,768]{1,0:T(1,128)} %get-tuple-element.174.grad_sum_ref, ...), custom_call_target="tpu_custom_call" | custom-call | flops 25300000768 | bytes 1000000 | tf_op jit(solution)/shard_map/attention_back/pallas_call | solution.py:1077
  170.6 1.7 collective-permute-start.22
  172.3 1.4 add_convert_fusion.1
  173.7 1.5 collective-permute-start.26
  175.2 2.2 last_messages.3
  177.5 3.3 %collective-permute-start.23 = (bf16[48,1536]{1,0:T(8,128)(2,1)}, bf16[48,1536]{1,0:T(8,128)(2,1)S(1)}, u32[]{:S(2)}, u32[]{:S(2)}) collective-permute-start(bf16[48,1536]{1,0:T(8,128)(2,1)} %get-tuple-element.189), channel_id=1, source_target_pairs={{0,24},{2,26},{4,28},{6,30},{8,16},{10,18},{12,20},{14,22},{16,8},... | collective-permute-start | bytes 442376 | tf_op jit(solution)/shard_map/ppermute | solution.py:116
  180.7 1.1 collective-permute-start.25
  181.9 3.7 %select_convert_fusion = bf16[1088,384]{1,0:T(8,128)(2,1)} fusion(bf16[384]{0:T(512)(128)(2,1)S(1)} %copy-done.28, pred[1088]{0:T(1024)(128)(4,1)S(1)} %reshape.320, bf16[1152,1088]{1,0:T(8,128)(2,1)S(1)} %fusion, bf16[1152,384]{1,0:T(8,128)(2,1)} %bitcast.18), kind=kOutput, calls=%fused_computation.8 | convolution fusion | flops 963010560 | bytes 4228928 | tf_op jit(solution)/shard_map/dot_general | solution.py:44
  186.4 2.3 collective-permute-done.24.refs_4_
  188.7 3.3 %collective-permute-done.25.refs_5_ = bf16[48,1536]{1,0:T(8,128)(2,1)S(1)} collective-permute-done((bf16[48,1536]{1,0:T(8,128)(2,1)}, bf16[48,1536]{1,0:T(8,128)(2,1)S(1)}, u32[]{:S(2)}, u32[]{:S(2)}) %collective-permute-start.25) | collective-permute-done | bytes 147488 | tf_op jit(solution)/shard_map/ppermute | solution.py:116
  192.0 2.0 collective-permute-done.22.one_ref.refs_1_
  194.0 1.2 add_convert_fusion.refs_0_
  195.2 1.8 collective-permute-start.27
  197.0 2.2 last_messages.4
  199.3 2.6 %collective-permute-start.28 = (bf16[48,1536]{1,0:T(8,128)(2,1)}, bf16[48,1536]{1,0:T(8,128)(2,1)S(1)}, u32[]{:S(2)}, u32[]{:S(2)}) collective-permute-start(bf16[48,1536]{1,0:T(8,128)(2,1)} %get-tuple-element.200), channel_id=1, source_target_pairs={{0,24},{2,26},{4,28},{6,30},{8,16},{10,18},{12,20},{14,22},{16,8},... | collective-permute-start | bytes 442376 | tf_op jit(solution)/shard_map/ppermute | solution.py:116
  201.9 1.8 collective-permute-start.34
  203.7 2.7 %adam_unit.5 = (f32[576,128]{1,0:T(8,128)}, f32[576,128]{1,0:T(8,128)}, f32[576,128]{1,0:T(8,128)}) custom-call(bf16[384,1536]{1,0:T(8,128)(2,1)} %get-tuple-element.166.kept_ref.refs_0_, bf16[384,1536]{1,0:T(8,128)(2,1)} %collective-permute-done.17.one_ref.refs_1_, bf16[192,1536]{1,0:T(8,128)(2,1)} %collective-permute-done.20.two_ref.refs_2_, ...), custom_call_target="tpu_custom_call" | custom-call | flops 2875000064 | bytes 1000000 | tf_op jit(solution)/shard_map/adam_unit/pallas_call | solution.py:1156
  206.4 1.6 collective-permute-done.28.refs_3_
  208.1 0.9 copy-done.18
  209.0 2.7 %last_messages.5 = (bf16[64,1536]{1,0:T(8,128)(2,1)}, bf16[64,1536]{1,0:T(8,128)(2,1)}, bf16[64,1536]{1,0:T(8,128)(2,1)}) custom-call(bf16[400,1536]{1,0:T(8,128)(2,1)} %get-tuple-element.197.kept_ref.refs_0_, bf16[400,1536]{1,0:T(8,128)(2,1)} %collective-permute-done.22.one_ref.refs_1_, bf16[208,1536]{1,0:T(8,128)(2,1)} %copy-done.18, ...), custom_call_target="tpu_custom_call" | custom-call | flops 1724999936 | bytes 1000000 | tf_op jit(solution)/shard_map/last_messages/pallas_call | solution.py:602
  211.7 2.7 %collective-permute-start.30 = (bf16[64,1536]{1,0:T(8,128)(2,1)}, bf16[64,1536]{1,0:T(8,128)(2,1)S(1)}, u32[]{:S(2)}, u32[]{:S(2)}) collective-permute-start(bf16[64,1536]{1,0:T(8,128)(2,1)} %get-tuple-element.216), channel_id=1, source_target_pairs={{0,24},{2,26},{4,28},{6,30},{8,16},{10,18},{12,20},{14,22},{16,8},... | collective-permute-start | bytes 589832 | tf_op jit(solution)/shard_map/ppermute | solution.py:116
  214.4 0.9 collective-permute-start.31
  216.1 4.7 %input_gradient.1 = f32[768,768]{1,0:T(8,128)} custom-call(bf16[768,768]{1,0:T(8,128)(2,1)} %bitcast.83, bf16[768,768]{1,0:T(8,128)(2,1)} %get-tuple-element.201.own_ref, bf16[768,768]{1,0:T(8,128)(2,1)} %copy-done.17, f32[768,768]{1,0:T(8,128)} %get-tuple-element.208.middle_ref, f32[6,768]{1,0:T(8,128)} %rep_ref.7), custom_call_target="tpu_custom_call" | custom-call | flops 6554999808 | bytes 1000000 | tf_op jit(solution)/shard_map/input_gradient/pallas_call | solution.py:1123
  221.5 2.7 %adam_unit.3 = (f32[576,128]{1,0:T(8,128)}, f32[576,128]{1,0:T(8,128)}, f32[576,128]{1,0:T(8,128)}) custom-call(bf16[384,1536]{1,0:T(8,128)(2,1)} %get-tuple-element.192.kept_ref.refs_0_, bf16[384,1536]{1,0:T(8,128)(2,1)} %collective-permute-done.21.one_ref.refs_1_, bf16[192,1536]{1,0:T(8,128)(2,1)} %collective-permute-done.26.two_ref.refs_2_, ...), custom_call_target="tpu_custom_call" | custom-call | flops 2875000064 | bytes 1000000 | tf_op jit(solution)/shard_map/adam_unit/pallas_call | solution.py:1156
  224.5 8.5 %collective-permute-done.32.refs_5_ = bf16[64,1536]{1,0:T(8,128)(2,1)S(1)} collective-permute-done((bf16[64,1536]{1,0:T(8,128)(2,1)}, bf16[64,1536]{1,0:T(8,128)(2,1)S(1)}, u32[]{:S(2)}, u32[]{:S(2)}) %collective-permute-start.32) | collective-permute-done | bytes 196640 | tf_op jit(solution)/shard_map/ppermute | solution.py:116
  233.0 0.8 add_add_fusion
  234.8 2.7 %adam_unit.4 = (f32[432,128]{1,0:T(8,128)}, f32[432,128]{1,0:T(8,128)}, f32[432,128]{1,0:T(8,128)}, f32[144,128]{1,0:T(8,128)}, f32[144,128]{1,0:T(8,128)}, /*index=5*/f32[144,128]{1,0:T(8,128)}) custom-call(bf16[400,1536]{1,0:T(8,128)(2,1)} %get-tuple-element.197.kept_ref.refs_0_, bf16[400,1536]{1,0:T(8,128)(2,1)} %collective-permute-done.22.one_ref.refs_1_, ...), custom_call_target="tpu_custom_call" | custom-call | flops 2875000064 | bytes 1000000 | tf_op jit(solution)/shard_map/adam_unit/pallas_call | solution.py:1156
  (144 shorter events, 17.5 us)
Async XLA Ops:
  0.7 22.6 %copy-start = (bf16[32,34,1,384]{3,0,2,1:T(8,128)(2,1)S(1)}, bf16[32,34,1,384]{3,0,2,1:T(8,128)(2,1)}, u32[]{:S(2)}) copy-start(bf16[32,34,1,384]{3,0,2,1:T(8,128)(2,1)} %param.25) | copy-start | bytes 2506756
  0.7 11.7 %copy-start.5 = (s32[32,529]{1,0:T(8,128)S(1)}, s32[32,529]{1,0:T(8,128)}, u32[]{:S(2)}) copy-start(s32[32,529]{1,0:T(8,128)} %param.28) | copy-start | bytes 203140
  0.7 11.7 %copy-start.15 = (s32[32]{0:T(128)S(1)}, s32[32]{0:T(128)}, u32[]{:S(2)}) copy-start(s32[32]{0:T(128)} %param.27) | copy-start | bytes 388
  0.7 12.5 %copy-start.16 = (s32[32]{0:T(128)S(1)}, s32[32]{0:T(128)}, u32[]{:S(2)}) copy-start(s32[32]{0:T(128)} %param.29) | copy-start | bytes 388
  2.9 20.3 %collective-permute-start.3 = (bf16[3,48,1536]{2,1,0:T(8,128)(2,1)}, bf16[3,48,1536]{2,1,0:T(8,128)(2,1)}, u32[]{:S(2)}, u32[]{:S(2)}) collective-permute-start(bf16[3,48,1536]{2,1,0:T(8,128)(2,1)} %get-tuple-element.129.o0), channel_id=1, source_target_pairs={{0,2},{1,5},{2,0},{3,7},{4,6},{5,1},{6,4},{7,3},{8,10},{9,13},{10,... | collective-permute-start | bytes 1327112 | tf_op jit(solution)/shard_map/ppermute | solution.py:514
  5.9 17.4 %collective-permute-start.4 = (bf16[3,48,1536]{2,1,0:T(8,128)(2,1)}, bf16[3,48,1536]{2,1,0:T(8,128)(2,1)}, u32[]{:S(2)}, u32[]{:S(2)}) collective-permute-start(bf16[3,48,1536]{2,1,0:T(8,128)(2,1)} %get-tuple-element.129.o0), channel_id=1, source_target_pairs={{0,4},{1,3},{2,6},{3,1},{4,0},{5,7},{6,2},{7,5},{8,12},{9,11},{10,... | collective-permute-start | bytes 1327112 | tf_op jit(solution)/shard_map/ppermute | solution.py:514
  7.4 13.6 %collective-permute-start = (bf16[1,48,1536]{2,1,0:T(8,128)(2,1)}, bf16[1,48,1536]{2,1,0:T(8,128)(2,1)}, u32[]{:S(2)}, u32[]{:S(2)}) collective-permute-start(bf16[1,48,1536]{2,1,0:T(8,128)(2,1)} %get-tuple-element.128), channel_id=1, source_target_pairs={{0,24},{2,26},{4,28},{6,30},{8,16},{10,18},{12,20},{14,22},{16,8},... | collective-permute-start | bytes 442376 | tf_op jit(solution)/shard_map/ppermute | solution.py:116
  11.0 10.0 %collective-permute-start.1 = (bf16[1,48,1536]{2,1,0:T(8,128)(2,1)}, bf16[1,48,1536]{2,1,0:T(8,128)(2,1)}, u32[]{:S(2)}, u32[]{:S(2)}) collective-permute-start(bf16[1,48,1536]{2,1,0:T(8,128)(2,1)} %get-tuple-element.128), channel_id=1, source_target_pairs={{0,8},{2,10},{4,12},{6,14},{8,0},{10,2},{12,4},{14,6},{16,24},{18,... | collective-permute-start | bytes 442376 | tf_op jit(solution)/shard_map/ppermute | solution.py:116
  11.0 12.2 %collective-permute-start.2 = (bf16[1,48,1536]{2,1,0:T(8,128)(2,1)}, bf16[1,48,1536]{2,1,0:T(8,128)(2,1)}, u32[]{:S(2)}, u32[]{:S(2)}) collective-permute-start(bf16[1,48,1536]{2,1,0:T(8,128)(2,1)} %get-tuple-element.128), channel_id=1, source_target_pairs={{0,16},{2,18},{4,20},{6,22},{8,24},{10,26},{12,28},{14,30},{16,0},... | collective-permute-start | bytes 442376 | tf_op jit(solution)/shard_map/ppermute | solution.py:116
  25.1 19.7 %copy-start.6 = (f32[1,6,384]{2,0,1:T(1,128)S(1)}, f32[1,6,384]{2,0,1:T(1,128)}, u32[]{:S(2)}) copy-start(f32[1,6,384]{2,0,1:T(1,128)} %param.45) | copy-start | bytes 27652
  25.1 13.4 %collective-permute-start.5 = (bf16[3,48,1536]{2,1,0:T(8,128)(2,1)}, bf16[3,48,1536]{2,1,0:T(8,128)(2,1)}, u32[]{:S(2)}, u32[]{:S(2)}) collective-permute-start(bf16[3,48,1536]{2,1,0:T(8,128)(2,1)} %join_chunks.2.p0), channel_id=1, source_target_pairs={{0,2},{1,5},{2,0},{3,7},{4,6},{5,1},{6,4},{7,3},{8,10},{9,13},{10,... | collective-permute-start | bytes 1327112 | tf_op jit(solution)/shard_map/ppermute | solution.py:514
  25.6 12.9 %collective-permute-start.6 = (bf16[3,48,1536]{2,1,0:T(8,128)(2,1)}, bf16[3,48,1536]{2,1,0:T(8,128)(2,1)}, u32[]{:S(2)}, u32[]{:S(2)}) collective-permute-start(bf16[3,48,1536]{2,1,0:T(8,128)(2,1)} %join_chunks.2.p0), channel_id=1, source_target_pairs={{0,4},{1,3},{2,6},{3,1},{4,0},{5,7},{6,2},{7,5},{8,12},{9,11},{10,... | collective-permute-start | bytes 1327112 | tf_op jit(solution)/shard_map/ppermute | solution.py:514
  26.1 15.2 %collective-permute-start.7 = (bf16[3,48,1536]{2,1,0:T(8,128)(2,1)}, bf16[3,48,1536]{2,1,0:T(8,128)(2,1)}, u32[]{:S(2)}, u32[]{:S(2)}) collective-permute-start(bf16[3,48,1536]{2,1,0:T(8,128)(2,1)} %collective-permute-done.3.o1), channel_id=1, source_target_pairs={{0,4},{1,3},{2,6},{3,1},{4,0},{5,7},{6,2},{7,5},{8,12},{9,11},{10,... | collective-permute-start | bytes 1327112 | tf_op jit(solution)/shard_map/ppermute | solution.py:514
  27.7 9.3 %collective-permute-start.8 = (bf16[2,48,1536]{2,1,0:T(8,128)(2,1)}, bf16[2,48,1536]{2,1,0:T(8,128)(2,1)S(1)}, u32[]{:S(2)}, u32[]{:S(2)}) collective-permute-start(bf16[2,48,1536]{2,1,0:T(8,128)(2,1)} %get-tuple-element.140), channel_id=1, source_target_pairs={{0,24},{2,26},{4,28},{6,30},{8,16},{10,18},{12,20},{14,22},{16,8},... | collective-permute-start | bytes 884744 | tf_op jit(solution)/shard_map/ppermute | solution.py:116
  36.9 4.4 %copy-start.20 = (bf16[2,48,1536]{2,1,0:T(8,128)(2,1)}, bf16[2,48,1536]{2,1,0:T(8,128)(2,1)S(1)}, u32[]{:S(2)}) copy-start(bf16[2,48,1536]{2,1,0:T(8,128)(2,1)S(1)} %collective-permute-done.8.refs_0_) | copy-start | bytes 884740
  41.3 16.9 %collective-permute-start.9 = (bf16[3,48,1536]{2,1,0:T(8,128)(2,1)}, bf16[3,48,1536]{2,1,0:T(8,128)(2,1)S(1)}, u32[]{:S(2)}, u32[]{:S(2)}) collective-permute-start(bf16[3,48,1536]{2,1,0:T(8,128)(2,1)} %collective-permute-done.5.p1), channel_id=1, source_target_pairs={{0,4},{1,3},{2,6},{3,1},{4,0},{5,7},{6,2},{7,5},{8,12},{9,11},{10,... | collective-permute-start | bytes 1327112 | tf_op jit(solution)/shard_map/ppermute | solution.py:514
  41.8 15.0 %collective-permute-start.10 = (bf16[2,48,1536]{2,1,0:T(8,128)(2,1)}, bf16[2,48,1536]{2,1,0:T(8,128)(2,1)S(1)}, u32[]{:S(2)}, u32[]{:S(2)}) collective-permute-start(bf16[2,48,1536]{2,1,0:T(8,128)(2,1)} %get-tuple-element.140), channel_id=1, source_target_pairs={{0,8},{2,10},{4,12},{6,14},{8,0},{10,2},{12,4},{14,6},{16,24},{18,... | collective-permute-start | bytes 884744 | tf_op jit(solution)/shard_map/ppermute | solution.py:116
  42.2 16.0 %collective-permute-start.11 = (bf16[2,48,1536]{2,1,0:T(8,128)(2,1)}, bf16[2,48,1536]{2,1,0:T(8,128)(2,1)}, u32[]{:S(2)}, u32[]{:S(2)}) collective-permute-start(bf16[2,48,1536]{2,1,0:T(8,128)(2,1)} %get-tuple-element.140), channel_id=1, source_target_pairs={{0,16},{2,18},{4,20},{6,22},{8,24},{10,26},{12,28},{14,30},{16,0},... | collective-permute-start | bytes 884744 | tf_op jit(solution)/shard_map/ppermute | solution.py:116
  56.9 1.3 copy-start.21
  58.2 2.3 copy-start.19
  60.5 29.9 %collective-permute-start.12 = (bf16[6,48,1536]{2,1,0:T(8,128)(2,1)}, bf16[6,48,1536]{2,1,0:T(8,128)(2,1)}, u32[]{:S(2)}, u32[]{:S(2)}) collective-permute-start(bf16[6,48,1536]{2,1,0:T(8,128)(2,1)} %join_chunks.3.p0), channel_id=1, source_target_pairs={{0,2},{1,5},{2,0},{3,7},{4,6},{5,1},{6,4},{7,3},{8,10},{9,13},{10,... | collective-permute-start | bytes 2654216 | tf_op jit(solution)/shard_map/ppermute | solution.py:514
  62.0 28.5 %collective-permute-start.13 = (bf16[6,48,1536]{2,1,0:T(8,128)(2,1)}, bf16[6,48,1536]{2,1,0:T(8,128)(2,1)}, u32[]{:S(2)}, u32[]{:S(2)}) collective-permute-start(bf16[6,48,1536]{2,1,0:T(8,128)(2,1)} %join_chunks.3.p0), channel_id=1, source_target_pairs={{0,4},{1,3},{2,6},{3,1},{4,0},{5,7},{6,2},{7,5},{8,12},{9,11},{10,... | collective-permute-start | bytes 2654216 | tf_op jit(solution)/shard_map/ppermute | solution.py:514
  63.5 29.3 %all-to-all-start = ((bf16[16,72,384]{2,1,0:T(8,128)(2,1)}), bf16[16,72,384]{2,1,0:T(8,128)(2,1)}, u32[]{:S(2)}, u32[]{:S(2)}) async-start(bf16[16,72,384]{2,1,0:T(8,128)(2,1)} %bitcast.72), calls=%async_computation | async-start | bytes 1769472 | tf_op jit(solution)/shard_map/all_to_all | solution.py:1264
  84.6 15.7 %collective-permute-start.15 = (bf16[768,768]{1,0:T(8,128)(2,1)}, bf16[768,768]{1,0:T(8,128)(2,1)}, u32[]{:S(2)}, u32[]{:S(2)}) collective-permute-start(bf16[768,768]{1,0:T(8,128)(2,1)} %get-tuple-element.148.own_any), channel_id=1, source_target_pairs={{0,1},{1,0},{2,3},{3,2},{4,5},{5,4},{6,7},{7,6},{8,9},{9,8},{10,11... | collective-permute-start | bytes 3538952 | tf_op jit(solution)/shard_map/ppermute | solution.py:120
  90.5 13.4 %collective-permute-start.14 = (bf16[6,48,1536]{2,1,0:T(8,128)(2,1)}, bf16[6,48,1536]{2,1,0:T(8,128)(2,1)}, u32[]{:S(2)}, u32[]{:S(2)}) collective-permute-start(bf16[6,48,1536]{2,1,0:T(8,128)(2,1)} %collective-permute-done.12.p1), channel_id=1, source_target_pairs={{0,4},{1,3},{2,6},{3,1},{4,0},{5,7},{6,2},{7,5},{8,12},{9,11},{10,... | collective-permute-start | bytes 2654216 | tf_op jit(solution)/shard_map/ppermute | solution.py:514
  95.5 2.2 collective-permute-start.16
  125.5 4.1 %collective-permute-start.19 = (bf16[768,768]{1,0:T(8,128)(2,1)}, bf16[768,768]{1,0:T(8,128)(2,1)}, u32[]{:S(2)}, u32[]{:S(2)}) collective-permute-start(bf16[768,768]{1,0:T(8,128)(2,1)} %get-tuple-element.170), channel_id=1, source_target_pairs={{0,1},{1,0},{2,3},{3,2},{4,5},{5,4},{6,7},{7,6},{8,9},{9,8},{10,11... | collective-permute-start | bytes 3538952 | tf_op jit(solution)/shard_map/ppermute | solution.py:120
  125.6 16.6 %collective-permute-start.17 = (bf16[384,1536]{1,0:T(8,128)(2,1)}, bf16[384,1536]{1,0:T(8,128)(2,1)}, u32[]{:S(2)}, u32[]{:S(2)}) collective-permute-start(bf16[384,1536]{1,0:T(8,128)(2,1)} %get-tuple-element.167), channel_id=1, source_target_pairs={{0,4},{1,3},{2,6},{3,1},{4,0},{5,7},{6,2},{7,5},{8,12},{9,11},{10,... | collective-permute-start | bytes 3538952 | tf_op jit(solution)/shard_map/ppermute | solution.py:514
  127.0 15.2 %collective-permute-start.18 = (bf16[768,768]{1,0:T(8,128)(2,1)}, bf16[768,768]{1,0:T(8,128)(2,1)}, u32[]{:S(2)}, u32[]{:S(2)}) collective-permute-start(bf16[768,768]{1,0:T(8,128)(2,1)} %get-tuple-element.168.own_any), channel_id=1, source_target_pairs={{0,1},{1,0},{2,3},{3,2},{4,5},{5,4},{6,7},{7,6},{8,9},{9,8},{10,11... | collective-permute-start | bytes 3538952 | tf_op jit(solution)/shard_map/ppermute | solution.py:120
  128.0 14.1 %copy-start.4 = (bf16[384,1536]{1,0:T(8,128)(2,1)S(1)}, bf16[384,1536]{1,0:T(8,128)(2,1)}, u32[]{:S(2)}) copy-start(bf16[384,1536]{1,0:T(8,128)(2,1)} %get-tuple-element.166.kept_ref.refs_0_) | copy-start | bytes 3538948
  128.0 42.3 %collective-permute-start.21 = (bf16[384,1536]{1,0:T(8,128)(2,1)}, bf16[384,1536]{1,0:T(8,128)(2,1)}, u32[]{:S(2)}, u32[]{:S(2)}) collective-permute-start(bf16[384,1536]{1,0:T(8,128)(2,1)} %get-tuple-element.172), channel_id=1, source_target_pairs={{0,4},{1,3},{2,6},{3,1},{4,0},{5,7},{6,2},{7,5},{8,12},{9,11},{10,... | collective-permute-start | bytes 3538952 | tf_op jit(solution)/shard_map/ppermute | solution.py:514
  143.4 27.0 %collective-permute-start.20 = (bf16[192,1536]{1,0:T(8,128)(2,1)S(1)}, bf16[192,1536]{1,0:T(8,128)(2,1)}, u32[]{:S(2)}, u32[]{:S(2)}) collective-permute-start(bf16[192,1536]{1,0:T(8,128)(2,1)S(1)} %add_convert_fusion.2), channel_id=1, source_target_pairs={{0,2},{1,5},{2,0},{3,7},{4,6},{5,1},{6,4},{7,3},{8,10},{9,13},{10,... | collective-permute-start | bytes 1769480 | tf_op jit(solution)/shard_map/ppermute | solution.py:514
  144.8 25.8 %all-to-all-start.1 = ((bf16[16,72,384]{2,1,0:T(8,128)(2,1)}), bf16[16,72,384]{2,1,0:T(8,128)(2,1)}, u32[]{:S(2)}, u32[]{:S(2)}) async-start(bf16[16,72,384]{2,1,0:T(8,128)(2,1)} %bitcast.73), calls=%async_computation.1 | async-start | bytes 1769472 | tf_op jit(solution)/shard_map/all_to_all | solution.py:1264
  170.6 23.4 %collective-permute-start.22 = (bf16[400,1536]{1,0:T(8,128)(2,1)}, bf16[400,1536]{1,0:T(8,128)(2,1)}, u32[]{:S(2)}, u32[]{:S(2)}) collective-permute-start(bf16[400,1536]{1,0:T(8,128)(2,1)} %get-tuple-element.187), channel_id=1, source_target_pairs={{0,4},{1,3},{2,6},{3,1},{4,0},{5,7},{6,2},{7,5},{8,12},{9,11},{10,... | collective-permute-start | bytes 3686408 | tf_op jit(solution)/shard_map/ppermute | solution.py:514
  173.7 8.1 %copy-start.28 = (bf16[384]{0:T(512)(128)(2,1)S(1)}, bf16[384]{0:T(512)(128)(2,1)}, u32[]{:S(2)}) copy-start(bf16[384]{0:T(512)(128)(2,1)} %param.26) | copy-start | bytes 2308
  173.7 18.3 %collective-permute-start.26 = (bf16[192,1536]{1,0:T(8,128)(2,1)S(1)}, bf16[192,1536]{1,0:T(8,128)(2,1)}, u32[]{:S(2)}, u32[]{:S(2)}) collective-permute-start(bf16[192,1536]{1,0:T(8,128)(2,1)S(1)} %add_convert_fusion.1), channel_id=1, source_target_pairs={{0,2},{1,5},{2,0},{3,7},{4,6},{5,1},{6,4},{7,3},{8,10},{9,13},{10,... | collective-permute-start | bytes 1769480 | tf_op jit(solution)/shard_map/ppermute | solution.py:514
  177.5 8.9 %collective-permute-start.23 = (bf16[48,1536]{1,0:T(8,128)(2,1)}, bf16[48,1536]{1,0:T(8,128)(2,1)S(1)}, u32[]{:S(2)}, u32[]{:S(2)}) collective-permute-start(bf16[48,1536]{1,0:T(8,128)(2,1)} %get-tuple-element.189), channel_id=1, source_target_pairs={{0,24},{2,26},{4,28},{6,30},{8,16},{10,18},{12,20},{14,22},{16,8},... | collective-permute-start | bytes 442376 | tf_op jit(solution)/shard_map/ppermute | solution.py:116
  180.7 7.9 %collective-permute-start.24 = (bf16[48,1536]{1,0:T(8,128)(2,1)}, bf16[48,1536]{1,0:T(8,128)(2,1)S(1)}, u32[]{:S(2)}, u32[]{:S(2)}) collective-permute-start(bf16[48,1536]{1,0:T(8,128)(2,1)} %get-tuple-element.190), channel_id=1, source_target_pairs={{0,8},{2,10},{4,12},{6,14},{8,0},{10,2},{12,4},{14,6},{16,24},{18,... | collective-permute-start | bytes 442376 | tf_op jit(solution)/shard_map/ppermute | solution.py:116
  180.7 13.2 %copy-start.3 = (bf16[400,1536]{1,0:T(8,128)(2,1)S(1)}, bf16[400,1536]{1,0:T(8,128)(2,1)}, u32[]{:S(2)}) copy-start(bf16[400,1536]{1,0:T(8,128)(2,1)} %get-tuple-element.197.kept_ref.refs_0_) | copy-start | bytes 3686404
  180.7 11.2 %collective-permute-start.25 = (bf16[48,1536]{1,0:T(8,128)(2,1)}, bf16[48,1536]{1,0:T(8,128)(2,1)S(1)}, u32[]{:S(2)}, u32[]{:S(2)}) collective-permute-start(bf16[48,1536]{1,0:T(8,128)(2,1)} %get-tuple-element.191), channel_id=1, source_target_pairs={{0,16},{2,18},{4,20},{6,22},{8,24},{10,26},{12,28},{14,30},{16,0},... | collective-permute-start | bytes 442376 | tf_op jit(solution)/shard_map/ppermute | solution.py:116
  186.4 12.9 %copy-start.23 = (bf16[48,1536]{1,0:T(8,128)(2,1)}, bf16[48,1536]{1,0:T(8,128)(2,1)S(1)}, u32[]{:S(2)}) copy-start(bf16[48,1536]{1,0:T(8,128)(2,1)S(1)} %collective-permute-done.23.refs_3_) | copy-start | bytes 442372
  188.7 10.6 %copy-start.25 = (bf16[48,1536]{1,0:T(8,128)(2,1)}, bf16[48,1536]{1,0:T(8,128)(2,1)S(1)}, u32[]{:S(2)}) copy-start(bf16[48,1536]{1,0:T(8,128)(2,1)S(1)} %collective-permute-done.24.refs_4_) | copy-start | bytes 442372
  192.0 7.3 %copy-start.27 = (bf16[48,1536]{1,0:T(8,128)(2,1)}, bf16[48,1536]{1,0:T(8,128)(2,1)S(1)}, u32[]{:S(2)}) copy-start(bf16[48,1536]{1,0:T(8,128)(2,1)S(1)} %collective-permute-done.25.refs_5_) | copy-start | bytes 442372
  194.0 14.1 %collective-permute-start.29 = (bf16[768,768]{1,0:T(8,128)(2,1)}, bf16[768,768]{1,0:T(8,128)(2,1)S(1)}, u32[]{:S(2)}, u32[]{:S(2)}) collective-permute-start(bf16[768,768]{1,0:T(8,128)(2,1)} %get-tuple-element.201.own_ref), channel_id=1, source_target_pairs={{0,1},{1,0},{2,3},{3,2},{4,5},{5,4},{6,7},{7,6},{8,9},{9,8},{10,11... | collective-permute-start | bytes 3538952 | tf_op jit(solution)/shard_map/ppermute | solution.py:120
  195.2 4.0 %copy-start.2 = (bf16[208,1536]{1,0:T(8,128)(2,1)}, bf16[208,1536]{1,0:T(8,128)(2,1)S(1)}, u32[]{:S(2)}) copy-start(bf16[208,1536]{1,0:T(8,128)(2,1)S(1)} %add_convert_fusion.refs_0_) | copy-start | bytes 1916932
  195.2 12.8 %collective-permute-start.27 = (bf16[208,1536]{1,0:T(8,128)(2,1)S(1)}, bf16[208,1536]{1,0:T(8,128)(2,1)S(1)}, u32[]{:S(2)}, u32[]{:S(2)}) collective-permute-start(bf16[208,1536]{1,0:T(8,128)(2,1)S(1)} %add_convert_fusion.refs_0_), channel_id=1, source_target_pairs={{0,2},{1,5},{2,0},{3,7},{4,6},{5,1},{6,4},{7,3},{8,10},{9,13},{10,... | collective-permute-start | bytes 1916936 | tf_op jit(solution)/shard_map/ppermute | solution.py:514
  199.3 8.8 %collective-permute-start.28 = (bf16[48,1536]{1,0:T(8,128)(2,1)}, bf16[48,1536]{1,0:T(8,128)(2,1)S(1)}, u32[]{:S(2)}, u32[]{:S(2)}) collective-permute-start(bf16[48,1536]{1,0:T(8,128)(2,1)} %get-tuple-element.200), channel_id=1, source_target_pairs={{0,24},{2,26},{4,28},{6,30},{8,16},{10,18},{12,20},{14,22},{16,8},... | collective-permute-start | bytes 442376 | tf_op jit(solution)/shard_map/ppermute | solution.py:116
  201.9 18.9 %collective-permute-start.33 = (bf16[48,1536]{1,0:T(8,128)(2,1)}, bf16[48,1536]{1,0:T(8,128)(2,1)S(1)}, u32[]{:S(2)}, u32[]{:S(2)}) collective-permute-start(bf16[48,1536]{1,0:T(8,128)(2,1)} %get-tuple-element.210), channel_id=1, source_target_pairs={{0,8},{2,10},{4,12},{6,14},{8,0},{10,2},{12,4},{14,6},{16,24},{18,... | collective-permute-start | bytes 442376 | tf_op jit(solution)/shard_map/ppermute | solution.py:116
  201.9 18.9 %collective-permute-start.34 = (bf16[48,1536]{1,0:T(8,128)(2,1)}, bf16[48,1536]{1,0:T(8,128)(2,1)S(1)}, u32[]{:S(2)}, u32[]{:S(2)}) collective-permute-start(bf16[48,1536]{1,0:T(8,128)(2,1)} %get-tuple-element.211), channel_id=1, source_target_pairs={{0,16},{2,18},{4,20},{6,22},{8,24},{10,26},{12,28},{14,30},{16,0},... | collective-permute-start | bytes 442376 | tf_op jit(solution)/shard_map/ppermute | solution.py:116
  208.1 12.8 %copy-start.22 = (bf16[48,1536]{1,0:T(8,128)(2,1)}, bf16[48,1536]{1,0:T(8,128)(2,1)S(1)}, u32[]{:S(2)}) copy-start(bf16[48,1536]{1,0:T(8,128)(2,1)S(1)} %collective-permute-done.28.refs_3_) | copy-start | bytes 442372
  209.0 2.7 %copy-start.17 = (bf16[768,768]{1,0:T(8,128)(2,1)}, bf16[768,768]{1,0:T(8,128)(2,1)S(1)}, u32[]{:S(2)}) copy-start(bf16[768,768]{1,0:T(8,128)(2,1)S(1)} %collective-permute-done.29.other_ref) | copy-start | bytes 3538948
  211.7 12.5 %collective-permute-start.30 = (bf16[64,1536]{1,0:T(8,128)(2,1)}, bf16[64,1536]{1,0:T(8,128)(2,1)S(1)}, u32[]{:S(2)}, u32[]{:S(2)}) collective-permute-start(bf16[64,1536]{1,0:T(8,128)(2,1)} %get-tuple-element.216), channel_id=1, source_target_pairs={{0,24},{2,26},{4,28},{6,30},{8,16},{10,18},{12,20},{14,22},{16,8},... | collective-permute-start | bytes 589832 | tf_op jit(solution)/shard_map/ppermute | solution.py:116
  214.4 10.1 %collective-permute-start.31 = (bf16[64,1536]{1,0:T(8,128)(2,1)}, bf16[64,1536]{1,0:T(8,128)(2,1)S(1)}, u32[]{:S(2)}, u32[]{:S(2)}) collective-permute-start(bf16[64,1536]{1,0:T(8,128)(2,1)} %get-tuple-element.205), channel_id=1, source_target_pairs={{0,8},{2,10},{4,12},{6,14},{8,0},{10,2},{12,4},{14,6},{16,24},{18,... | collective-permute-start | bytes 589832 | tf_op jit(solution)/shard_map/ppermute | solution.py:116
  215.3 17.7 %collective-permute-start.32 = (bf16[64,1536]{1,0:T(8,128)(2,1)}, bf16[64,1536]{1,0:T(8,128)(2,1)S(1)}, u32[]{:S(2)}, u32[]{:S(2)}) collective-permute-start(bf16[64,1536]{1,0:T(8,128)(2,1)} %get-tuple-element.206), channel_id=1, source_target_pairs={{0,16},{2,18},{4,20},{6,22},{8,24},{10,26},{12,28},{14,30},{16,0},... | collective-permute-start | bytes 589832 | tf_op jit(solution)/shard_map/ppermute | solution.py:116
  221.5 12.6 %copy-start.13 = (f32[1,6,384]{2,0,1:T(1,128)S(1)}, f32[1,6,384]{2,0,1:T(1,128)}, u32[]{:S(2)}) copy-start(f32[1,6,384]{2,0,1:T(1,128)} %param.46) | copy-start | bytes 27652
  221.5 12.6 %copy-start.14 = (f32[1,6,384]{2,0,1:T(1,128)S(1)}, f32[1,6,384]{2,0,1:T(1,128)}, u32[]{:S(2)}) copy-start(f32[1,6,384]{2,0,1:T(1,128)} %param.47) | copy-start | bytes 27652
  224.3 10.5 %copy-start.10 = (bf16[64,1536]{1,0:T(8,128)(2,1)}, bf16[64,1536]{1,0:T(8,128)(2,1)S(1)}, u32[]{:S(2)}) copy-start(bf16[64,1536]{1,0:T(8,128)(2,1)S(1)} %collective-permute-done.30.refs_3_) | copy-start | bytes 589828
  224.5 10.3 %copy-start.11 = (bf16[64,1536]{1,0:T(8,128)(2,1)}, bf16[64,1536]{1,0:T(8,128)(2,1)S(1)}, u32[]{:S(2)}) copy-start(bf16[64,1536]{1,0:T(8,128)(2,1)S(1)} %collective-permute-done.31.refs_4_) | copy-start | bytes 589828
  233.0 1.8 copy-start.12
  233.9 4.2 %collective-permute-start.35 = (f32[3,1536]{1,0:T(4,128)S(1)}, f32[3,1536]{1,0:T(4,128)S(1)}, u32[]{:S(2)}, u32[]{:S(2)}) collective-permute-start(f32[3,1536]{1,0:T(4,128)S(1)} %slice.85), channel_id=1, source_target_pairs={{0,1},{1,0},{2,3},{3,2},{4,5},{5,4},{6,7},{7,6},{8,9},{9,8},{10,11... | collective-permute-start | bytes 55304 | tf_op jit(solution)/shard_map/ppermute | solution.py:120
  234.8 3.4 %copy-start.7 = (f32[6,768]{1,0:T(8,128)S(1)}, f32[6,768]{1,0:T(8,128)}, u32[]{:S(2)}) copy-start(f32[6,768]{1,0:T(8,128)} %rep_ref.7) | copy-start | bytes 55300
  234.8 3.4 %copy-start.8 = (f32[6,768]{1,0:T(8,128)S(1)}, f32[6,768]{1,0:T(8,128)}, u32[]{:S(2)}) copy-start(f32[6,768]{1,0:T(8,128)} %param.43) | copy-start | bytes 55300
  234.8 3.4 %copy-start.9 = (f32[6,768]{1,0:T(8,128)S(1)}, f32[6,768]{1,0:T(8,128)}, u32[]{:S(2)}) copy-start(f32[6,768]{1,0:T(8,128)} %param.44) | copy-start | bytes 55300
  234.8 4.1 %copy-start.1 = (bf16[32,34,1,384]{3,0,2,1:T(8,128)(2,1)S(1)}, bf16[32,34,1,384]{3,0,2,1:T(8,128)(2,1)}, u32[]{:S(2)}) copy-start(bf16[32,34,1,384]{3,0,2,1:T(8,128)(2,1)} %param.25) | copy-start | bytes 2506756
  (3 other events, 2.3 us)

commit v3 on v2

--- a/solution.py
+++ b/solution.py
@@ -809,16 +809,19 @@
     parts = hidden_width // wide
 
     def body(
-        words_ref, rep_ref, bias_ref, in_any, own_any, other_any, grad_any,
+        words_ref, rep_any, bias_any, in_any, own_any, other_any, grad_any,
         o0, o1, o2, o3, p0, p1, p2, p3,
-        hidden_sum_ref, grad_sum_ref, middle_any, back_any, second_any,
+        hidden_sum_any, grad_sum_any, middle_any, back_any, second_any,
         sent_b, kept_b, sent_c, kept_c,
-        w_first, w_second, rows_ref, own_ref, other_ref, grad_ref, middle_ref, normed_ref,
+        rep_ref, bias_ref, hidden_sum_ref, grad_sum_ref, w_first, w_second, rows_ref, own_ref, other_ref, grad_ref, middle_ref, normed_ref,
         active_ref, slope_ref, grad_hidden_ref, back_ref, second_ref, whole_b, whole_c, semaphores,
     ):
         copies = Copies(semaphores)
         first_loads = copies.start(
-            [(in_any, rows_ref), (own_any, own_ref), (other_any, other_ref)]
+            [
+                (in_any, rows_ref), (own_any, own_ref), (other_any, other_ref),
+                (rep_any, rep_ref), (bias_any, bias_ref),
+            ]
         )
         own_refs, later = (o0, o1, o2, o3), (p0, p1, p2, p3)
         loads_b = copies.start(chunk_pairs(words_ref, own_refs, later, 1, w_first))
@@ -869,7 +872,12 @@
             )
 
         back_ref[...] = contract_last(grad_hidden_ref[...], w_first[...]).astype(jnp.bfloat16)
-        stores += copies.start([(back_ref, back_any)])
+        stores += copies.start(
+            [
+                (back_ref, back_any), (hidden_sum_ref, hidden_sum_any),
+                (grad_sum_ref, grad_sum_any),
+            ]
+        )
 
         @pl.loop(0, hidden_width // half)
         def _(part):
@@ -903,8 +911,8 @@
     low, full = jnp.bfloat16, jnp.float32
     return pl.pallas_call(
         body,
-        in_specs=[IN_SMEM, IN_VMEM, IN_VMEM] + [ANY] * 12,
-        out_specs=[IN_VMEM, IN_VMEM] + [ANY] * 7,
+        in_specs=[IN_SMEM] + [ANY] * 14,
+        out_specs=[ANY] * 9,
         out_shape=[
             shaped((1, hidden_width), full),
             shaped((1, width), full),
@@ -915,6 +923,10 @@
         + unit_shapes()
         + unit_shapes(),
         scratch_shapes=[
+            pltpu.VMEM(rep.shape, full),
+            pltpu.VMEM((1, hidden_width), full),
+            pltpu.VMEM((1, hidden_width), full),
+            pltpu.VMEM((1, width), full),
             pltpu.VMEM((width, hidden_width), low),
             pltpu.VMEM((hidden_width, width), low),
             pltpu.VMEM((count, width), low),
@@ -930,7 +942,7 @@
             pltpu.VMEM((count, width), low),
             pltpu.VMEM((width, hidden_width), low),
             pltpu.VMEM((hidden_width, width), low),
-            pltpu.SemaphoreType.DMA((104,)),
+            pltpu.SemaphoreType.DMA((112,)),
         ],
         compiler_params=params(),
         cost_estimate=cost(18),
@@ -949,10 +961,11 @@
     low, full = jnp.bfloat16, jnp.float32
 
     def body(
-        words_ref, rep_ref, hidden_sum_ref, grad_sum_ref, mask_sum_ref,
+        words_ref, rep_any, hidden_sum_any, grad_sum_any, mask_sum_any,
         middle_any, own_any, other_any, grad_any, w_out_any, attended_any, qkv_any, prob_any,
         normed_any, weights_any, in_any,
         grad_middle_any, back_any, sent, kept,
+        rep_ref, hidden_sum_ref, grad_sum_ref, mask_sum_ref,
         middle_ref, own_ref, other_ref, grad_ref, w_out_ref, attended_ref, qkv_ref, prob_ref,
         normed_ref, weights_ref, in_ref, grad_middle_ref, back_ref, branch, grad_attended,
         grad_qkv, spread, whole, vectors, low_vectors, semaphores,
@@ -961,7 +974,7 @@
         early = copies.start(
             [
                 (middle_any, middle_ref), (own_any, own_ref), (other_any, other_ref),
-                (grad_any, grad_ref),
+                (grad_any, grad_ref), (rep_any, rep_ref),
             ]
         )
         outer = copies.start([(w_out_any, w_out_ref), (attended_any, attended_ref)])
@@ -971,6 +984,8 @@
         )
         late = copies.start(
             [(normed_any, normed_ref), (weights_any, weights_ref), (in_any, in_ref)]
+            + [(hidden_sum_any, hidden_sum_ref), (grad_sum_any, grad_sum_ref)]
+            + [(mask_sum_any, mask_sum_ref)]
         )
         vectors[...] = jnp.zeros_like(vectors)
         finish(early)
@@ -1076,10 +1091,14 @@
 
     return pl.pallas_call(
         body,
-        in_specs=[IN_SMEM] + [IN_VMEM] * 4 + [ANY] * 11,
+        in_specs=[IN_SMEM] + [ANY] * 15,
         out_specs=[ANY] * 4,
         out_shape=[shaped((count, width), full), shaped((count, width), low)] + unit_shapes(16),
         scratch_shapes=[
+            pltpu.VMEM(rep.shape, full),
+            pltpu.VMEM(hidden_sum.shape, full),
+            pltpu.VMEM(grad_sum.shape, full),
+            pltpu.VMEM(mask_sum.shape, full),
             pltpu.VMEM((count, width), full),
             pltpu.VMEM((count, width), low),
             pltpu.VMEM((count, width), low),

time: 240 us -> 239 us (level)
  no operation moved by 1% of the time
where the time goes in v3:
time: 239 us; the launch traced here: 238 us
  Pallas kernels  85 us (36%)
  waiting for transfers between devices  61.4 us (26%)
  starting transfers between devices  53.8 us (23%)
  other arithmetic  14.1 us (6%)
  matrix products  14.1 us (6%)
  local copies, waits for them, and re-layouts  8.56 us (4%)
    ppermute x15, waiting for transfers between devices, hop(): lax.ppermute(array, 'dp', [(i, i ^ distance) for i in range(axis_count)])  34.6 us
    ppermute x15, waiting for transfers between devices, hop_by_core(): return lax.ppermute(array, ('dp', 'mp'), pairs)  24.1 us
    ppermute x15, starting transfers between devices, hop(): lax.ppermute(array, 'dp', [(i, i ^ distance) for i in range(axis_count)])  23.1 us
    ppermute x15, starting transfers between devices, hop_by_core(): return lax.ppermute(array, ('dp', 'mp'), pairs)  21.1 us
    pallas_call x1, Pallas kernels, mlp_all(): pl.pallas_call(body, in_specs=[IN_SMEM] + [ANY] * 14, out_specs=[ANY] * 9...  21 us
    pallas_call x1, Pallas kernels, attention_back(): pl.pallas_call(body, in_specs=[IN_SMEM] + [ANY] * 15, out_specs=[ANY] * 4...  20.7 us
    pallas_call x1, Pallas kernels, attention_forward(): pl.pallas_call(body, grid=(pairs_of_heads,), in_specs=[IN_SMEM, fixed(cou...  16.8 us
    all_to_all x2, starting transfers between devices, exchanged(): array = lax.all_to_all(array, 'dp', split_axis=0, concat_axis=0, tiled=True)  9.06 us
  transfers between devices with their start and end apart: 38, of which 19 were waited for; matrix products, arithmetic and copies ran while one was open for 14% of the time, Pallas kernels for 24%

profile of v3, /device:TPU:0, one launch (start us, length us, event | category | flops | bytes accessed | tf_op | source)
XLA Modules:
  0.0 238.1 jit_solution(3333068029646472282)
XLA Ops:
  0.7 2.2 pack_units.1
  2.9 2.9 %collective-permute-start.3 = (bf16[3,48,1536]{2,1,0:T(8,128)(2,1)}, bf16[3,48,1536]{2,1,0:T(8,128)(2,1)}, u32[]{:S(2)}, u32[]{:S(2)}) collective-permute-start(bf16[3,48,1536]{2,1,0:T(8,128)(2,1)} %get-tuple-element.129.o0), channel_id=1, source_target_pairs={{0,2},{1,5},{2,0},{3,7},{4,6},{5,1},{6,4},{7,3},{8,10},{9,13},{10,... | collective-permute-start | bytes 1327112 | tf_op jit(solution)/shard_map/ppermute | solution.py:514
  5.9 1.5 collective-permute-start.4
  7.4 3.6 %collective-permute-start = (bf16[1,48,1536]{2,1,0:T(8,128)(2,1)}, bf16[1,48,1536]{2,1,0:T(8,128)(2,1)}, u32[]{:S(2)}, u32[]{:S(2)}) collective-permute-start(bf16[1,48,1536]{2,1,0:T(8,128)(2,1)} %get-tuple-element.128), channel_id=1, source_target_pairs={{0,24},{2,26},{4,28},{6,30},{8,16},{10,18},{12,20},{14,22},{16,8},... | collective-permute-start | bytes 442376 | tf_op jit(solution)/shard_map/ppermute | solution.py:116
  16.1 1.8 fusion.1
  17.9 1.5 gather_fusion
  21.0 2.3 collective-permute-done.2.refs_2_
  23.2 1.9 join_chunks.2.p0
  26.1 1.5 collective-permute-start.7
  27.7 2.6 %collective-permute-start.8 = (bf16[2,48,1536]{2,1,0:T(8,128)(2,1)}, bf16[2,48,1536]{2,1,0:T(8,128)(2,1)S(1)}, u32[]{:S(2)}, u32[]{:S(2)}) collective-permute-start(bf16[2,48,1536]{2,1,0:T(8,128)(2,1)} %get-tuple-element.140), channel_id=1, source_target_pairs={{0,24},{2,26},{4,28},{6,30},{8,16},{10,18},{12,20},{14,22},{16,8},... | collective-permute-start | bytes 884744 | tf_op jit(solution)/shard_map/ppermute | solution.py:116
  30.3 2.6 %convolution_convert_fusion.1 = bf16[1152,384]{1,0:T(8,128)(2,1)} fusion(bf16[1152,1088]{1,0:T(8,128)(2,1)S(1)} %fusion, bf16[1088,384]{1,0:T(8,128)(2,1)S(1)} %bitcast.71), kind=kOutput, calls=%fused_computation.7 | convolution fusion | flops 963035136 | bytes 4227072 | tf_op jit(solution)/shard_map/dot_general | solution.py:34
  33.7 3.2 %collective-permute-done.8.refs_0_ = bf16[2,48,1536]{2,1,0:T(8,128)(2,1)S(1)} collective-permute-done((bf16[2,48,1536]{2,1,0:T(8,128)(2,1)}, bf16[2,48,1536]{2,1,0:T(8,128)(2,1)S(1)}, u32[]{:S(2)}, u32[]{:S(2)}) %collective-permute-start.8) | collective-permute-done | bytes 294944 | tf_op jit(solution)/shard_map/ppermute | solution.py:116
  36.9 1.6 collective-permute-done.5.p1
  38.5 2.8 %collective-permute-done.7.o3 = bf16[3,48,1536]{2,1,0:T(8,128)(2,1)} collective-permute-done((bf16[3,48,1536]{2,1,0:T(8,128)(2,1)}, bf16[3,48,1536]{2,1,0:T(8,128)(2,1)}, u32[]{:S(2)}, u32[]{:S(2)}) %collective-permute-start.7) | collective-permute-done | bytes 442400 | tf_op jit(solution)/shard_map/ppermute | solution.py:514
  42.2 2.5 %collective-permute-start.11 = (bf16[2,48,1536]{2,1,0:T(8,128)(2,1)}, bf16[2,48,1536]{2,1,0:T(8,128)(2,1)}, u32[]{:S(2)}, u32[]{:S(2)}) collective-permute-start(bf16[2,48,1536]{2,1,0:T(8,128)(2,1)} %get-tuple-element.140), channel_id=1, source_target_pairs={{0,16},{2,18},{4,20},{6,22},{8,24},{10,26},{12,28},{14,30},{16,0},... | collective-permute-start | bytes 884744 | tf_op jit(solution)/shard_map/ppermute | solution.py:116
  45.9 10.9 %collective-permute-done.10.refs_1_ = bf16[2,48,1536]{2,1,0:T(8,128)(2,1)S(1)} collective-permute-done((bf16[2,48,1536]{2,1,0:T(8,128)(2,1)}, bf16[2,48,1536]{2,1,0:T(8,128)(2,1)S(1)}, u32[]{:S(2)}, u32[]{:S(2)}) %collective-permute-start.10) | collective-permute-done | bytes 294944 | tf_op jit(solution)/shard_map/ppermute | solution.py:116
  56.9 1.3 collective-permute-done.11.refs_2_
  58.2 2.3 join_chunks.3.p0
  60.5 1.5 collective-permute-start.12
  62.0 1.5 collective-permute-start.13
  63.5 4.3 %all-to-all-start = ((bf16[16,72,384]{2,1,0:T(8,128)(2,1)}), bf16[16,72,384]{2,1,0:T(8,128)(2,1)}, u32[]{:S(2)}, u32[]{:S(2)}) async-start(bf16[16,72,384]{2,1,0:T(8,128)(2,1)} %bitcast.72), calls=%async_computation | async-start | bytes 1769472 | tf_op jit(solution)/shard_map/all_to_all | solution.py:1283
  67.8 16.8 %attention_forward.1 = (bf16[768,768]{1,0:T(8,128)(2,1)}, bf16[768,1152]{1,0:T(8,128)(2,1)}, bf16[6,768,768]{2,1,0:T(8,128)(2,1)}, bf16[768,384]{1,0:T(8,128)(2,...) custom-call(s32[4]{0:T(128)} %pad_add_fusion.words_ref, ...), custom_call_target="tpu_custom_call" | custom-call | flops 20700000256 | bytes 1000000 | tf_op jit(solution)/shard_map/attention_forward/pallas_call | solution.py:770
  84.7 5.8 %collective-permute-done.12.p1 = bf16[6,48,1536]{2,1,0:T(8,128)(2,1)} collective-permute-done((bf16[6,48,1536]{2,1,0:T(8,128)(2,1)}, bf16[6,48,1536]{2,1,0:T(8,128)(2,1)}, u32[]{:S(2)}, u32[]{:S(2)}) %collective-permute-start.12) | collective-permute-done | bytes 884768 | tf_op jit(solution)/shard_map/ppermute | solution.py:514
  90.5 1.3 collective-permute-start.14
  91.8 0.9 all-to-all-done
  92.7 2.8 %convolution_convert_fusion.2 = bf16[768,384]{1,0:T(8,128)(2,1)S(1)} fusion(bf16[768,1152]{1,0:T(8,128)(2,1)} %fusion.1, bf16[1152,384]{1,0:T(8,128)(2,1)} %bitcast.16), kind=kOutput, calls=%fused_computation.9 | convolution fusion | flops 679772160 | bytes 3244032 | tf_op jit(solution)/shard_map/dot_general | solution.py:34
  96.2 1.5 collective-permute-done.16
  97.7 2.6 %maximum_select_fusion.grad_any = bf16[768,768]{1,0:T(8,128)(2,1)} fusion(bf16[768,384]{1,0:T(8,128)(2,1)} %collective-permute-done.16, bf16[768,384]{1,0:T(8,128)(2,1)S(1)} %convolution_convert_fusion.2, pred[]{:T(512)S(6)} %eq.46), kind=kLoop, calls=%fused_computation.13 | loop fusion | flops 5308416 | bytes 2359297 | tf_op jit(solution)/shard_map/jit(_where)/select_n | solution.py:1329
  100.3 3.5 %collective-permute-done.14.p3 = bf16[6,48,1536]{2,1,0:T(8,128)(2,1)} collective-permute-done((bf16[6,48,1536]{2,1,0:T(8,128)(2,1)}, bf16[6,48,1536]{2,1,0:T(8,128)(2,1)}, u32[]{:S(2)}, u32[]{:S(2)}) %collective-permute-start.14) | collective-permute-done | bytes 884768 | tf_op jit(solution)/shard_map/ppermute | solution.py:514
  103.8 21.0 %mlp_all.1 = (f32[1,1536]{1,0:T(1,128)}, f32[1,768]{1,0:T(1,128)}, f32[768,768]{1,0:T(8,128)}, bf16[768,768]{1,0:T(8,128)(2,1)}, bf16[768,768]{1,0:T(8,128)(2,1)...) custom-call(s32[4]{0:T(128)} %pad_add_fusion.words_ref, ...), custom_call_target="tpu_custom_call" | custom-call | flops 20700000256 | bytes 1000000 | tf_op jit(solution)/shard_map/mlp_all/pallas_call | solution.py:912
  124.9 1.4 collective-permute-start.17
  127.4 1.6 collective-permute-start.21
  129.0 4.2 %convolution_convert_fusion = bf16[1152,384]{1,0:T(8,128)(2,1)} fusion(bf16[768,1152]{1,0:T(8,128)(2,1)} %fusion.1, f32[768,768]{1,0:T(8,128)} %get-tuple-element.169.middle_any, s32[]{:T(128)S(6)} %select_n.70, f32[384]{0:T(512)S(1)} %dynamic-slice, bf16[768,768]{1,0:T(8,128)(2,1)} %collective-permute-done.19, bf16[768,768]{1,0:T(8,128)(2,1)} %get-tuple-element.170), kind=kOutput, calls=%fused_computation.6 | convolution fusion | flops 681689088 | bytes 5015044 | tf_op jit(solution)/shard_map/dot_general | solution.py:44
  133.2 8.4 %collective-permute-done.17.one_ref.refs_1_ = bf16[384,1536]{1,0:T(8,128)(2,1)} collective-permute-done((bf16[384,1536]{1,0:T(8,128)(2,1)}, bf16[384,1536]{1,0:T(8,128)(2,1)}, u32[]{:S(2)}, u32[]{:S(2)}) %collective-permute-start.17) | collective-permute-done | bytes 1179680 | tf_op jit(solution)/shard_map/ppermute | solution.py:514
  141.5 1.2 add_convert_fusion.2
  142.7 1.5 collective-permute-start.20
  144.2 4.8 %all-to-all-start.1 = ((bf16[16,72,384]{2,1,0:T(8,128)(2,1)}), bf16[16,72,384]{2,1,0:T(8,128)(2,1)}, u32[]{:S(2)}, u32[]{:S(2)}) async-start(bf16[16,72,384]{2,1,0:T(8,128)(2,1)} %bitcast.73), calls=%async_computation.1 | async-start | bytes 1769472 | tf_op jit(solution)/shard_map/all_to_all | solution.py:1283
  149.0 20.7 %attention_back.1 = (f32[768,768]{1,0:T(8,128)}, bf16[768,768]{1,0:T(8,128)(2,1)}, bf16[400,1536]{1,0:T(8,128)(2,1)}, bf16[400,1536]{1,0:T(8,128)(2,1)}) custom-call(s32[4]{0:T(128)} %pad_add_fusion.words_ref, f32[6,768]{1,0:T(8,128)} %rep_ref.3, f32[1,1536]{1,0:T(1,128)} %get-tuple-element.173.hidden_sum_any, f32[1,768]{1,0:T(1,128)} %get-tuple-element.174.grad_sum_any, ...), custom_call_target="tpu_custom_call" | custom-call | flops 25300000768 | bytes 1000000 | tf_op jit(solution)/shard_map/attention_back/pallas_call | solution.py:1092
  170.0 1.7 collective-permute-start.22
  171.7 1.4 add_convert_fusion.1
  173.1 1.4 collective-permute-start.26
  174.5 2.2 last_messages.3
  176.8 3.3 %collective-permute-start.23 = (bf16[48,1536]{1,0:T(8,128)(2,1)}, bf16[48,1536]{1,0:T(8,128)(2,1)S(1)}, u32[]{:S(2)}, u32[]{:S(2)}) collective-permute-start(bf16[48,1536]{1,0:T(8,128)(2,1)} %get-tuple-element.189), channel_id=1, source_target_pairs={{0,24},{2,26},{4,28},{6,30},{8,16},{10,18},{12,20},{14,22},{16,8},... | collective-permute-start | bytes 442376 | tf_op jit(solution)/shard_map/ppermute | solution.py:116
  180.0 1.1 collective-permute-start.25
  181.2 3.7 %select_convert_fusion = bf16[1088,384]{1,0:T(8,128)(2,1)} fusion(bf16[384]{0:T(512)(128)(2,1)S(1)} %copy-done.28, pred[1088]{0:T(1024)(128)(4,1)S(1)} %reshape.320, bf16[1152,1088]{1,0:T(8,128)(2,1)S(1)} %fusion, bf16[1152,384]{1,0:T(8,128)(2,1)} %bitcast.18), kind=kOutput, calls=%fused_computation.8 | convolution fusion | flops 963010560 | bytes 4228928 | tf_op jit(solution)/shard_map/dot_general | solution.py:44
  185.7 2.5 %collective-permute-done.24.refs_4_ = bf16[48,1536]{1,0:T(8,128)(2,1)S(1)} collective-permute-done((bf16[48,1536]{1,0:T(8,128)(2,1)}, bf16[48,1536]{1,0:T(8,128)(2,1)S(1)}, u32[]{:S(2)}, u32[]{:S(2)}) %collective-permute-start.24) | collective-permute-done | bytes 147488 | tf_op jit(solution)/shard_map/ppermute | solution.py:116
  188.1 3.2 %collective-permute-done.25.refs_5_ = bf16[48,1536]{1,0:T(8,128)(2,1)S(1)} collective-permute-done((bf16[48,1536]{1,0:T(8,128)(2,1)}, bf16[48,1536]{1,0:T(8,128)(2,1)S(1)}, u32[]{:S(2)}, u32[]{:S(2)}) %collective-permute-start.25) | collective-permute-done | bytes 147488 | tf_op jit(solution)/shard_map/ppermute | solution.py:116
  191.3 2.0 collective-permute-done.22.one_ref.refs_1_
  193.3 1.2 add_convert_fusion.refs_0_
  194.6 1.7 collective-permute-start.27
  196.3 2.2 last_messages.4
  198.5 2.7 %collective-permute-start.28 = (bf16[48,1536]{1,0:T(8,128)(2,1)}, bf16[48,1536]{1,0:T(8,128)(2,1)S(1)}, u32[]{:S(2)}, u32[]{:S(2)}) collective-permute-start(bf16[48,1536]{1,0:T(8,128)(2,1)} %get-tuple-element.200), channel_id=1, source_target_pairs={{0,24},{2,26},{4,28},{6,30},{8,16},{10,18},{12,20},{14,22},{16,8},... | collective-permute-start | bytes 442376 | tf_op jit(solution)/shard_map/ppermute | solution.py:116
  201.3 1.7 collective-permute-start.34
  203.0 2.7 %adam_unit.5 = (f32[576,128]{1,0:T(8,128)}, f32[576,128]{1,0:T(8,128)}, f32[576,128]{1,0:T(8,128)}) custom-call(bf16[384,1536]{1,0:T(8,128)(2,1)} %get-tuple-element.166.kept_ref.refs_0_, bf16[384,1536]{1,0:T(8,128)(2,1)} %collective-permute-done.17.one_ref.refs_1_, bf16[192,1536]{1,0:T(8,128)(2,1)} %collective-permute-done.20.two_ref.refs_2_, ...), custom_call_target="tpu_custom_call" | custom-call | flops 2875000064 | bytes 1000000 | tf_op jit(solution)/shard_map/adam_unit/pallas_call | solution.py:1175
  205.7 1.6 collective-permute-done.28.refs_3_
  207.4 0.9 copy-done.18
  208.3 2.7 %last_messages.5 = (bf16[64,1536]{1,0:T(8,128)(2,1)}, bf16[64,1536]{1,0:T(8,128)(2,1)}, bf16[64,1536]{1,0:T(8,128)(2,1)}) custom-call(bf16[400,1536]{1,0:T(8,128)(2,1)} %get-tuple-element.197.kept_ref.refs_0_, bf16[400,1536]{1,0:T(8,128)(2,1)} %collective-permute-done.22.one_ref.refs_1_, bf16[208,1536]{1,0:T(8,128)(2,1)} %copy-done.18, ...), custom_call_target="tpu_custom_call" | custom-call | flops 1724999936 | bytes 1000000 | tf_op jit(solution)/shard_map/last_messages/pallas_call | solution.py:602
  211.0 2.7 %collective-permute-start.30 = (bf16[64,1536]{1,0:T(8,128)(2,1)}, bf16[64,1536]{1,0:T(8,128)(2,1)S(1)}, u32[]{:S(2)}, u32[]{:S(2)}) collective-permute-start(bf16[64,1536]{1,0:T(8,128)(2,1)} %get-tuple-element.216), channel_id=1, source_target_pairs={{0,24},{2,26},{4,28},{6,30},{8,16},{10,18},{12,20},{14,22},{16,8},... | collective-permute-start | bytes 589832 | tf_op jit(solution)/shard_map/ppermute | solution.py:116
  213.7 0.9 collective-permute-start.31
  215.4 4.7 %input_gradient.1 = f32[768,768]{1,0:T(8,128)} custom-call(bf16[768,768]{1,0:T(8,128)(2,1)} %bitcast.83, bf16[768,768]{1,0:T(8,128)(2,1)} %get-tuple-element.201.own_ref, bf16[768,768]{1,0:T(8,128)(2,1)} %copy-done.17, f32[768,768]{1,0:T(8,128)} %get-tuple-element.208.middle_ref, f32[6,768]{1,0:T(8,128)} %rep_ref.3), custom_call_target="tpu_custom_call" | custom-call | flops 6554999808 | bytes 1000000 | tf_op jit(solution)/shard_map/input_gradient/pallas_call | solution.py:1142
  220.8 2.7 %adam_unit.3 = (f32[576,128]{1,0:T(8,128)}, f32[576,128]{1,0:T(8,128)}, f32[576,128]{1,0:T(8,128)}) custom-call(bf16[384,1536]{1,0:T(8,128)(2,1)} %get-tuple-element.192.kept_ref.refs_0_, bf16[384,1536]{1,0:T(8,128)(2,1)} %collective-permute-done.21.one_ref.refs_1_, bf16[192,1536]{1,0:T(8,128)(2,1)} %collective-permute-done.26.two_ref.refs_2_, ...), custom_call_target="tpu_custom_call" | custom-call | flops 2875000064 | bytes 1000000 | tf_op jit(solution)/shard_map/adam_unit/pallas_call | solution.py:1175
  223.8 8.5 %collective-permute-done.32.refs_5_ = bf16[64,1536]{1,0:T(8,128)(2,1)S(1)} collective-permute-done((bf16[64,1536]{1,0:T(8,128)(2,1)}, bf16[64,1536]{1,0:T(8,128)(2,1)S(1)}, u32[]{:S(2)}, u32[]{:S(2)}) %collective-permute-start.32) | collective-permute-done | bytes 196640 | tf_op jit(solution)/shard_map/ppermute | solution.py:116
  232.3 0.8 add_add_fusion
  234.1 2.7 %adam_unit.4 = (f32[432,128]{1,0:T(8,128)}, f32[432,128]{1,0:T(8,128)}, f32[432,128]{1,0:T(8,128)}, f32[144,128]{1,0:T(8,128)}, f32[144,128]{1,0:T(8,128)}, /*index=5*/f32[144,128]{1,0:T(8,128)}) custom-call(bf16[400,1536]{1,0:T(8,128)(2,1)} %get-tuple-element.197.kept_ref.refs_0_, bf16[400,1536]{1,0:T(8,128)(2,1)} %collective-permute-done.22.one_ref.refs_1_, ...), custom_call_target="tpu_custom_call" | custom-call | flops 2875000064 | bytes 1000000 | tf_op jit(solution)/shard_map/adam_unit/pallas_call | solution.py:1175
  (144 shorter events, 17.5 us)
Async XLA Ops:
  0.7 22.6 %copy-start = (bf16[32,34,1,384]{3,0,2,1:T(8,128)(2,1)S(1)}, bf16[32,34,1,384]{3,0,2,1:T(8,128)(2,1)}, u32[]{:S(2)}) copy-start(bf16[32,34,1,384]{3,0,2,1:T(8,128)(2,1)} %param.25) | copy-start | bytes 2506756
  0.7 11.7 %copy-start.5 = (s32[32,529]{1,0:T(8,128)S(1)}, s32[32,529]{1,0:T(8,128)}, u32[]{:S(2)}) copy-start(s32[32,529]{1,0:T(8,128)} %param.28) | copy-start | bytes 203140
  0.7 11.7 %copy-start.15 = (s32[32]{0:T(128)S(1)}, s32[32]{0:T(128)}, u32[]{:S(2)}) copy-start(s32[32]{0:T(128)} %param.27) | copy-start | bytes 388
  0.7 12.5 %copy-start.16 = (s32[32]{0:T(128)S(1)}, s32[32]{0:T(128)}, u32[]{:S(2)}) copy-start(s32[32]{0:T(128)} %param.29) | copy-start | bytes 388
  2.9 20.3 %collective-permute-start.3 = (bf16[3,48,1536]{2,1,0:T(8,128)(2,1)}, bf16[3,48,1536]{2,1,0:T(8,128)(2,1)}, u32[]{:S(2)}, u32[]{:S(2)}) collective-permute-start(bf16[3,48,1536]{2,1,0:T(8,128)(2,1)} %get-tuple-element.129.o0), channel_id=1, source_target_pairs={{0,2},{1,5},{2,0},{3,7},{4,6},{5,1},{6,4},{7,3},{8,10},{9,13},{10,... | collective-permute-start | bytes 1327112 | tf_op jit(solution)/shard_map/ppermute | solution.py:514
  5.9 17.4 %collective-permute-start.4 = (bf16[3,48,1536]{2,1,0:T(8,128)(2,1)}, bf16[3,48,1536]{2,1,0:T(8,128)(2,1)}, u32[]{:S(2)}, u32[]{:S(2)}) collective-permute-start(bf16[3,48,1536]{2,1,0:T(8,128)(2,1)} %get-tuple-element.129.o0), channel_id=1, source_target_pairs={{0,4},{1,3},{2,6},{3,1},{4,0},{5,7},{6,2},{7,5},{8,12},{9,11},{10,... | collective-permute-start | bytes 1327112 | tf_op jit(solution)/shard_map/ppermute | solution.py:514
  7.4 13.6 %collective-permute-start = (bf16[1,48,1536]{2,1,0:T(8,128)(2,1)}, bf16[1,48,1536]{2,1,0:T(8,128)(2,1)}, u32[]{:S(2)}, u32[]{:S(2)}) collective-permute-start(bf16[1,48,1536]{2,1,0:T(8,128)(2,1)} %get-tuple-element.128), channel_id=1, source_target_pairs={{0,24},{2,26},{4,28},{6,30},{8,16},{10,18},{12,20},{14,22},{16,8},... | collective-permute-start | bytes 442376 | tf_op jit(solution)/shard_map/ppermute | solution.py:116
  11.0 10.0 %collective-permute-start.1 = (bf16[1,48,1536]{2,1,0:T(8,128)(2,1)}, bf16[1,48,1536]{2,1,0:T(8,128)(2,1)}, u32[]{:S(2)}, u32[]{:S(2)}) collective-permute-start(bf16[1,48,1536]{2,1,0:T(8,128)(2,1)} %get-tuple-element.128), channel_id=1, source_target_pairs={{0,8},{2,10},{4,12},{6,14},{8,0},{10,2},{12,4},{14,6},{16,24},{18,... | collective-permute-start | bytes 442376 | tf_op jit(solution)/shard_map/ppermute | solution.py:116
  11.0 12.2 %collective-permute-start.2 = (bf16[1,48,1536]{2,1,0:T(8,128)(2,1)}, bf16[1,48,1536]{2,1,0:T(8,128)(2,1)}, u32[]{:S(2)}, u32[]{:S(2)}) collective-permute-start(bf16[1,48,1536]{2,1,0:T(8,128)(2,1)} %get-tuple-element.128), channel_id=1, source_target_pairs={{0,16},{2,18},{4,20},{6,22},{8,24},{10,26},{12,28},{14,30},{16,0},... | collective-permute-start | bytes 442376 | tf_op jit(solution)/shard_map/ppermute | solution.py:116
  25.1 19.7 %copy-start.6 = (f32[1,6,384]{2,0,1:T(1,128)S(1)}, f32[1,6,384]{2,0,1:T(1,128)}, u32[]{:S(2)}) copy-start(f32[1,6,384]{2,0,1:T(1,128)} %param.45) | copy-start | bytes 27652
  25.1 13.4 %collective-permute-start.5 = (bf16[3,48,1536]{2,1,0:T(8,128)(2,1)}, bf16[3,48,1536]{2,1,0:T(8,128)(2,1)}, u32[]{:S(2)}, u32[]{:S(2)}) collective-permute-start(bf16[3,48,1536]{2,1,0:T(8,128)(2,1)} %join_chunks.2.p0), channel_id=1, source_target_pairs={{0,2},{1,5},{2,0},{3,7},{4,6},{5,1},{6,4},{7,3},{8,10},{9,13},{10,... | collective-permute-start | bytes 1327112 | tf_op jit(solution)/shard_map/ppermute | solution.py:514
  25.6 12.9 %collective-permute-start.6 = (bf16[3,48,1536]{2,1,0:T(8,128)(2,1)}, bf16[3,48,1536]{2,1,0:T(8,128)(2,1)}, u32[]{:S(2)}, u32[]{:S(2)}) collective-permute-start(bf16[3,48,1536]{2,1,0:T(8,128)(2,1)} %join_chunks.2.p0), channel_id=1, source_target_pairs={{0,4},{1,3},{2,6},{3,1},{4,0},{5,7},{6,2},{7,5},{8,12},{9,11},{10,... | collective-permute-start | bytes 1327112 | tf_op jit(solution)/shard_map/ppermute | solution.py:514
  26.1 15.2 %collective-permute-start.7 = (bf16[3,48,1536]{2,1,0:T(8,128)(2,1)}, bf16[3,48,1536]{2,1,0:T(8,128)(2,1)}, u32[]{:S(2)}, u32[]{:S(2)}) collective-permute-start(bf16[3,48,1536]{2,1,0:T(8,128)(2,1)} %collective-permute-done.3.o1), channel_id=1, source_target_pairs={{0,4},{1,3},{2,6},{3,1},{4,0},{5,7},{6,2},{7,5},{8,12},{9,11},{10,... | collective-permute-start | bytes 1327112 | tf_op jit(solution)/shard_map/ppermute | solution.py:514
  27.7 9.3 %collective-permute-start.8 = (bf16[2,48,1536]{2,1,0:T(8,128)(2,1)}, bf16[2,48,1536]{2,1,0:T(8,128)(2,1)S(1)}, u32[]{:S(2)}, u32[]{:S(2)}) collective-permute-start(bf16[2,48,1536]{2,1,0:T(8,128)(2,1)} %get-tuple-element.140), channel_id=1, source_target_pairs={{0,24},{2,26},{4,28},{6,30},{8,16},{10,18},{12,20},{14,22},{16,8},... | collective-permute-start | bytes 884744 | tf_op jit(solution)/shard_map/ppermute | solution.py:116
  36.9 4.4 %copy-start.20 = (bf16[2,48,1536]{2,1,0:T(8,128)(2,1)}, bf16[2,48,1536]{2,1,0:T(8,128)(2,1)S(1)}, u32[]{:S(2)}) copy-start(bf16[2,48,1536]{2,1,0:T(8,128)(2,1)S(1)} %collective-permute-done.8.refs_0_) | copy-start | bytes 884740
  41.3 16.9 %collective-permute-start.9 = (bf16[3,48,1536]{2,1,0:T(8,128)(2,1)}, bf16[3,48,1536]{2,1,0:T(8,128)(2,1)S(1)}, u32[]{:S(2)}, u32[]{:S(2)}) collective-permute-start(bf16[3,48,1536]{2,1,0:T(8,128)(2,1)} %collective-permute-done.5.p1), channel_id=1, source_target_pairs={{0,4},{1,3},{2,6},{3,1},{4,0},{5,7},{6,2},{7,5},{8,12},{9,11},{10,... | collective-permute-start | bytes 1327112 | tf_op jit(solution)/shard_map/ppermute | solution.py:514
  41.8 15.0 %collective-permute-start.10 = (bf16[2,48,1536]{2,1,0:T(8,128)(2,1)}, bf16[2,48,1536]{2,1,0:T(8,128)(2,1)S(1)}, u32[]{:S(2)}, u32[]{:S(2)}) collective-permute-start(bf16[2,48,1536]{2,1,0:T(8,128)(2,1)} %get-tuple-element.140), channel_id=1, source_target_pairs={{0,8},{2,10},{4,12},{6,14},{8,0},{10,2},{12,4},{14,6},{16,24},{18,... | collective-permute-start | bytes 884744 | tf_op jit(solution)/shard_map/ppermute | solution.py:116
  42.2 16.0 %collective-permute-start.11 = (bf16[2,48,1536]{2,1,0:T(8,128)(2,1)}, bf16[2,48,1536]{2,1,0:T(8,128)(2,1)}, u32[]{:S(2)}, u32[]{:S(2)}) collective-permute-start(bf16[2,48,1536]{2,1,0:T(8,128)(2,1)} %get-tuple-element.140), channel_id=1, source_target_pairs={{0,16},{2,18},{4,20},{6,22},{8,24},{10,26},{12,28},{14,30},{16,0},... | collective-permute-start | bytes 884744 | tf_op jit(solution)/shard_map/ppermute | solution.py:116
  56.9 1.3 copy-start.21
  58.2 2.3 copy-start.19
  60.5 29.9 %collective-permute-start.12 = (bf16[6,48,1536]{2,1,0:T(8,128)(2,1)}, bf16[6,48,1536]{2,1,0:T(8,128)(2,1)}, u32[]{:S(2)}, u32[]{:S(2)}) collective-permute-start(bf16[6,48,1536]{2,1,0:T(8,128)(2,1)} %join_chunks.3.p0), channel_id=1, source_target_pairs={{0,2},{1,5},{2,0},{3,7},{4,6},{5,1},{6,4},{7,3},{8,10},{9,13},{10,... | collective-permute-start | bytes 2654216 | tf_op jit(solution)/shard_map/ppermute | solution.py:514
  62.0 28.5 %collective-permute-start.13 = (bf16[6,48,1536]{2,1,0:T(8,128)(2,1)}, bf16[6,48,1536]{2,1,0:T(8,128)(2,1)}, u32[]{:S(2)}, u32[]{:S(2)}) collective-permute-start(bf16[6,48,1536]{2,1,0:T(8,128)(2,1)} %join_chunks.3.p0), channel_id=1, source_target_pairs={{0,4},{1,3},{2,6},{3,1},{4,0},{5,7},{6,2},{7,5},{8,12},{9,11},{10,... | collective-permute-start | bytes 2654216 | tf_op jit(solution)/shard_map/ppermute | solution.py:514
  63.5 29.3 %all-to-all-start = ((bf16[16,72,384]{2,1,0:T(8,128)(2,1)}), bf16[16,72,384]{2,1,0:T(8,128)(2,1)}, u32[]{:S(2)}, u32[]{:S(2)}) async-start(bf16[16,72,384]{2,1,0:T(8,128)(2,1)} %bitcast.72), calls=%async_computation | async-start | bytes 1769472 | tf_op jit(solution)/shard_map/all_to_all | solution.py:1283
  84.6 15.7 %collective-permute-start.15 = (bf16[768,768]{1,0:T(8,128)(2,1)}, bf16[768,768]{1,0:T(8,128)(2,1)}, u32[]{:S(2)}, u32[]{:S(2)}) collective-permute-start(bf16[768,768]{1,0:T(8,128)(2,1)} %get-tuple-element.148.own_any), channel_id=1, source_target_pairs={{0,1},{1,0},{2,3},{3,2},{4,5},{5,4},{6,7},{7,6},{8,9},{9,8},{10,11... | collective-permute-start | bytes 3538952 | tf_op jit(solution)/shard_map/ppermute | solution.py:120
  90.5 13.4 %collective-permute-start.14 = (bf16[6,48,1536]{2,1,0:T(8,128)(2,1)}, bf16[6,48,1536]{2,1,0:T(8,128)(2,1)}, u32[]{:S(2)}, u32[]{:S(2)}) collective-permute-start(bf16[6,48,1536]{2,1,0:T(8,128)(2,1)} %collective-permute-done.12.p1), channel_id=1, source_target_pairs={{0,4},{1,3},{2,6},{3,1},{4,0},{5,7},{6,2},{7,5},{8,12},{9,11},{10,... | collective-permute-start | bytes 2654216 | tf_op jit(solution)/shard_map/ppermute | solution.py:514
  95.5 2.2 collective-permute-start.16
  124.9 4.1 %collective-permute-start.19 = (bf16[768,768]{1,0:T(8,128)(2,1)}, bf16[768,768]{1,0:T(8,128)(2,1)}, u32[]{:S(2)}, u32[]{:S(2)}) collective-permute-start(bf16[768,768]{1,0:T(8,128)(2,1)} %get-tuple-element.170), channel_id=1, source_target_pairs={{0,1},{1,0},{2,3},{3,2},{4,5},{5,4},{6,7},{7,6},{8,9},{9,8},{10,11... | collective-permute-start | bytes 3538952 | tf_op jit(solution)/shard_map/ppermute | solution.py:120
  124.9 16.6 %collective-permute-start.17 = (bf16[384,1536]{1,0:T(8,128)(2,1)}, bf16[384,1536]{1,0:T(8,128)(2,1)}, u32[]{:S(2)}, u32[]{:S(2)}) collective-permute-start(bf16[384,1536]{1,0:T(8,128)(2,1)} %get-tuple-element.167), channel_id=1, source_target_pairs={{0,4},{1,3},{2,6},{3,1},{4,0},{5,7},{6,2},{7,5},{8,12},{9,11},{10,... | collective-permute-start | bytes 3538952 | tf_op jit(solution)/shard_map/ppermute | solution.py:514
  126.4 15.2 %collective-permute-start.18 = (bf16[768,768]{1,0:T(8,128)(2,1)}, bf16[768,768]{1,0:T(8,128)(2,1)}, u32[]{:S(2)}, u32[]{:S(2)}) collective-permute-start(bf16[768,768]{1,0:T(8,128)(2,1)} %get-tuple-element.168.own_any), channel_id=1, source_target_pairs={{0,1},{1,0},{2,3},{3,2},{4,5},{5,4},{6,7},{7,6},{8,9},{9,8},{10,11... | collective-permute-start | bytes 3538952 | tf_op jit(solution)/shard_map/ppermute | solution.py:120
  127.4 14.2 %copy-start.4 = (bf16[384,1536]{1,0:T(8,128)(2,1)S(1)}, bf16[384,1536]{1,0:T(8,128)(2,1)}, u32[]{:S(2)}) copy-start(bf16[384,1536]{1,0:T(8,128)(2,1)} %get-tuple-element.166.kept_ref.refs_0_) | copy-start | bytes 3538948
  127.4 42.3 %collective-permute-start.21 = (bf16[384,1536]{1,0:T(8,128)(2,1)}, bf16[384,1536]{1,0:T(8,128)(2,1)}, u32[]{:S(2)}, u32[]{:S(2)}) collective-permute-start(bf16[384,1536]{1,0:T(8,128)(2,1)} %get-tuple-element.172), channel_id=1, source_target_pairs={{0,4},{1,3},{2,6},{3,1},{4,0},{5,7},{6,2},{7,5},{8,12},{9,11},{10,... | collective-permute-start | bytes 3538952 | tf_op jit(solution)/shard_map/ppermute | solution.py:514
  142.7 26.9 %collective-permute-start.20 = (bf16[192,1536]{1,0:T(8,128)(2,1)S(1)}, bf16[192,1536]{1,0:T(8,128)(2,1)}, u32[]{:S(2)}, u32[]{:S(2)}) collective-permute-start(bf16[192,1536]{1,0:T(8,128)(2,1)S(1)} %add_convert_fusion.2), channel_id=1, source_target_pairs={{0,2},{1,5},{2,0},{3,7},{4,6},{5,1},{6,4},{7,3},{8,10},{9,13},{10,... | collective-permute-start | bytes 1769480 | tf_op jit(solution)/shard_map/ppermute | solution.py:514
  144.2 25.8 %all-to-all-start.1 = ((bf16[16,72,384]{2,1,0:T(8,128)(2,1)}), bf16[16,72,384]{2,1,0:T(8,128)(2,1)}, u32[]{:S(2)}, u32[]{:S(2)}) async-start(bf16[16,72,384]{2,1,0:T(8,128)(2,1)} %bitcast.73), calls=%async_computation.1 | async-start | bytes 1769472 | tf_op jit(solution)/shard_map/all_to_all | solution.py:1283
  170.0 23.4 %collective-permute-start.22 = (bf16[400,1536]{1,0:T(8,128)(2,1)}, bf16[400,1536]{1,0:T(8,128)(2,1)}, u32[]{:S(2)}, u32[]{:S(2)}) collective-permute-start(bf16[400,1536]{1,0:T(8,128)(2,1)} %get-tuple-element.187), channel_id=1, source_target_pairs={{0,4},{1,3},{2,6},{3,1},{4,0},{5,7},{6,2},{7,5},{8,12},{9,11},{10,... | collective-permute-start | bytes 3686408 | tf_op jit(solution)/shard_map/ppermute | solution.py:514
  173.1 8.1 %copy-start.28 = (bf16[384]{0:T(512)(128)(2,1)S(1)}, bf16[384]{0:T(512)(128)(2,1)}, u32[]{:S(2)}) copy-start(bf16[384]{0:T(512)(128)(2,1)} %param.26) | copy-start | bytes 2308
  173.1 18.2 %collective-permute-start.26 = (bf16[192,1536]{1,0:T(8,128)(2,1)S(1)}, bf16[192,1536]{1,0:T(8,128)(2,1)}, u32[]{:S(2)}, u32[]{:S(2)}) collective-permute-start(bf16[192,1536]{1,0:T(8,128)(2,1)S(1)} %add_convert_fusion.1), channel_id=1, source_target_pairs={{0,2},{1,5},{2,0},{3,7},{4,6},{5,1},{6,4},{7,3},{8,10},{9,13},{10,... | collective-permute-start | bytes 1769480 | tf_op jit(solution)/shard_map/ppermute | solution.py:514
  176.8 8.9 %collective-permute-start.23 = (bf16[48,1536]{1,0:T(8,128)(2,1)}, bf16[48,1536]{1,0:T(8,128)(2,1)S(1)}, u32[]{:S(2)}, u32[]{:S(2)}) collective-permute-start(bf16[48,1536]{1,0:T(8,128)(2,1)} %get-tuple-element.189), channel_id=1, source_target_pairs={{0,24},{2,26},{4,28},{6,30},{8,16},{10,18},{12,20},{14,22},{16,8},... | collective-permute-start | bytes 442376 | tf_op jit(solution)/shard_map/ppermute | solution.py:116
  180.0 8.1 %collective-permute-start.24 = (bf16[48,1536]{1,0:T(8,128)(2,1)}, bf16[48,1536]{1,0:T(8,128)(2,1)S(1)}, u32[]{:S(2)}, u32[]{:S(2)}) collective-permute-start(bf16[48,1536]{1,0:T(8,128)(2,1)} %get-tuple-element.190), channel_id=1, source_target_pairs={{0,8},{2,10},{4,12},{6,14},{8,0},{10,2},{12,4},{14,6},{16,24},{18,... | collective-permute-start | bytes 442376 | tf_op jit(solution)/shard_map/ppermute | solution.py:116
  180.0 13.3 %copy-start.3 = (bf16[400,1536]{1,0:T(8,128)(2,1)S(1)}, bf16[400,1536]{1,0:T(8,128)(2,1)}, u32[]{:S(2)}) copy-start(bf16[400,1536]{1,0:T(8,128)(2,1)} %get-tuple-element.197.kept_ref.refs_0_) | copy-start | bytes 3686404
  180.0 11.2 %collective-permute-start.25 = (bf16[48,1536]{1,0:T(8,128)(2,1)}, bf16[48,1536]{1,0:T(8,128)(2,1)S(1)}, u32[]{:S(2)}, u32[]{:S(2)}) collective-permute-start(bf16[48,1536]{1,0:T(8,128)(2,1)} %get-tuple-element.191), channel_id=1, source_target_pairs={{0,16},{2,18},{4,20},{6,22},{8,24},{10,26},{12,28},{14,30},{16,0},... | collective-permute-start | bytes 442376 | tf_op jit(solution)/shard_map/ppermute | solution.py:116
  185.7 12.9 %copy-start.23 = (bf16[48,1536]{1,0:T(8,128)(2,1)}, bf16[48,1536]{1,0:T(8,128)(2,1)S(1)}, u32[]{:S(2)}) copy-start(bf16[48,1536]{1,0:T(8,128)(2,1)S(1)} %collective-permute-done.23.refs_3_) | copy-start | bytes 442372
  188.1 10.4 %copy-start.25 = (bf16[48,1536]{1,0:T(8,128)(2,1)}, bf16[48,1536]{1,0:T(8,128)(2,1)S(1)}, u32[]{:S(2)}) copy-start(bf16[48,1536]{1,0:T(8,128)(2,1)S(1)} %collective-permute-done.24.refs_4_) | copy-start | bytes 442372
  191.3 7.3 %copy-start.27 = (bf16[48,1536]{1,0:T(8,128)(2,1)}, bf16[48,1536]{1,0:T(8,128)(2,1)S(1)}, u32[]{:S(2)}) copy-start(bf16[48,1536]{1,0:T(8,128)(2,1)S(1)} %collective-permute-done.25.refs_5_) | copy-start | bytes 442372
  193.3 14.0 %collective-permute-start.29 = (bf16[768,768]{1,0:T(8,128)(2,1)}, bf16[768,768]{1,0:T(8,128)(2,1)S(1)}, u32[]{:S(2)}, u32[]{:S(2)}) collective-permute-start(bf16[768,768]{1,0:T(8,128)(2,1)} %get-tuple-element.201.own_ref), channel_id=1, source_target_pairs={{0,1},{1,0},{2,3},{3,2},{4,5},{5,4},{6,7},{7,6},{8,9},{9,8},{10,11... | collective-permute-start | bytes 3538952 | tf_op jit(solution)/shard_map/ppermute | solution.py:120
  194.6 4.0 %copy-start.2 = (bf16[208,1536]{1,0:T(8,128)(2,1)}, bf16[208,1536]{1,0:T(8,128)(2,1)S(1)}, u32[]{:S(2)}) copy-start(bf16[208,1536]{1,0:T(8,128)(2,1)S(1)} %add_convert_fusion.refs_0_) | copy-start | bytes 1916932
  194.6 12.8 %collective-permute-start.27 = (bf16[208,1536]{1,0:T(8,128)(2,1)S(1)}, bf16[208,1536]{1,0:T(8,128)(2,1)S(1)}, u32[]{:S(2)}, u32[]{:S(2)}) collective-permute-start(bf16[208,1536]{1,0:T(8,128)(2,1)S(1)} %add_convert_fusion.refs_0_), channel_id=1, source_target_pairs={{0,2},{1,5},{2,0},{3,7},{4,6},{5,1},{6,4},{7,3},{8,10},{9,13},{10,... | collective-permute-start | bytes 1916936 | tf_op jit(solution)/shard_map/ppermute | solution.py:514
  198.5 8.8 %collective-permute-start.28 = (bf16[48,1536]{1,0:T(8,128)(2,1)}, bf16[48,1536]{1,0:T(8,128)(2,1)S(1)}, u32[]{:S(2)}, u32[]{:S(2)}) collective-permute-start(bf16[48,1536]{1,0:T(8,128)(2,1)} %get-tuple-element.200), channel_id=1, source_target_pairs={{0,24},{2,26},{4,28},{6,30},{8,16},{10,18},{12,20},{14,22},{16,8},... | collective-permute-start | bytes 442376 | tf_op jit(solution)/shard_map/ppermute | solution.py:116
  201.3 18.9 %collective-permute-start.33 = (bf16[48,1536]{1,0:T(8,128)(2,1)}, bf16[48,1536]{1,0:T(8,128)(2,1)S(1)}, u32[]{:S(2)}, u32[]{:S(2)}) collective-permute-start(bf16[48,1536]{1,0:T(8,128)(2,1)} %get-tuple-element.210), channel_id=1, source_target_pairs={{0,8},{2,10},{4,12},{6,14},{8,0},{10,2},{12,4},{14,6},{16,24},{18,... | collective-permute-start | bytes 442376 | tf_op jit(solution)/shard_map/ppermute | solution.py:116
  201.3 18.9 %collective-permute-start.34 = (bf16[48,1536]{1,0:T(8,128)(2,1)}, bf16[48,1536]{1,0:T(8,128)(2,1)S(1)}, u32[]{:S(2)}, u32[]{:S(2)}) collective-permute-start(bf16[48,1536]{1,0:T(8,128)(2,1)} %get-tuple-element.211), channel_id=1, source_target_pairs={{0,16},{2,18},{4,20},{6,22},{8,24},{10,26},{12,28},{14,30},{16,0},... | collective-permute-start | bytes 442376 | tf_op jit(solution)/shard_map/ppermute | solution.py:116
  207.3 12.8 %copy-start.22 = (bf16[48,1536]{1,0:T(8,128)(2,1)}, bf16[48,1536]{1,0:T(8,128)(2,1)S(1)}, u32[]{:S(2)}) copy-start(bf16[48,1536]{1,0:T(8,128)(2,1)S(1)} %collective-permute-done.28.refs_3_) | copy-start | bytes 442372
  208.3 2.7 %copy-start.17 = (bf16[768,768]{1,0:T(8,128)(2,1)}, bf16[768,768]{1,0:T(8,128)(2,1)S(1)}, u32[]{:S(2)}) copy-start(bf16[768,768]{1,0:T(8,128)(2,1)S(1)} %collective-permute-done.29.other_ref) | copy-start | bytes 3538948
  211.0 12.5 %collective-permute-start.30 = (bf16[64,1536]{1,0:T(8,128)(2,1)}, bf16[64,1536]{1,0:T(8,128)(2,1)S(1)}, u32[]{:S(2)}, u32[]{:S(2)}) collective-permute-start(bf16[64,1536]{1,0:T(8,128)(2,1)} %get-tuple-element.216), channel_id=1, source_target_pairs={{0,24},{2,26},{4,28},{6,30},{8,16},{10,18},{12,20},{14,22},{16,8},... | collective-permute-start | bytes 589832 | tf_op jit(solution)/shard_map/ppermute | solution.py:116
  213.7 10.1 %collective-permute-start.31 = (bf16[64,1536]{1,0:T(8,128)(2,1)}, bf16[64,1536]{1,0:T(8,128)(2,1)S(1)}, u32[]{:S(2)}, u32[]{:S(2)}) collective-permute-start(bf16[64,1536]{1,0:T(8,128)(2,1)} %get-tuple-element.205), channel_id=1, source_target_pairs={{0,8},{2,10},{4,12},{6,14},{8,0},{10,2},{12,4},{14,6},{16,24},{18,... | collective-permute-start | bytes 589832 | tf_op jit(solution)/shard_map/ppermute | solution.py:116
  214.6 17.7 %collective-permute-start.32 = (bf16[64,1536]{1,0:T(8,128)(2,1)}, bf16[64,1536]{1,0:T(8,128)(2,1)S(1)}, u32[]{:S(2)}, u32[]{:S(2)}) collective-permute-start(bf16[64,1536]{1,0:T(8,128)(2,1)} %get-tuple-element.206), channel_id=1, source_target_pairs={{0,16},{2,18},{4,20},{6,22},{8,24},{10,26},{12,28},{14,30},{16,0},... | collective-permute-start | bytes 589832 | tf_op jit(solution)/shard_map/ppermute | solution.py:116
  220.8 12.5 %copy-start.13 = (f32[1,6,384]{2,0,1:T(1,128)S(1)}, f32[1,6,384]{2,0,1:T(1,128)}, u32[]{:S(2)}) copy-start(f32[1,6,384]{2,0,1:T(1,128)} %param.46) | copy-start | bytes 27652
  220.8 12.5 %copy-start.14 = (f32[1,6,384]{2,0,1:T(1,128)S(1)}, f32[1,6,384]{2,0,1:T(1,128)}, u32[]{:S(2)}) copy-start(f32[1,6,384]{2,0,1:T(1,128)} %param.47) | copy-start | bytes 27652
  223.6 10.5 %copy-start.10 = (bf16[64,1536]{1,0:T(8,128)(2,1)}, bf16[64,1536]{1,0:T(8,128)(2,1)S(1)}, u32[]{:S(2)}) copy-start(bf16[64,1536]{1,0:T(8,128)(2,1)S(1)} %collective-permute-done.30.refs_3_) | copy-start | bytes 589828
  223.8 10.2 %copy-start.11 = (bf16[64,1536]{1,0:T(8,128)(2,1)}, bf16[64,1536]{1,0:T(8,128)(2,1)S(1)}, u32[]{:S(2)}) copy-start(bf16[64,1536]{1,0:T(8,128)(2,1)S(1)} %collective-permute-done.31.refs_4_) | copy-start | bytes 589828
  232.3 1.7 copy-start.12
  233.2 4.2 %collective-permute-start.35 = (f32[3,1536]{1,0:T(4,128)S(1)}, f32[3,1536]{1,0:T(4,128)S(1)}, u32[]{:S(2)}, u32[]{:S(2)}) collective-permute-start(f32[3,1536]{1,0:T(4,128)S(1)} %slice.85), channel_id=1, source_target_pairs={{0,1},{1,0},{2,3},{3,2},{4,5},{5,4},{6,7},{7,6},{8,9},{9,8},{10,11... | collective-permute-start | bytes 55304 | tf_op jit(solution)/shard_map/ppermute | solution.py:120
  234.0 3.4 %copy-start.7 = (f32[6,768]{1,0:T(8,128)S(1)}, f32[6,768]{1,0:T(8,128)}, u32[]{:S(2)}) copy-start(f32[6,768]{1,0:T(8,128)} %rep_ref.3) | copy-start | bytes 55300
  234.0 3.4 %copy-start.8 = (f32[6,768]{1,0:T(8,128)S(1)}, f32[6,768]{1,0:T(8,128)}, u32[]{:S(2)}) copy-start(f32[6,768]{1,0:T(8,128)} %param.43) | copy-start | bytes 55300
  234.0 3.4 %copy-start.9 = (f32[6,768]{1,0:T(8,128)S(1)}, f32[6,768]{1,0:T(8,128)}, u32[]{:S(2)}) copy-start(f32[6,768]{1,0:T(8,128)} %param.44) | copy-start | bytes 55300
  234.0 4.1 %copy-start.1 = (bf16[32,34,1,384]{3,0,2,1:T(8,128)(2,1)S(1)}, bf16[32,34,1,384]{3,0,2,1:T(8,128)(2,1)}, u32[]{:S(2)}) copy-start(bf16[32,34,1,384]{3,0,2,1:T(8,128)(2,1)} %param.25) | copy-start | bytes 2506756
  (3 other events, 2.3 us)
